TPU v7x, 256 devices: a whole 4x4x8 slice. The times are simulated.
256 devices in a mesh: ctx: 16 (over y, z_lo, core), fsdp: 16 (over x, z_hi).
Axes of the slice: x: 4, y: 4, z: 8 (z_hi: 4, z_lo: 2; z = z_hi * 2 + z_lo), core: 2. Of those that a mesh axis runs over, the one named last changes fastest.
Arguments:
- queries: bfloat16 [16, 4096, 2048], P('fsdp', 'ctx'), may hold values from -6 to 6
- keys: bfloat16 [16, 4096, 2048], P('fsdp', 'ctx'), may hold values from -6 to 6
- values: bfloat16 [16, 4096, 2048], P('fsdp', 'ctx'), may hold values from -6 to 6
- out_weight: bfloat16 [2048, 2048], P('fsdp'), may hold values from -0.125 to 0.125
- out_grad: bfloat16 [16, 4096, 2048], P('fsdp', 'ctx'), may hold values from -6 to 6
Outputs:
- grad_queries: bfloat16 [16, 4096, 2048], P('fsdp', 'ctx')
- grad_keys: bfloat16 [16, 4096, 2048], P('fsdp', 'ctx')
- grad_values: bfloat16 [16, 4096, 2048], P('fsdp', 'ctx')
- grad_weight: float32 [2048, 2048], P('fsdp')
All inputs are finite; a program needn't handle non-finite values.
Results may differ from a plain program's by a relative error of at most 0.008.
Values may be sent and summed in bfloat16 or wider, within the bound.
No kernel may reach another device: no remote copies, remote signals or barrier semaphores. Data moves between devices by JAX's collectives and lax.ppermute only.
A program may use at most 128 MiB of HBM per device.

v0:
```python
import functools

import jax
import jax.numpy as jnp
from jax import lax
from jax.experimental import pallas as pl
from jax.experimental.pallas import tpu as pltpu
from jax.sharding import PartitionSpec as P

HEADS = 16
HEAD = 128
F32 = jnp.float32
BF16 = jnp.bfloat16


def dot(a, b, da, db):
    return lax.dot_general(a, b, (((da,), (db,)), ((), ())), preferred_element_type=F32)


AXES = ("y", "zl", "c", "x", "zh")
CTX, FSDP = AXES[:3], AXES[3:]


def from_core(v):
    return lax.ppermute(v, "c", [(0, 1), (1, 0)])


def copies(v, axis):
    return [v] + [lax.ppermute(v, axis, [((i + k) % 4, i) for i in range(4)]) for k in (1, 2, 3)]


def spread(pieces, axis):
    return [pieces[0]] + [
        lax.ppermute(pieces[k], axis, [(i, (i + k) % 4) for i in range(4)]) for k in (1, 2, 3)
    ]


def call(body, out, *args, grid=None, in_specs=None, out_specs=None, flops=0, room=None):
    size = sum(a.size * a.dtype.itemsize for a in args)
    outs = out if isinstance(out, (tuple, list)) else [out]
    size += sum(o.size * jnp.dtype(o.dtype).itemsize for o in outs)
    kwargs = {}
    if grid is not None:
        kwargs = dict(grid=grid)
    else:
        full = pl.BlockSpec(memory_space=pltpu.VMEM)
        small = pl.BlockSpec(memory_space=pltpu.SMEM)
        in_specs = [small if a.dtype == jnp.int32 else full for a in args]
        out_specs = jax.tree.map(lambda o: full, out)
    if room is None:
        room = 2 * size + 8 * 2**20
    return pl.pallas_call(
        body,
        out_shape=out,
        in_specs=list(in_specs),
        out_specs=out_specs,
        cost_estimate=pl.CostEstimate(flops=flops, bytes_accessed=size, transcendentals=0),
        compiler_params=pltpu.CompilerParams(vmem_limit_bytes=min(room, 56 * 2**20)),
        **kwargs,
    )(*args)


def shape(dims, dtype=BF16):
    return jax.ShapeDtypeStruct(dims, dtype)


PER = 4


def head_slices():
    return [(h, slice(h * HEAD, (h + 1) * HEAD)) for h in range(PER)]


def rows_spec(tokens):
    return pl.BlockSpec((tokens, PER * HEAD), lambda i: (0, i))


STATE_SPEC = pl.BlockSpec((PER, HEAD, HEAD), lambda i: (i, 0, 0))


def states_body(a_ref, b_ref, o_ref):
    for h, s in head_slices():
        o_ref[h] = dot(a_ref[:, s], b_ref[:, s], 0, 0).astype(BF16)


def scan_body(reverse, i_ref, o_ref):
    count = i_ref.shape[0]
    total = jnp.zeros(i_ref.shape[1:], F32)
    for n in range(count):
        at = count - 1 - n if reverse else n
        o_ref[at] = total.astype(BF16)
        total = total + i_ref[at].astype(F32)


def causal(tokens):
    return lax.broadcasted_iota(jnp.int32, (tokens, tokens), 0) >= lax.broadcasted_iota(
        jnp.int32, (tokens, tokens), 1
    )


def attended_body(factor, q_ref, k_ref, v_ref, p_ref, o_ref):
    keep = causal(q_ref.shape[0])
    for h, s in head_slices():
        q = q_ref[:, s]
        scores = jnp.where(keep, dot(q, k_ref[:, s], 1, 1), 0.0).astype(BF16)
        o_ref[s, :] = (factor * (dot(p_ref[h], q, 0, 1) + dot(v_ref[:, s], scores, 0, 1))).astype(BF16)


def grad_queries_body(factor, g_ref, k_ref, v_ref, p_ref, o_ref):
    keep = causal(g_ref.shape[0])
    for h, s in head_slices():
        g = g_ref[:, s]
        reverse = jnp.where(keep, dot(g, v_ref[:, s], 1, 1), 0.0).astype(BF16)
        o_ref[:, s] = (factor * (dot(g, p_ref[h], 1, 1) + dot(reverse, k_ref[:, s], 1, 0))).astype(BF16)


def grad_keys_values_body(factor, g_ref, q_ref, k_ref, v_ref, l_ref, gk_ref, gv_ref):
    keep = causal(g_ref.shape[0])
    for h, s in head_slices():
        g, q, k, v, later = g_ref[:, s], q_ref[:, s], k_ref[:, s], v_ref[:, s], l_ref[h]
        scores = jnp.where(keep, dot(q, k, 1, 1), 0.0).astype(BF16)
        reverse = jnp.where(keep, dot(g, v, 1, 1), 0.0).astype(BF16)
        gk_ref[:, s] = (factor * (dot(v, later, 1, 1) + dot(reverse, q, 0, 0))).astype(BF16)
        gv_ref[:, s] = (factor * (dot(k, later, 1, 0) + dot(scores, g, 0, 0))).astype(BF16)


def block(at, k, size):
    return pl.ds(pl.multiple_of(lax.rem(at + k, 4) * size, size), size)


def half_a(at_ref, width):
    return pl.ds(pl.multiple_of(at_ref[0] * width, width), width // 2)


def block_b(at_ref, k, width):
    start = at_ref[0] * width + width // 2 + lax.rem(at_ref[1] + k, 4) * (width // 8)
    return pl.ds(pl.multiple_of(start, width // 8), width // 8)


def other_b(at_ref, k, width):
    start = width // 2 + lax.rem(at_ref[1] + k, 4) * (width // 8)
    return pl.ds(pl.multiple_of(start, width // 8), width // 8)


def weight_y_body(at_ref, mine_ref, theirs_ref, og_ref, oog_ref, *o_refs):
    width = oog_ref.shape[1]
    og = jnp.concatenate([og_ref[:, block_b(at_ref, k, width)] for k in range(4)], axis=1)
    oog = jnp.concatenate([oog_ref[:, other_b(at_ref, k, width)] for k in range(4)], axis=1)
    step = 512

    def body(r, carry):
        rows = pl.ds(pl.multiple_of(r * step, step), step)
        both = dot(mine_ref[rows, :], og, 1, 0) + dot(theirs_ref[rows, :], oog, 1, 0)
        for k in range(4):
            o_refs[k][rows, :] = both[:, k * (width // 8) : (k + 1) * (width // 8)].astype(BF16)
        return carry

    lax.fori_loop(0, mine_ref.shape[0] // step, body, 0)


def weight_x_body(at_ref, mine_ref, theirs_ref, og_ref, oog_ref, *o_refs):
    width = oog_ref.shape[1]
    og = og_ref[:, half_a(at_ref, width)]
    oog = oog_ref[:, : width // 2]
    step = 512
    size = o_refs[0].shape[0]
    for k in range(4):
        start = lax.rem(at_ref[2] + k, 4) * size

        def body(r, carry, start=start, k=k):
            rows = pl.ds(pl.multiple_of(start + r * step, step), step)
            both = dot(mine_ref[rows, :], og, 1, 0) + dot(theirs_ref[rows, :], oog, 1, 0)
            o_refs[k][pl.ds(pl.multiple_of(r * step, step), step), :] = both.astype(BF16)
            return carry

        lax.fori_loop(0, size // step, body, 0)


def added(refs):
    total = refs[0][...].astype(F32)
    for ref in refs[1:]:
        total = total + ref[...].astype(F32)
    return total


def add_then_x_body(at_ref, *refs):
    size = refs[0].shape[0] // 4
    for k in range(4):
        rows = block(at_ref[2], k, size)
        total = refs[0][rows, :].astype(F32)
        for ref in refs[1:4]:
            total = total + ref[rows, :].astype(F32)
        refs[4 + k][...] = total.astype(BF16)


def add_then_y_body(at_ref, *refs):
    size = refs[0].shape[1] // 4
    for k in range(4):
        columns = block(at_ref[1], k, size)
        total = refs[0][:, columns].astype(F32)
        for ref in refs[1:4]:
            total = total + ref[:, columns].astype(F32)
        refs[4 + k][...] = total.astype(BF16)


def add_then_z_body(*refs):
    size = refs[8].shape[1]
    for first, total in ((0, added(refs[:4])), (4, added(refs[4:8]))):
        for n in range(4):
            refs[8][first + n] = total[n * size : (n + 1) * size, :].astype(BF16)


def add_then_all_body(i_ref, o_ref):
    total = added([i_ref.at[n] for n in range(i_ref.shape[0])]).astype(BF16)
    for n in range(o_ref.shape[0]):
        o_ref[n] = total


def finish_weight_body(scale, i_ref, o_ref):
    for n in range(i_ref.shape[0]):
        y, zl, core = n // 4, n // 2 % 2, n % 2
        column = (core * 8 + (1 - zl) * 4 + y) * i_ref.shape[2]
        o_ref[:, column : column + i_ref.shape[2]] = i_ref[n].astype(F32) * scale


def place_body(at_ref, *refs):
    size = refs[0].shape[0]
    for k in range(4):
        refs[4][block(at_ref[3], k, size), :] = refs[k][...]


def projected_body(other, at_ref, og_ref, a0, a1, a2, a3, b0, b1, b2, b3, o_ref):
    if other:
        width = og_ref.shape[1]
        parts = [og_ref[:, : width // 2]] + [og_ref[:, other_b(at_ref, k, width)] for k in range(4)]
    else:
        width = og_ref.shape[1] // 2
        parts = [og_ref[:, half_a(at_ref, width)]] + [og_ref[:, block_b(at_ref, k, width)] for k in range(4)]
    rows = jnp.concatenate(parts, axis=1)
    for k, a_ref in enumerate((a0, a1, a2, a3)):
        s = block(at_ref[2], k, a_ref.shape[0])
        weight = jnp.concatenate([a_ref[...]] + [b[s, :] for b in (b0, b1, b2, b3)], axis=1)
        o_ref[:, s] = dot(rows, weight, 1, 1)


def grad_attn_body(mine_ref, theirs_ref, q_ref, g_ref, o_ref):
    g_ref[...] = (mine_ref[...] + theirs_ref[...]).astype(BF16)
    for h, s in head_slices():
        o_ref[h] = dot(q_ref[:, s], g_ref[:, s], 0, 0).astype(BF16)


def local(queries, keys, values, out_weight, out_grad):
    q, k, v, og = queries[0], keys[0], values[0], out_grad[0]
    tokens, inner = q.shape
    width = og.shape[1] // 2
    y, _, core, x, zh = [lax.axis_index(name) for name in AXES]
    at = jnp.stack([core, y, x, zh]).astype(jnp.int32)
    factor = (HEAD * tokens * 16) ** (-0.5)
    scale = (tokens * 16 * 16) ** (-0.5)
    rows = rows_spec(tokens)
    heads = (HEADS // PER,)
    token_flops = 2 * tokens * inner * HEAD

    oog = from_core(lax.dynamic_slice(og, (0, (1 - core) * width), (tokens, width)))

    key_states = call(
        states_body, shape((HEADS, HEAD, HEAD)), k, v,
        grid=heads, in_specs=[rows, rows], out_specs=STATE_SPEC, flops=token_flops,
    )

    def exchange(states, reverse):
        by_head = lax.all_to_all(states, CTX, 0, 0)
        sums = call(functools.partial(scan_body, reverse), shape(by_head.shape), by_head, flops=by_head.size)
        return lax.all_to_all(sums, CTX, 0, 0)

    wa = lax.dynamic_slice(out_weight, (0, core * width), (out_weight.shape[0], width // 2))
    wb = lax.dynamic_slice(
        out_weight, (0, core * width + width // 2 + y * (width // 8)), (out_weight.shape[0], width // 8)
    )
    za = copies(wa, "zh")
    wb = lax.all_to_all(jnp.broadcast_to(wb[None], (16, *wb.shape)), FSDP, 0, 0).reshape(inner, -1)
    yb = copies(wb, "y")
    wa = call(place_body, shape((4 * out_weight.shape[0], wa.shape[1])), at, *za)
    xa = copies(wa, "x")
    prior = exchange(key_states, False)

    attended = call(
        functools.partial(attended_body, factor), shape((inner, tokens)), q, k, v, prior,
        grid=heads, in_specs=[rows, rows, rows, STATE_SPEC],
        out_specs=pl.BlockSpec((PER * HEAD, tokens), lambda i: (i, 0)), flops=5 * token_flops,
    )
    partner = from_core(attended)

    project_flops = 2 * tokens * inner * width
    for_partner = call(
        functools.partial(projected_body, True), shape((tokens, inner), F32), at, oog, *xa, *yb,
        flops=project_flops,
    )
    from_partner = from_core(for_partner)

    gw_flops = 2 * inner * 2 * tokens * (width // 2)
    gy = call(
        weight_y_body, [shape((inner, width // 8))] * 4, at, attended, partner, og, oog,
        flops=gw_flops,
    )
    gx = call(
        weight_x_body, [shape((inner // 4, width // 2))] * 4, at, attended, partner, og, oog,
        flops=gw_flops,
    )
    mine = call(
        functools.partial(projected_body, False), shape((tokens, inner), F32), at, og, *xa, *yb,
        flops=project_flops,
    )
    gy = spread(gy, "y")
    gx = spread(gx, "x")
    ga, grad_states = call(
        grad_attn_body, [shape((tokens, inner)), shape((HEADS, HEAD, HEAD))], mine, from_partner, q,
        grid=heads, in_specs=[rows, rows, rows], out_specs=[rows, STATE_SPEC], flops=token_flops,
    )
    quarter = shape((inner // 4, width // 8))
    gyx = call(add_then_x_body, [quarter] * 4, at, *gy)
    gyx = spread(gyx, "x")
    later = exchange(grad_states, True)
    gxy = call(add_then_y_body, [quarter] * 4, at, *gx)
    gxy = spread(gxy, "y")
    grad_queries = call(
        functools.partial(grad_queries_body, factor), shape((tokens, inner)), ga, k, v, prior,
        grid=heads, in_specs=[rows, rows, rows, STATE_SPEC], out_specs=rows, flops=5 * token_flops,
    )
    gz = call(add_then_z_body, shape((8, inner // 16, width // 8)), *gyx, *gxy)
    grad_keys, grad_values = call(
        functools.partial(grad_keys_values_body, factor), [shape((tokens, inner))] * 2, ga, q, k, v, later,
        grid=heads, in_specs=[rows, rows, rows, rows, STATE_SPEC], out_specs=[rows, rows], flops=10 * token_flops,
    )
    gz = lax.all_to_all(gz, ("zl", "zh"), 0, 0)
    total = call(add_then_all_body, shape((16, inner // 16, width // 8)), gz)
    gathered = lax.all_to_all(total, CTX, 0, 0)
    grad_weight = call(functools.partial(finish_weight_body, scale), shape((inner // 16, 2 * width), F32), gathered)

    return grad_queries[None], grad_keys[None], grad_values[None], grad_weight


def solution(mesh):
    fine = jax.sharding.Mesh(mesh.devices.reshape(4, 2, 2, 4, 4), AXES)
    tokens, rows = P(FSDP, CTX, None), P(FSDP, None)

    return jax.shard_map(
        local, mesh=fine, in_specs=(tokens, tokens, tokens, rows, tokens), out_specs=(tokens, tokens, tokens, rows), check_vma=False
    )
```

profile of v0, /device:TPU:1, one launch (start us, length us, event | category | flops | bytes accessed | tf_op | source)
XLA Modules:
  0.0 273.7 jit_solution(6265892904308840086)
XLA Ops:
  0.7 1.3 copy-done.1
  3.2 1.3 shard_map.88
  4.4 16.8 %all_to_all.35.i_ref = bf16[16,128,128]{2,1,0:T(8,128)(2,1)S(1)} all-to-all(bf16[16,128,128]{2,1,0:T(8,128)(2,1)S(1)} %shard_map.88), channel_id=1, replica_groups=mesh['y'=4,'zl'=2,'c'=2,'x'=4,'zh'=4] {'y','zl','c'}, dimensions={0} | all-to-all | bytes 1048576 | tf_op jit(solution)/shard_map/all_to_all | solution.py:272
  22.1 4.6 %all-to-all-start.2 = ((bf16[16,128,128]{2,1,0:T(8,128)(2,1)}), bf16[16,128,128]{2,1,0:T(8,128)(2,1)S(1)}, u32[]{:S(2)}, u32[]{:S(2)}) async-start(bf16[16,128,128]{2,1,0:T(8,128)(2,1)} %shard_map.89), calls=%async_computation.2 | async-start | bytes 1048576 | tf_op jit(solution)/shard_map/all_to_all | solution.py:274
  26.8 9.7 %all-to-all-done.2.p_ref = bf16[16,128,128]{2,1,0:T(8,128)(2,1)S(1)} async-done(((bf16[16,128,128]{2,1,0:T(8,128)(2,1)}), bf16[16,128,128]{2,1,0:T(8,128)(2,1)S(1)}, u32[]{:S(2)}, u32[]{:S(2)}) %all-to-all-start.2) | async-done | bytes 524320 | tf_op jit(solution)/shard_map/all_to_all | solution.py:274
  37.4 9.9 %all-to-all-start = ((bf16[16,128,128]{2,1,0:T(8,128)(2,1)}), bf16[16,128,128]{2,1,0:T(8,128)(2,1)}, u32[]{:S(2)}, u32[]{:S(2)}) async-start(bf16[16,128,128]{2,1,0:T(8,128)(2,1)} %broadcast_in_dim.15), calls=%async_computation | async-start | bytes 1048576 | tf_op jit(solution)/shard_map/all_to_all | solution.py:281
  47.3 3.5 %collective-permute-start = (bf16[128,512]{1,0:T(8,128)(2,1)S(1)}, bf16[128,512]{1,0:T(8,128)(2,1)S(1)}, u32[]{:S(2)}, u32[]{:S(2)}) collective-permute-start(bf16[128,512]{1,0:T(8,128)(2,1)S(1)} %constant_dynamic-slice_fusion.1.refs_0_), channel_id=1, source_target_pairs={{1,0},{2,1},{3,2},{0,3},{5,4},{6,5},{7,6},{4,7},{9,8},{10,9},{11,1... | collective-permute-start | bytes 393224 | tf_op jit(solution)/shard_map/ppermute | solution.py:29
  50.8 2.1 collective-permute-start.1
  52.9 2.1 collective-permute-start.2
  55.0 1.9 dynamic-slice_bitcast_fusion
  56.8 2.7 collective-permute-start.9
  59.6 1.9 collective-permute-done.refs_1_
  61.5 4.4 %collective-permute-done.1.refs_2_ = bf16[128,512]{1,0:T(8,128)(2,1)S(1)} collective-permute-done((bf16[128,512]{1,0:T(8,128)(2,1)S(1)}, bf16[128,512]{1,0:T(8,128)(2,1)S(1)}, u32[]{:S(2)}, u32[]{:S(2)}) %collective-permute-start.1) | collective-permute-done | bytes 131104 | tf_op jit(solution)/shard_map/ppermute | solution.py:29
  66.5 1.7 shard_map.84.a0
  68.3 2.4 collective-permute-start.3
  71.3 1.2 copy-done.5
  72.5 3.8 %shard_map.93.mine_ref = bf16[2048,256]{1,0:T(8,128)(2,1)} custom-call(bf16[256,2048]{1,0:T(8,128)(2,1)S(1)} %bitcast.22, bf16[256,2048]{1,0:T(8,128)(2,1)S(1)} %bitcast.15, bf16[256,2048]{1,0:T(8,128)(2,1)S(1)} %bitcast.19, bf16[16,128,128]{2,1,0:T(8,128)(2,1)S(1)} %all-to-all-done.2.p_ref), custom_call_target="tpu_custom_call" | custom-call | flops 671088640 | bytes 4718592 | tf_op jit(solution)/shard_map/pallas_call | solution.py:52
  76.3 3.9 %collective-permute-start.11 = (bf16[2048,256]{1,0:T(8,128)(2,1)}, bf16[2048,256]{1,0:T(8,128)(2,1)}, u32[]{:S(2)}, u32[]{:S(2)}) collective-permute-start(bf16[2048,256]{1,0:T(8,128)(2,1)} %shard_map.93.mine_ref), channel_id=1, source_target_pairs={{0,16},{16,0},{1,17},{17,1},{2,18},{18,2},{3,19},{19,3},{4,20},{20... | collective-permute-start | bytes 3145736 | tf_op jit(solution)/shard_map/ppermute | solution.py:25
  80.8 1.3 collective-permute-start.6
  82.1 3.0 %collective-permute-start.7 = (bf16[2048,128]{1,0:T(8,128)(2,1)}, bf16[2048,128]{1,0:T(8,128)(2,1)S(1)}, u32[]{:S(2)}, u32[]{:S(2)}) collective-permute-start(bf16[2048,128]{1,0:T(8,128)(2,1)} %bitcast.5.b0), channel_id=1, source_target_pairs={{128,0},{192,64},{0,128},{64,192},{129,1},{193,65},{1,129},{65,193... | collective-permute-start | bytes 1572872 | tf_op jit(solution)/shard_map/ppermute | solution.py:29
  85.9 11.7 %collective-permute-done.5.a3 = bf16[512,512]{1,0:T(8,128)(2,1)} collective-permute-done((bf16[512,512]{1,0:T(8,128)(2,1)}, bf16[512,512]{1,0:T(8,128)(2,1)}, u32[]{:S(2)}, u32[]{:S(2)}) %collective-permute-start.5) | collective-permute-done | bytes 524320 | tf_op jit(solution)/shard_map/ppermute | solution.py:29
  97.8 4.8 %shard_map.86 = f32[256,2048]{1,0:T(8,128)} custom-call(s32[4]{0:T(128)S(1)} %pad_add_fusion.at_ref, bf16[256,1024]{1,0:T(8,128)(2,1)} %collective-permute-done.9.og_ref.oog_ref, bf16[512,512]{1,0:T(8,128)(2,1)} %shard_map.84.a0, bf16[512,512]{1,0:T(8,128)(2,1)} %collective-permute-done.3.a1, bf16[512,512]{1,0:T(8,128)(2,1)} %collective-permute-done.4.a2, ...), custom_call_target="tpu_custom_call" | custom-call | flops 1073741824 | bytes 6815760 | tf_op jit(solution)/shard_map/pallas_call | solution.py:52
  102.7 14.5 %collective-permute-start.10 = (f32[256,2048]{1,0:T(8,128)}, f32[256,2048]{1,0:T(8,128)}, u32[]{:S(2)}, u32[]{:S(2)}) collective-permute-start(f32[256,2048]{1,0:T(8,128)} %shard_map.86), channel_id=1, source_target_pairs={{0,16},{16,0},{1,17},{17,1},{2,18},{18,2},{3,19},{19,3},{4,20},{20... | collective-permute-start | bytes 6291464 | tf_op jit(solution)/shard_map/ppermute | solution.py:25
  117.2 3.6 %shard_map.94 = (bf16[2048,128]{1,0:T(8,128)(2,1)S(1)}, bf16[2048,128]{1,0:T(8,128)(2,1)S(1)}, bf16[2048,128]{1,0:T(8,128)(2,1)S(1)}, bf16[2048,128]{1,0:T(8,128)(2,1)S(1)}) custom-call(s32[4]{0:T(128)S(1)} %pad_add_fusion.at_ref, bf16[2048,256]{1,0:T(8,128)(2,1)} %shard_map.93.mine_ref, bf16[2048,256]{1,0:T(8,128)(2,1)} %collective-permute-done.11.theirs_ref, ...), custom_call_target="tpu_custom_call" | custom-call | flops 1073741824 | bytes 5767184 | tf_op jit(solution)/shard_map/pallas_call | solution.py:52
  120.8 1.9 collective-permute-start.12
  122.9 2.4 collective-permute-start.14
  125.4 2.9 %shard_map.96 = (bf16[512,512]{1,0:T(8,128)(2,1)S(1)}, bf16[512,512]{1,0:T(8,128)(2,1)S(1)}, bf16[512,512]{1,0:T(8,128)(2,1)S(1)}, bf16[512,512]{1,0:T(8,128)(2,1)S(1)}) custom-call(s32[4]{0:T(128)S(1)} %pad_add_fusion.at_ref, bf16[2048,256]{1,0:T(8,128)(2,1)} %shard_map.93.mine_ref, bf16[2048,256]{1,0:T(8,128)(2,1)} %collective-permute-done.11.theirs_ref, ...), custom_call_target="tpu_custom_call" | custom-call | flops 1073741824 | bytes 5767184 | tf_op jit(solution)/shard_map/pallas_call | solution.py:52
  128.4 18.4 %collective-permute-done.12.refs_1_ = bf16[2048,128]{1,0:T(8,128)(2,1)S(1)} collective-permute-done((bf16[2048,128]{1,0:T(8,128)(2,1)S(1)}, bf16[2048,128]{1,0:T(8,128)(2,1)S(1)}, u32[]{:S(2)}, u32[]{:S(2)}) %collective-permute-start.12) | collective-permute-done | bytes 524320 | tf_op jit(solution)/shard_map/ppermute | solution.py:34
  146.8 4.4 %collective-permute-start.20 = (bf16[512,512]{1,0:T(8,128)(2,1)S(1)}, bf16[512,512]{1,0:T(8,128)(2,1)S(1)}, u32[]{:S(2)}, u32[]{:S(2)}) collective-permute-start(bf16[512,512]{1,0:T(8,128)(2,1)S(1)} %get-tuple-element.39), channel_id=1, source_target_pairs={{0,12},{4,0},{8,4},{12,8},{1,13},{5,1},{9,5},{13,9},{2,14},{6,2},{... | collective-permute-start | bytes 1572872 | tf_op jit(solution)/shard_map/ppermute | solution.py:34
  152.7 1.9 collective-permute-start.16
  154.6 6.4 %collective-permute-done.19.refs_2_ = bf16[512,512]{1,0:T(8,128)(2,1)S(1)} collective-permute-done((bf16[512,512]{1,0:T(8,128)(2,1)S(1)}, bf16[512,512]{1,0:T(8,128)(2,1)S(1)}, u32[]{:S(2)}, u32[]{:S(2)}) %collective-permute-start.19) | collective-permute-done | bytes 524320 | tf_op jit(solution)/shard_map/ppermute | solution.py:34
  160.9 4.4 %collective-permute-start.17 = (bf16[512,128]{1,0:T(8,128)(2,1)S(1)}, bf16[512,128]{1,0:T(8,128)(2,1)S(1)}, u32[]{:S(2)}, u32[]{:S(2)}) collective-permute-start(bf16[512,128]{1,0:T(8,128)(2,1)S(1)} %get-tuple-element.35), channel_id=1, source_target_pairs={{0,12},{4,0},{8,4},{12,8},{1,13},{5,1},{9,5},{13,9},{2,14},{6,2},{... | collective-permute-start | bytes 393224 | tf_op jit(solution)/shard_map/ppermute | solution.py:34
  165.4 8.8 %collective-permute-done.20.refs_3_ = bf16[512,512]{1,0:T(8,128)(2,1)S(1)} collective-permute-done((bf16[512,512]{1,0:T(8,128)(2,1)S(1)}, bf16[512,512]{1,0:T(8,128)(2,1)S(1)}, u32[]{:S(2)}, u32[]{:S(2)}) %collective-permute-start.20) | collective-permute-done | bytes 524320 | tf_op jit(solution)/shard_map/ppermute | solution.py:34
  175.3 2.6 collective-permute-start.23
  177.9 1.9 collective-permute-done.17.refs_3_
  179.8 1.7 collective-permute-done.21.refs_5_
  183.1 18.1 %all-to-all-start.5 = ((bf16[8,128,128]{2,1,0:T(8,128)(2,1)}), bf16[8,128,128]{2,1,0:T(8,128)(2,1)S(1)}, u32[]{:S(2)}, u32[]{:S(2)}) async-start(bf16[8,128,128]{2,1,0:T(8,128)(2,1)} %copy-done.18), calls=%async_computation.5 | async-start | bytes 524288 | tf_op jit(solution)/shard_map/all_to_all | solution.py:335
  205.5 3.1 %shard_map.85.mine_ref = f32[256,2048]{1,0:T(8,128)S(1)} custom-call(s32[4]{0:T(128)S(1)} %pad_add_fusion.at_ref, bf16[256,2048]{1,0:T(8,128)(2,1)S(1)} %bitcast.27, bf16[512,512]{1,0:T(8,128)(2,1)} %shard_map.84.a0, bf16[512,512]{1,0:T(8,128)(2,1)} %collective-permute-done.3.a1, bf16[512,512]{1,0:T(8,128)(2,1)} %collective-permute-done.4.a2, ...), custom_call_target="tpu_custom_call" | custom-call | flops 1073741824 | bytes 7340048 | tf_op jit(solution)/shard_map/pallas_call | solution.py:52
  208.6 3.2 %shard_map.87 = (bf16[256,2048]{1,0:T(8,128)(2,1)S(1)}, bf16[16,128,128]{2,1,0:T(8,128)(2,1)S(1)}) custom-call(f32[256,2048]{1,0:T(8,128)S(1)} %shard_map.85.mine_ref, f32[256,2048]{1,0:T(8,128)} %collective-permute-done.10.theirs_ref, bf16[256,2048]{1,0:T(8,128)(2,1)S(1)} %bitcast.23), custom_call_target="tpu_custom_call" | custom-call | flops 134217728 | bytes 6815744 | tf_op jit(solution)/shard_map/pallas_call | solution.py:52
  213.6 9.9 %all-to-all-start.3 = ((bf16[16,128,128]{2,1,0:T(8,128)(2,1)}), bf16[16,128,128]{2,1,0:T(8,128)(2,1)}, u32[]{:S(2)}, u32[]{:S(2)}) async-start(bf16[16,128,128]{2,1,0:T(8,128)(2,1)} %copy-done.22), calls=%async_computation.3 | async-start | bytes 1048576 | tf_op jit(solution)/shard_map/all_to_all | solution.py:272
  224.3 8.9 %all-to-all-done.3.i_ref = bf16[16,128,128]{2,1,0:T(8,128)(2,1)} async-done(((bf16[16,128,128]{2,1,0:T(8,128)(2,1)}), bf16[16,128,128]{2,1,0:T(8,128)(2,1)}, u32[]{:S(2)}, u32[]{:S(2)}) %all-to-all-start.3) | async-done | bytes 524320 | tf_op jit(solution)/shard_map/all_to_all | solution.py:272
  233.2 5.2 %all-to-all-start.6 = ((bf16[16,128,128]{2,1,0:T(8,128)(2,1)}), bf16[16,128,128]{2,1,0:T(8,128)(2,1)}, u32[]{:S(2)}, u32[]{:S(2)}) async-start(bf16[16,128,128]{2,1,0:T(8,128)(2,1)} %copy-done.11), calls=%async_computation.6 | async-start | bytes 1048576 | tf_op jit(solution)/shard_map/all_to_all | solution.py:337
  240.4 7.9 %all-to-all-done.6.i_ref = bf16[16,128,128]{2,1,0:T(8,128)(2,1)} async-done(((bf16[16,128,128]{2,1,0:T(8,128)(2,1)}), bf16[16,128,128]{2,1,0:T(8,128)(2,1)}, u32[]{:S(2)}, u32[]{:S(2)}) %all-to-all-start.6) | async-done | bytes 524320 | tf_op jit(solution)/shard_map/all_to_all | solution.py:337
  248.3 5.2 %all-to-all-start.4 = ((bf16[16,128,128]{2,1,0:T(8,128)(2,1)}), bf16[16,128,128]{2,1,0:T(8,128)(2,1)}, u32[]{:S(2)}, u32[]{:S(2)}) async-start(bf16[16,128,128]{2,1,0:T(8,128)(2,1)} %copy-done.10), calls=%async_computation.4 | async-start | bytes 1048576 | tf_op jit(solution)/shard_map/all_to_all | solution.py:274
  254.7 4.3 %shard_map.90 = bf16[256,2048]{1,0:T(8,128)(2,1)} custom-call(bf16[256,2048]{1,0:T(8,128)(2,1)S(1)} %copy-done.20, bf16[256,2048]{1,0:T(8,128)(2,1)S(1)} %bitcast.16, bf16[256,2048]{1,0:T(8,128)(2,1)S(1)} %bitcast.20, bf16[16,128,128]{2,1,0:T(8,128)(2,1)S(1)} %all-to-all-done.2.p_ref), custom_call_target="tpu_custom_call" | custom-call | flops 671088640 | bytes 4718592 | tf_op jit(solution)/shard_map/pallas_call | solution.py:52
  259.1 2.1 shard_map.100
  261.2 2.2 all-to-all-done.4.l_ref
  265.8 7.8 %shard_map.92 = (bf16[256,2048]{1,0:T(8,128)(2,1)}, bf16[256,2048]{1,0:T(8,128)(2,1)}) custom-call(bf16[256,2048]{1,0:T(8,128)(2,1)S(1)} %copy-done.21, bf16[256,2048]{1,0:T(8,128)(2,1)S(1)} %bitcast.24, bf16[256,2048]{1,0:T(8,128)(2,1)S(1)} %bitcast.17, bf16[256,2048]{1,0:T(8,128)(2,1)S(1)} %bitcast.21, bf16[16,128,128]{2,1,0:T(8,128)(2,1)} %all-to-all-done.4.l_ref), custom_call_target="tpu_custom_call" | custom-call | flops 1342177280 | bytes 6815744 | tf_op jit(solution)/shard_map/pallas_call | solution.py:52
  (81 shorter events, 22.8 us)
Async XLA Ops:
  0.6 26.1 %copy-start = (bf16[128,2048]{1,0:T(8,128)(2,1)S(1)}, bf16[128,2048]{1,0:T(8,128)(2,1)}, u32[]{:S(2)}) copy-start(bf16[128,2048]{1,0:T(8,128)(2,1)} %param.8) | copy-start | bytes 1572868
  0.6 1.3 copy-start.1
  1.9 1.2 copy-start.3
  22.1 14.4 %all-to-all-start.2 = ((bf16[16,128,128]{2,1,0:T(8,128)(2,1)}), bf16[16,128,128]{2,1,0:T(8,128)(2,1)S(1)}, u32[]{:S(2)}, u32[]{:S(2)}) async-start(bf16[16,128,128]{2,1,0:T(8,128)(2,1)} %shard_map.89), calls=%async_computation.2 | async-start | bytes 1048576 | tf_op jit(solution)/shard_map/all_to_all | solution.py:274
  26.7 44.5 %copy-start.2 = (bf16[1,256,2048]{2,1,0:T(8,128)(2,1)S(1)}, bf16[1,256,2048]{2,1,0:T(8,128)(2,1)}, u32[]{:S(2)}) copy-start(bf16[1,256,2048]{2,1,0:T(8,128)(2,1)} %param.6) | copy-start | bytes 3145732
  26.7 44.5 %copy-start.4 = (bf16[1,256,2048]{2,1,0:T(8,128)(2,1)S(1)}, bf16[1,256,2048]{2,1,0:T(8,128)(2,1)}, u32[]{:S(2)}) copy-start(bf16[1,256,2048]{2,1,0:T(8,128)(2,1)} %param.7) | copy-start | bytes 3145732
  37.4 43.5 %all-to-all-start = ((bf16[16,128,128]{2,1,0:T(8,128)(2,1)}), bf16[16,128,128]{2,1,0:T(8,128)(2,1)}, u32[]{:S(2)}, u32[]{:S(2)}) async-start(bf16[16,128,128]{2,1,0:T(8,128)(2,1)} %broadcast_in_dim.15), calls=%async_computation | async-start | bytes 1048576 | tf_op jit(solution)/shard_map/all_to_all | solution.py:281
  47.3 14.2 %collective-permute-start = (bf16[128,512]{1,0:T(8,128)(2,1)S(1)}, bf16[128,512]{1,0:T(8,128)(2,1)S(1)}, u32[]{:S(2)}, u32[]{:S(2)}) collective-permute-start(bf16[128,512]{1,0:T(8,128)(2,1)S(1)} %constant_dynamic-slice_fusion.1.refs_0_), channel_id=1, source_target_pairs={{1,0},{2,1},{3,2},{0,3},{5,4},{6,5},{7,6},{4,7},{9,8},{10,9},{11,1... | collective-permute-start | bytes 393224 | tf_op jit(solution)/shard_map/ppermute | solution.py:29
  50.8 15.1 %collective-permute-start.1 = (bf16[128,512]{1,0:T(8,128)(2,1)S(1)}, bf16[128,512]{1,0:T(8,128)(2,1)S(1)}, u32[]{:S(2)}, u32[]{:S(2)}) collective-permute-start(bf16[128,512]{1,0:T(8,128)(2,1)S(1)} %constant_dynamic-slice_fusion.1.refs_0_), channel_id=1, source_target_pairs={{2,0},{3,1},{0,2},{1,3},{6,4},{7,5},{4,6},{5,7},{10,8},{11,9},{8,1... | collective-permute-start | bytes 393224 | tf_op jit(solution)/shard_map/ppermute | solution.py:29
  52.9 13.7 %collective-permute-start.2 = (bf16[128,512]{1,0:T(8,128)(2,1)S(1)}, bf16[128,512]{1,0:T(8,128)(2,1)}, u32[]{:S(2)}, u32[]{:S(2)}) collective-permute-start(bf16[128,512]{1,0:T(8,128)(2,1)S(1)} %constant_dynamic-slice_fusion.1.refs_0_), channel_id=1, source_target_pairs={{3,0},{0,1},{1,2},{2,3},{7,4},{4,5},{5,6},{6,7},{11,8},{8,9},{9,10... | collective-permute-start | bytes 393224 | tf_op jit(solution)/shard_map/ppermute | solution.py:29
  56.8 24.0 %collective-permute-start.9 = (bf16[256,1024]{1,0:T(8,128)(2,1)}, bf16[256,1024]{1,0:T(8,128)(2,1)}, u32[]{:S(2)}, u32[]{:S(2)}) collective-permute-start(bf16[256,1024]{1,0:T(8,128)(2,1)} %dynamic-slice_bitcast_fusion), channel_id=1, source_target_pairs={{0,16},{16,0},{1,17},{17,1},{2,18},{18,2},{3,19},{19,3},{4,20},{20... | collective-permute-start | bytes 1572872 | tf_op jit(solution)/shard_map/ppermute | solution.py:25
  68.3 13.9 %collective-permute-start.3 = (bf16[512,512]{1,0:T(8,128)(2,1)}, bf16[512,512]{1,0:T(8,128)(2,1)}, u32[]{:S(2)}, u32[]{:S(2)}) collective-permute-start(bf16[512,512]{1,0:T(8,128)(2,1)} %shard_map.84.a0), channel_id=1, source_target_pairs={{4,0},{8,4},{12,8},{0,12},{5,1},{9,5},{13,9},{1,13},{6,2},{10,6},{... | collective-permute-start | bytes 1572872 | tf_op jit(solution)/shard_map/ppermute | solution.py:29
  70.7 14.4 %collective-permute-start.4 = (bf16[512,512]{1,0:T(8,128)(2,1)}, bf16[512,512]{1,0:T(8,128)(2,1)}, u32[]{:S(2)}, u32[]{:S(2)}) collective-permute-start(bf16[512,512]{1,0:T(8,128)(2,1)} %shard_map.84.a0), channel_id=1, source_target_pairs={{8,0},{12,4},{0,8},{4,12},{9,1},{13,5},{1,9},{5,13},{10,2},{14,6},... | collective-permute-start | bytes 1572872 | tf_op jit(solution)/shard_map/ppermute | solution.py:29
  71.3 1.2 copy-start.5
  76.3 40.9 %collective-permute-start.11 = (bf16[2048,256]{1,0:T(8,128)(2,1)}, bf16[2048,256]{1,0:T(8,128)(2,1)}, u32[]{:S(2)}, u32[]{:S(2)}) collective-permute-start(bf16[2048,256]{1,0:T(8,128)(2,1)} %shard_map.93.mine_ref), channel_id=1, source_target_pairs={{0,16},{16,0},{1,17},{17,1},{2,18},{18,2},{3,19},{19,3},{4,20},{20... | collective-permute-start | bytes 3145736 | tf_op jit(solution)/shard_map/ppermute | solution.py:25
  80.3 17.4 %collective-permute-start.5 = (bf16[512,512]{1,0:T(8,128)(2,1)}, bf16[512,512]{1,0:T(8,128)(2,1)}, u32[]{:S(2)}, u32[]{:S(2)}) collective-permute-start(bf16[512,512]{1,0:T(8,128)(2,1)} %shard_map.84.a0), channel_id=1, source_target_pairs={{12,0},{0,4},{4,8},{8,12},{13,1},{1,5},{5,9},{9,13},{14,2},{2,6},{... | collective-permute-start | bytes 1572872 | tf_op jit(solution)/shard_map/ppermute | solution.py:29
  80.8 36.4 %copy-start.8 = (bf16[1,256,2048]{2,1,0:T(8,128)(2,1)S(1)}, bf16[1,256,2048]{2,1,0:T(8,128)(2,1)}, u32[]{:S(2)}) copy-start(bf16[1,256,2048]{2,1,0:T(8,128)(2,1)} %param.9) | copy-start | bytes 3145732
  80.8 16.8 %collective-permute-start.6 = (bf16[2048,128]{1,0:T(8,128)(2,1)}, bf16[2048,128]{1,0:T(8,128)(2,1)S(1)}, u32[]{:S(2)}, u32[]{:S(2)}) collective-permute-start(bf16[2048,128]{1,0:T(8,128)(2,1)} %bitcast.5.b0), channel_id=1, source_target_pairs={{64,0},{128,64},{192,128},{0,192},{65,1},{129,65},{193,129},{1,193... | collective-permute-start | bytes 1572872 | tf_op jit(solution)/shard_map/ppermute | solution.py:29
  82.1 15.5 %collective-permute-start.7 = (bf16[2048,128]{1,0:T(8,128)(2,1)}, bf16[2048,128]{1,0:T(8,128)(2,1)S(1)}, u32[]{:S(2)}, u32[]{:S(2)}) collective-permute-start(bf16[2048,128]{1,0:T(8,128)(2,1)} %bitcast.5.b0), channel_id=1, source_target_pairs={{128,0},{192,64},{0,128},{64,192},{129,1},{193,65},{1,129},{65,193... | collective-permute-start | bytes 1572872 | tf_op jit(solution)/shard_map/ppermute | solution.py:29
  85.1 12.7 %collective-permute-start.8 = (bf16[2048,128]{1,0:T(8,128)(2,1)}, bf16[2048,128]{1,0:T(8,128)(2,1)S(1)}, u32[]{:S(2)}, u32[]{:S(2)}) collective-permute-start(bf16[2048,128]{1,0:T(8,128)(2,1)} %bitcast.5.b0), channel_id=1, source_target_pairs={{192,0},{0,64},{64,128},{128,192},{193,1},{1,65},{65,129},{129,193... | collective-permute-start | bytes 1572872 | tf_op jit(solution)/shard_map/ppermute | solution.py:29
  97.6 5.0 %copy-start.12 = (bf16[2048,128]{1,0:T(8,128)(2,1)}, bf16[2048,128]{1,0:T(8,128)(2,1)S(1)}, u32[]{:S(2)}) copy-start(bf16[2048,128]{1,0:T(8,128)(2,1)S(1)} %collective-permute-done.6.b1) | copy-start | bytes 1572868
  97.6 5.0 %copy-start.14 = (bf16[2048,128]{1,0:T(8,128)(2,1)}, bf16[2048,128]{1,0:T(8,128)(2,1)S(1)}, u32[]{:S(2)}) copy-start(bf16[2048,128]{1,0:T(8,128)(2,1)S(1)} %collective-permute-done.7.b2) | copy-start | bytes 1572868
  97.8 4.8 %copy-start.16 = (bf16[2048,128]{1,0:T(8,128)(2,1)}, bf16[2048,128]{1,0:T(8,128)(2,1)S(1)}, u32[]{:S(2)}) copy-start(bf16[2048,128]{1,0:T(8,128)(2,1)S(1)} %collective-permute-done.8.b3) | copy-start | bytes 1572868
  102.7 105.9 %collective-permute-start.10 = (f32[256,2048]{1,0:T(8,128)}, f32[256,2048]{1,0:T(8,128)}, u32[]{:S(2)}, u32[]{:S(2)}) collective-permute-start(f32[256,2048]{1,0:T(8,128)} %shard_map.86), channel_id=1, source_target_pairs={{0,16},{16,0},{1,17},{17,1},{2,18},{18,2},{3,19},{19,3},{4,20},{20... | collective-permute-start | bytes 6291464 | tf_op jit(solution)/shard_map/ppermute | solution.py:25
  120.8 26.0 %collective-permute-start.12 = (bf16[2048,128]{1,0:T(8,128)(2,1)S(1)}, bf16[2048,128]{1,0:T(8,128)(2,1)S(1)}, u32[]{:S(2)}, u32[]{:S(2)}) collective-permute-start(bf16[2048,128]{1,0:T(8,128)(2,1)S(1)} %get-tuple-element.29), channel_id=1, source_target_pairs={{0,64},{64,128},{128,192},{192,0},{1,65},{65,129},{129,193},{193,1... | collective-permute-start | bytes 1572872 | tf_op jit(solution)/shard_map/ppermute | solution.py:34
  122.7 24.1 %collective-permute-start.13 = (bf16[2048,128]{1,0:T(8,128)(2,1)S(1)}, bf16[2048,128]{1,0:T(8,128)(2,1)S(1)}, u32[]{:S(2)}, u32[]{:S(2)}) collective-permute-start(bf16[2048,128]{1,0:T(8,128)(2,1)S(1)} %get-tuple-element.30), channel_id=1, source_target_pairs={{0,128},{64,192},{128,0},{192,64},{1,129},{65,193},{129,1},{193,65... | collective-permute-start | bytes 1572872 | tf_op jit(solution)/shard_map/ppermute | solution.py:34
  122.9 28.3 %collective-permute-start.14 = (bf16[2048,128]{1,0:T(8,128)(2,1)S(1)}, bf16[2048,128]{1,0:T(8,128)(2,1)S(1)}, u32[]{:S(2)}, u32[]{:S(2)}) collective-permute-start(bf16[2048,128]{1,0:T(8,128)(2,1)S(1)} %get-tuple-element.31), channel_id=1, source_target_pairs={{0,192},{64,0},{128,64},{192,128},{1,193},{65,1},{129,65},{193,129... | collective-permute-start | bytes 1572872 | tf_op jit(solution)/shard_map/ppermute | solution.py:34
  128.3 24.4 %collective-permute-start.18 = (bf16[512,512]{1,0:T(8,128)(2,1)S(1)}, bf16[512,512]{1,0:T(8,128)(2,1)S(1)}, u32[]{:S(2)}, u32[]{:S(2)}) collective-permute-start(bf16[512,512]{1,0:T(8,128)(2,1)S(1)} %get-tuple-element.37), channel_id=1, source_target_pairs={{0,4},{4,8},{8,12},{12,0},{1,5},{5,9},{9,13},{13,1},{2,6},{6,10},{... | collective-permute-start | bytes 1572872 | tf_op jit(solution)/shard_map/ppermute | solution.py:34
  146.8 14.1 %collective-permute-start.19 = (bf16[512,512]{1,0:T(8,128)(2,1)S(1)}, bf16[512,512]{1,0:T(8,128)(2,1)S(1)}, u32[]{:S(2)}, u32[]{:S(2)}) collective-permute-start(bf16[512,512]{1,0:T(8,128)(2,1)S(1)} %get-tuple-element.38), channel_id=1, source_target_pairs={{0,8},{4,12},{8,0},{12,4},{1,9},{5,13},{9,1},{13,5},{2,10},{6,14},... | collective-permute-start | bytes 1572872 | tf_op jit(solution)/shard_map/ppermute | solution.py:34
  146.8 27.4 %collective-permute-start.20 = (bf16[512,512]{1,0:T(8,128)(2,1)S(1)}, bf16[512,512]{1,0:T(8,128)(2,1)S(1)}, u32[]{:S(2)}, u32[]{:S(2)}) collective-permute-start(bf16[512,512]{1,0:T(8,128)(2,1)S(1)} %get-tuple-element.39), channel_id=1, source_target_pairs={{0,12},{4,0},{8,4},{12,8},{1,13},{5,1},{9,5},{13,9},{2,14},{6,2},{... | collective-permute-start | bytes 1572872 | tf_op jit(solution)/shard_map/ppermute | solution.py:34
  152.0 23.1 %collective-permute-start.15 = (bf16[512,128]{1,0:T(8,128)(2,1)S(1)}, bf16[512,128]{1,0:T(8,128)(2,1)S(1)}, u32[]{:S(2)}, u32[]{:S(2)}) collective-permute-start(bf16[512,128]{1,0:T(8,128)(2,1)S(1)} %get-tuple-element.33), channel_id=1, source_target_pairs={{0,4},{4,8},{8,12},{12,0},{1,5},{5,9},{9,13},{13,1},{2,6},{6,10},{... | collective-permute-start | bytes 393224 | tf_op jit(solution)/shard_map/ppermute | solution.py:34
  152.7 22.6 %collective-permute-start.16 = (bf16[512,128]{1,0:T(8,128)(2,1)S(1)}, bf16[512,128]{1,0:T(8,128)(2,1)S(1)}, u32[]{:S(2)}, u32[]{:S(2)}) collective-permute-start(bf16[512,128]{1,0:T(8,128)(2,1)S(1)} %get-tuple-element.34), channel_id=1, source_target_pairs={{0,8},{4,12},{8,0},{12,4},{1,9},{5,13},{9,1},{13,5},{2,10},{6,14},... | collective-permute-start | bytes 393224 | tf_op jit(solution)/shard_map/ppermute | solution.py:34
  160.9 18.9 %collective-permute-start.17 = (bf16[512,128]{1,0:T(8,128)(2,1)S(1)}, bf16[512,128]{1,0:T(8,128)(2,1)S(1)}, u32[]{:S(2)}, u32[]{:S(2)}) collective-permute-start(bf16[512,128]{1,0:T(8,128)(2,1)S(1)} %get-tuple-element.35), channel_id=1, source_target_pairs={{0,12},{4,0},{8,4},{12,8},{1,13},{5,1},{9,5},{13,9},{2,14},{6,2},{... | collective-permute-start | bytes 393224 | tf_op jit(solution)/shard_map/ppermute | solution.py:34
  175.0 6.5 %collective-permute-start.21 = (bf16[512,128]{1,0:T(8,128)(2,1)S(1)}, bf16[512,128]{1,0:T(8,128)(2,1)S(1)}, u32[]{:S(2)}, u32[]{:S(2)}) collective-permute-start(bf16[512,128]{1,0:T(8,128)(2,1)S(1)} %get-tuple-element.41), channel_id=1, source_target_pairs={{0,64},{64,128},{128,192},{192,0},{1,65},{65,129},{129,193},{193,1... | collective-permute-start | bytes 393224 | tf_op jit(solution)/shard_map/ppermute | solution.py:34
  175.1 6.4 %collective-permute-start.22 = (bf16[512,128]{1,0:T(8,128)(2,1)S(1)}, bf16[512,128]{1,0:T(8,128)(2,1)S(1)}, u32[]{:S(2)}, u32[]{:S(2)}) collective-permute-start(bf16[512,128]{1,0:T(8,128)(2,1)S(1)} %get-tuple-element.42), channel_id=1, source_target_pairs={{0,128},{64,192},{128,0},{192,64},{1,129},{65,193},{129,1},{193,65... | collective-permute-start | bytes 393224 | tf_op jit(solution)/shard_map/ppermute | solution.py:34
  175.3 6.9 %collective-permute-start.23 = (bf16[512,128]{1,0:T(8,128)(2,1)S(1)}, bf16[512,128]{1,0:T(8,128)(2,1)S(1)}, u32[]{:S(2)}, u32[]{:S(2)}) collective-permute-start(bf16[512,128]{1,0:T(8,128)(2,1)S(1)} %get-tuple-element.43), channel_id=1, source_target_pairs={{0,192},{64,0},{128,64},{192,128},{1,193},{65,1},{129,65},{193,129... | collective-permute-start | bytes 393224 | tf_op jit(solution)/shard_map/ppermute | solution.py:34
  183.1 30.5 %all-to-all-start.5 = ((bf16[8,128,128]{2,1,0:T(8,128)(2,1)}), bf16[8,128,128]{2,1,0:T(8,128)(2,1)S(1)}, u32[]{:S(2)}, u32[]{:S(2)}) async-start(bf16[8,128,128]{2,1,0:T(8,128)(2,1)} %copy-done.18), calls=%async_computation.5 | async-start | bytes 524288 | tf_op jit(solution)/shard_map/all_to_all | solution.py:335
  201.1 1.2 copy-start.9
  202.3 1.0 copy-start.13
  203.4 1.0 copy-start.15
  204.4 1.0 copy-start.17
  205.5 3.1 %copy-start.6 = (bf16[1,256,2048]{2,1,0:T(8,128)(2,1)S(1)}, bf16[1,256,2048]{2,1,0:T(8,128)(2,1)}, u32[]{:S(2)}) copy-start(bf16[1,256,2048]{2,1,0:T(8,128)(2,1)} %param.5) | copy-start | bytes 3145732
  213.6 19.6 %all-to-all-start.3 = ((bf16[16,128,128]{2,1,0:T(8,128)(2,1)}), bf16[16,128,128]{2,1,0:T(8,128)(2,1)}, u32[]{:S(2)}, u32[]{:S(2)}) async-start(bf16[16,128,128]{2,1,0:T(8,128)(2,1)} %copy-done.22), calls=%async_computation.3 | async-start | bytes 1048576 | tf_op jit(solution)/shard_map/all_to_all | solution.py:272
  233.2 15.1 %all-to-all-start.6 = ((bf16[16,128,128]{2,1,0:T(8,128)(2,1)}), bf16[16,128,128]{2,1,0:T(8,128)(2,1)}, u32[]{:S(2)}, u32[]{:S(2)}) async-start(bf16[16,128,128]{2,1,0:T(8,128)(2,1)} %copy-done.11), calls=%async_computation.6 | async-start | bytes 1048576 | tf_op jit(solution)/shard_map/all_to_all | solution.py:337
  248.3 15.1 %all-to-all-start.4 = ((bf16[16,128,128]{2,1,0:T(8,128)(2,1)}), bf16[16,128,128]{2,1,0:T(8,128)(2,1)}, u32[]{:S(2)}, u32[]{:S(2)}) async-start(bf16[16,128,128]{2,1,0:T(8,128)(2,1)} %copy-done.10), calls=%async_computation.4 | async-start | bytes 1048576 | tf_op jit(solution)/shard_map/all_to_all | solution.py:274
  253.5 1.2 copy-start.20
  263.4 1.2 copy-start.7
  264.6 1.2 copy-start.21
  (5 other events, 4.1 us)
where the time goes:
time: 275 us; the launch traced here: 274 us
  starting transfers between devices  109 us (40%)
  waiting for transfers between devices  85.6 us (31%)
  Pallas kernels  42.6 us (15%)
  local copies, waits for them, and re-layouts  18.6 us (7%)
  blocking collectives  16.8 us (6%)
    pallas_call x17, Pallas kernels, call(): pl.pallas_call(body, out_shape=out, in_specs=list(in_specs), out_specs=ou...  42.6 us
    ppermute x12, waiting for transfers between devices, spread(): lax.ppermute(pieces[k], axis, [(i, (i + k) % 4) for i in range(4)])  37.9 us
    ppermute x3, starting transfers between devices, from_core(): return lax.ppermute(v, 'c', [(0, 1), (1, 0)])  21.1 us
    ppermute x9, waiting for transfers between devices, copies(): lax.ppermute(v, axis, [((i + k) % 4, i) for i in range(4)])  18.9 us
    ppermute x12, starting transfers between devices, spread(): lax.ppermute(pieces[k], axis, [(i, (i + k) % 4) for i in range(4)])  18.8 us
    all_to_all x1, starting transfers between devices, local(): gz = lax.all_to_all(gz, ('zl', 'zh'), 0, 0)  18.1 us
    all_to_all x1, blocking collectives, exchange(): by_head = lax.all_to_all(states, CTX, 0, 0)  16.8 us
    ppermute x9, starting transfers between devices, copies(): lax.ppermute(v, axis, [((i + k) % 4, i) for i in range(4)])  16.2 us
  transfers between devices with their start and end apart: 30, of which 15 were waited for; matrix products, arithmetic and copies ran while one was open for 1% of the time, Pallas kernels for 12%

commit v1 on v0

--- a/solution.py
+++ b/solution.py
@@ -48,7 +48,7 @@
         in_specs = [small if a.dtype == jnp.int32 else full for a in args]
         out_specs = jax.tree.map(lambda o: full, out)
     if room is None:
-        room = 2 * size + 8 * 2**20
+        room = size + 6 * 2**20
     return pl.pallas_call(
         body,
         out_shape=out,
@@ -203,17 +203,20 @@
         refs[4 + k][...] = total.astype(BF16)
 
 
-def add_then_z_body(*refs):
-    size = refs[8].shape[1]
-    for first, total in ((0, added(refs[:4])), (4, added(refs[4:8]))):
-        for n in range(4):
-            refs[8][first + n] = total[n * size : (n + 1) * size, :].astype(BF16)
-
-
-def add_then_all_body(i_ref, o_ref):
-    total = added([i_ref.at[n] for n in range(i_ref.shape[0])]).astype(BF16)
-    for n in range(o_ref.shape[0]):
-        o_ref[n] = total
+def add_then_z_body(at_ref, *refs):
+    size = refs[8].shape[0]
+    low = at_ref[4] == 0
+    for k in range(4):
+        s = block(at_ref[3], k, size)
+        via_x, via_y = added([ref.at[s, :] for ref in refs[:4]]), added([ref.at[s, :] for ref in refs[4:8]])
+        refs[8 + k][...] = jnp.where(low, via_x, via_y).astype(BF16)
+        refs[12 + k][...] = jnp.where(low, via_y, via_x).astype(BF16)
+
+
+def add_then_all_body(*refs):
+    total = added(refs[:8]).astype(BF16)
+    for n in range(refs[8].shape[0]):
+        refs[8][n] = total
 
 
 def finish_weight_body(scale, i_ref, o_ref):
@@ -227,6 +230,12 @@
     size = refs[0].shape[0]
     for k in range(4):
         refs[4][block(at_ref[3], k, size), :] = refs[k][...]
+
+
+def stack_body(at_ref, *refs):
+    size = refs[0].shape[0]
+    for k in range(4):
+        refs[4][block(at_ref[2], k, size), :] = refs[k][...]
 
 
 def projected_body(other, at_ref, og_ref, a0, a1, a2, a3, b0, b1, b2, b3, o_ref):
@@ -253,8 +262,8 @@
     q, k, v, og = queries[0], keys[0], values[0], out_grad[0]
     tokens, inner = q.shape
     width = og.shape[1] // 2
-    y, _, core, x, zh = [lax.axis_index(name) for name in AXES]
-    at = jnp.stack([core, y, x, zh]).astype(jnp.int32)
+    y, zl, core, x, zh = [lax.axis_index(name) for name in AXES]
+    at = jnp.stack([core, y, x, zh, zl]).astype(jnp.int32)
     factor = (HEAD * tokens * 16) ** (-0.5)
     scale = (tokens * 16 * 16) ** (-0.5)
     rows = rows_spec(tokens)
@@ -278,7 +287,10 @@
         out_weight, (0, core * width + width // 2 + y * (width // 8)), (out_weight.shape[0], width // 8)
     )
     za = copies(wa, "zh")
-    wb = lax.all_to_all(jnp.broadcast_to(wb[None], (16, *wb.shape)), FSDP, 0, 0).reshape(inner, -1)
+    zb = copies(wb, "zh")
+    wb = call(place_body, shape((4 * out_weight.shape[0], wb.shape[1])), at, *zb)
+    xb = copies(wb, "x")
+    wb = call(stack_body, shape((inner, wb.shape[1])), at, *xb)
     yb = copies(wb, "y")
     wa = call(place_body, shape((4 * out_weight.shape[0], wa.shape[1])), at, *za)
     xa = copies(wa, "x")
@@ -291,6 +303,15 @@
     )
     partner = from_core(attended)
 
+    gw_flops = 2 * inner * 2 * tokens * (width // 2)
+    gy = call(
+        weight_y_body, [shape((inner, width // 8))] * 4, at, attended, partner, og, oog,
+        flops=gw_flops,
+    )
+    gx = call(
+        weight_x_body, [shape((inner // 4, width // 2))] * 4, at, attended, partner, og, oog,
+        flops=gw_flops,
+    )
     project_flops = 2 * tokens * inner * width
     for_partner = call(
         functools.partial(projected_body, True), shape((tokens, inner), F32), at, oog, *xa, *yb,
@@ -298,15 +319,6 @@
     )
     from_partner = from_core(for_partner)
 
-    gw_flops = 2 * inner * 2 * tokens * (width // 2)
-    gy = call(
-        weight_y_body, [shape((inner, width // 8))] * 4, at, attended, partner, og, oog,
-        flops=gw_flops,
-    )
-    gx = call(
-        weight_x_body, [shape((inner // 4, width // 2))] * 4, at, attended, partner, og, oog,
-        flops=gw_flops,
-    )
     mine = call(
         functools.partial(projected_body, False), shape((tokens, inner), F32), at, og, *xa, *yb,
         flops=project_flops,
@@ -327,13 +339,18 @@
         functools.partial(grad_queries_body, factor), shape((tokens, inner)), ga, k, v, prior,
         grid=heads, in_specs=[rows, rows, rows, STATE_SPEC], out_specs=rows, flops=5 * token_flops,
     )
-    gz = call(add_then_z_body, shape((8, inner // 16, width // 8)), *gyx, *gxy)
+    gz = call(add_then_z_body, [shape((inner // 16, width // 8))] * 8, at, *gyx, *gxy)
     grad_keys, grad_values = call(
         functools.partial(grad_keys_values_body, factor), [shape((tokens, inner))] * 2, ga, q, k, v, later,
         grid=heads, in_specs=[rows, rows, rows, rows, STATE_SPEC], out_specs=[rows, rows], flops=10 * token_flops,
     )
-    gz = lax.all_to_all(gz, ("zl", "zh"), 0, 0)
-    total = call(add_then_all_body, shape((16, inner // 16, width // 8)), gz)
+    gz = [gz[0]] + [
+        lax.ppermute(
+            gz[n], ("zl", "zh"), [(i, (i // 4 ^ n // 4) * 4 + (i % 4 + n % 4) % 4) for i in range(8)]
+        )
+        for n in range(1, 8)
+    ]
+    total = call(add_then_all_body, shape((16, inner // 16, width // 8)), *gz)
     gathered = lax.all_to_all(total, CTX, 0, 0)
     grad_weight = call(functools.partial(finish_weight_body, scale), shape((inner // 16, 2 * width), F32), gathered)
 

time: 275 us -> 240 us (0.87)
  waiting for transfers between devices: 85.6 us -> 64.1 us
  blocking collectives: 16.8 us -> 0 us
  Pallas kernels: 42.6 us -> 45.8 us
    all_to_all x2 -> x0, starting transfers between devices: 28 us -> none  [the longest x1 18.1 us: local(): gz = lax.all_to_all(gz, ('zl', 'zh'), 0, 0)]
    all_to_all x1 -> x0, blocking collectives: 16.8 us -> none  [exchange(): by_head = lax.all_to_all(states, CTX, 0, 0)]
    all_to_all x2, starting transfers between devices: 9.86 us -> 25.7 us  [exchange(): return lax.all_to_all(sums, CTX, 0, 0)]
    ppermute x0 -> x7, starting transfers between devices: none -> 13 us  [local(): lax.ppermute(gz[n], ('zl', 'zh'), [(i, (i // 4 ^ n // 4) * 4 + (i % 4 + n...]
    ppermute x12, waiting for transfers between devices: 37.9 us -> 27 us  [spread(): lax.ppermute(pieces[k], axis, [(i, (i + k) % 4) for i in range(4)])]
    all_to_all x2, waiting for transfers between devices: 11.9 us -> 2.17 us  [exchange(): return lax.all_to_all(sums, CTX, 0, 0)]
    ppermute x3, starting transfers between devices: 21.1 us -> 11.5 us  [from_core(): return lax.ppermute(v, 'c', [(0, 1), (1, 0)])]
    ppermute x12, starting transfers between devices: 18.8 us -> 9.83 us  [spread(): lax.ppermute(pieces[k], axis, [(i, (i + k) % 4) for i in range(4)])]
  transfers between devices with their start and end apart: 30 -> 42, of which waited for: 15 -> 16; matrix products, arithmetic and copies ran while one was open for 1% -> 0% of each run, Pallas kernels for 12% -> 15%
where the time goes in v1:
time: 240 us; the launch traced here: 239 us
  starting transfers between devices  110 us (46%)
  waiting for transfers between devices  64.1 us (27%)
  Pallas kernels  45.8 us (19%)
  local copies, waits for them, and re-layouts  18.2 us (8%)
    pallas_call x19, Pallas kernels, call(): pl.pallas_call(body, out_shape=out, in_specs=list(in_specs), out_specs=ou...  45.8 us
    ppermute x12, waiting for transfers between devices, spread(): lax.ppermute(pieces[k], axis, [(i, (i + k) % 4) for i in range(4)])  27 us
    all_to_all x2, starting transfers between devices, exchange(): return lax.all_to_all(sums, CTX, 0, 0)  25.7 us
    ppermute x15, waiting for transfers between devices, copies(): lax.ppermute(v, axis, [((i + k) % 4, i) for i in range(4)])  23.1 us
    ppermute x15, starting transfers between devices, copies(): lax.ppermute(v, axis, [((i + k) % 4, i) for i in range(4)])  22.9 us
    unnamed x56, local copies, waits for them, and re-layouts  18 us
    all_to_all x2, starting transfers between devices, exchange(): by_head = lax.all_to_all(states, CTX, 0, 0)  15.9 us
    ppermute x7, starting transfers between devices, local(): lax.ppermute(gz[n], ('zl', 'zh'), [(i, (i // 4 ^ n // 4) * 4 + (i % 4 + n...  13 us
  transfers between devices with their start and end apart: 42, of which 16 were waited for; matrix products, arithmetic and copies ran while one was open for 0% of the time, Pallas kernels for 15%

profile of v1, /device:TPU:1, one launch (start us, length us, event | category | flops | bytes accessed | tf_op | source)
XLA Modules:
  0.0 238.8 jit_solution(1608476387142588910)
XLA Ops:
  0.7 1.3 copy-done.1
  3.2 2.3 shard_map.90
  5.4 7.3 %all-to-all-start = ((bf16[16,128,128]{2,1,0:T(8,128)(2,1)}), bf16[16,128,128]{2,1,0:T(8,128)(2,1)S(1)}, u32[]{:S(2)}, u32[]{:S(2)}) async-start(bf16[16,128,128]{2,1,0:T(8,128)(2,1)} %shard_map.90), calls=%async_computation | async-start | bytes 1048576 | tf_op jit(solution)/shard_map/all_to_all | solution.py:281
  12.8 5.2 %collective-permute-start = (bf16[128,512]{1,0:T(8,128)(2,1)S(1)}, bf16[128,512]{1,0:T(8,128)(2,1)S(1)}, u32[]{:S(2)}, u32[]{:S(2)}) collective-permute-start(bf16[128,512]{1,0:T(8,128)(2,1)S(1)} %constant_dynamic-slice_fusion.1.refs_0_), channel_id=1, source_target_pairs={{1,0},{2,1},{3,2},{0,3},{5,4},{6,5},{7,6},{4,7},{9,8},{10,9},{11,1... | collective-permute-start | bytes 393224 | tf_op jit(solution)/shard_map/ppermute | solution.py:29
  19.1 2.1 collective-permute-start.2
  22.4 6.6 %collective-permute-done.1.refs_2_ = bf16[128,512]{1,0:T(8,128)(2,1)S(1)} collective-permute-done((bf16[128,512]{1,0:T(8,128)(2,1)S(1)}, bf16[128,512]{1,0:T(8,128)(2,1)S(1)}, u32[]{:S(2)}, u32[]{:S(2)}) %collective-permute-start.1) | collective-permute-done | bytes 131104 | tf_op jit(solution)/shard_map/ppermute | solution.py:29
  29.0 7.0 %collective-permute-done.2.refs_3_ = bf16[128,512]{1,0:T(8,128)(2,1)S(1)} collective-permute-done((bf16[128,512]{1,0:T(8,128)(2,1)S(1)}, bf16[128,512]{1,0:T(8,128)(2,1)S(1)}, u32[]{:S(2)}, u32[]{:S(2)}) %collective-permute-start.2) | collective-permute-done | bytes 131104 | tf_op jit(solution)/shard_map/ppermute | solution.py:29
  36.1 1.4 shard_map.84.a0
  37.4 2.5 %collective-permute-start.3 = (bf16[512,512]{1,0:T(8,128)(2,1)}, bf16[512,512]{1,0:T(8,128)(2,1)S(1)}, u32[]{:S(2)}, u32[]{:S(2)}) collective-permute-start(bf16[512,512]{1,0:T(8,128)(2,1)} %shard_map.84.a0), channel_id=1, source_target_pairs={{4,0},{8,4},{12,8},{0,12},{5,1},{9,5},{13,9},{1,13},{6,2},{10,6},{... | collective-permute-start | bytes 1572872 | tf_op jit(solution)/shard_map/ppermute | solution.py:29
  41.1 1.3 collective-permute-start.7
  43.7 4.5 %collective-permute-done.7.refs_2_ = bf16[128,128]{1,0:T(8,128)(2,1)S(1)} collective-permute-done((bf16[128,128]{1,0:T(8,128)(2,1)S(1)}, bf16[128,128]{1,0:T(8,128)(2,1)S(1)}, u32[]{:S(2)}, u32[]{:S(2)}) %collective-permute-start.7) | collective-permute-done | bytes 32800 | tf_op jit(solution)/shard_map/ppermute | solution.py:29
  50.3 4.8 %collective-permute-done.9.refs_1_ = bf16[512,128]{1,0:T(8,128)(2,1)S(1)} collective-permute-done((bf16[512,128]{1,0:T(8,128)(2,1)S(1)}, bf16[512,128]{1,0:T(8,128)(2,1)S(1)}, u32[]{:S(2)}, u32[]{:S(2)}) %collective-permute-start.9) | collective-permute-done | bytes 131104 | tf_op jit(solution)/shard_map/ppermute | solution.py:29
  56.1 2.9 %collective-permute-start.5 = (bf16[512,512]{1,0:T(8,128)(2,1)}, bf16[512,512]{1,0:T(8,128)(2,1)}, u32[]{:S(2)}, u32[]{:S(2)}) collective-permute-start(bf16[512,512]{1,0:T(8,128)(2,1)} %shard_map.84.a0), channel_id=1, source_target_pairs={{12,0},{0,4},{4,8},{8,12},{13,1},{1,5},{5,9},{9,13},{14,2},{2,6},{... | collective-permute-start | bytes 1572872 | tf_op jit(solution)/shard_map/ppermute | solution.py:29
  59.0 1.4 shard_map.86.b0
  60.4 1.7 collective-permute-start.12
  64.2 20.5 %all-to-all-start.1 = ((bf16[16,128,128]{2,1,0:T(8,128)(2,1)}), bf16[16,128,128]{2,1,0:T(8,128)(2,1)S(1)}, u32[]{:S(2)}, u32[]{:S(2)}) async-start(bf16[16,128,128]{2,1,0:T(8,128)(2,1)} %shard_map.91), calls=%async_computation.1 | async-start | bytes 1048576 | tf_op jit(solution)/shard_map/all_to_all | solution.py:283
  85.9 4.8 %shard_map.88 = f32[256,2048]{1,0:T(8,128)} custom-call(s32[5]{0:T(128)S(1)} %stack.23.at_ref, bf16[256,1024]{1,0:T(8,128)(2,1)} %collective-permute-done.15.og_ref.oog_ref, bf16[512,512]{1,0:T(8,128)(2,1)} %shard_map.84.a0, bf16[512,512]{1,0:T(8,128)(2,1)S(1)} %copy-done.14, bf16[512,512]{1,0:T(8,128)(2,1)} %collective-permute-done.4.a2, ...), custom_call_target="tpu_custom_call" | custom-call | flops 1073741824 | bytes 6815764 | tf_op jit(solution)/shard_map/pallas_call | solution.py:52
  90.7 10.4 %collective-permute-start.16 = (f32[256,2048]{1,0:T(8,128)}, f32[256,2048]{1,0:T(8,128)}, u32[]{:S(2)}, u32[]{:S(2)}) collective-permute-start(f32[256,2048]{1,0:T(8,128)} %shard_map.88), channel_id=1, source_target_pairs={{0,16},{16,0},{1,17},{17,1},{2,18},{18,2},{3,19},{19,3},{4,20},{20... | collective-permute-start | bytes 6291464 | tf_op jit(solution)/shard_map/ppermute | solution.py:25
  102.3 3.1 %shard_map.95.mine_ref = bf16[2048,256]{1,0:T(8,128)(2,1)S(1)} custom-call(bf16[256,2048]{1,0:T(8,128)(2,1)S(1)} %bitcast.22, bf16[256,2048]{1,0:T(8,128)(2,1)S(1)} %bitcast.15, bf16[256,2048]{1,0:T(8,128)(2,1)S(1)} %bitcast.19, bf16[16,128,128]{2,1,0:T(8,128)(2,1)S(1)} %all-to-all-done.1.p_ref), custom_call_target="tpu_custom_call" | custom-call | flops 671088640 | bytes 4718592 | tf_op jit(solution)/shard_map/pallas_call | solution.py:52
  105.6 2.6 %collective-permute-done.17.theirs_ref = bf16[2048,256]{1,0:T(8,128)(2,1)S(1)} collective-permute-done((bf16[2048,256]{1,0:T(8,128)(2,1)S(1)}, bf16[2048,256]{1,0:T(8,128)(2,1)S(1)}, u32[]{:S(2)}, u32[]{:S(2)}) %collective-permute-start.17) | collective-permute-done | bytes 1048608 | tf_op jit(solution)/shard_map/ppermute | solution.py:25
  108.3 4.2 %shard_map.96 = (bf16[2048,128]{1,0:T(8,128)(2,1)S(1)}, bf16[2048,128]{1,0:T(8,128)(2,1)}, bf16[2048,128]{1,0:T(8,128)(2,1)S(1)}, bf16[2048,128]{1,0:T(8,128)(2,1)S(1)}) custom-call(s32[5]{0:T(128)S(1)} %stack.23.at_ref, bf16[2048,256]{1,0:T(8,128)(2,1)S(1)} %shard_map.95.mine_ref, bf16[2048,256]{1,0:T(8,128)(2,1)S(1)} %collective-permute-done.17.theirs_ref, ...), custom_call_target="tpu_custom_call" | custom-call | flops 1073741824 | bytes 5767188 | tf_op jit(solution)/shard_map/pallas_call | solution.py:52
  114.9 3.4 %shard_map.87.mine_ref = f32[256,2048]{1,0:T(8,128)S(1)} custom-call(s32[5]{0:T(128)S(1)} %stack.23.at_ref, bf16[256,2048]{1,0:T(8,128)(2,1)S(1)} %bitcast.26, bf16[512,512]{1,0:T(8,128)(2,1)} %shard_map.84.a0, bf16[512,512]{1,0:T(8,128)(2,1)S(1)} %copy-done.15, bf16[512,512]{1,0:T(8,128)(2,1)} %collective-permute-done.4.a2, ...), custom_call_target="tpu_custom_call" | custom-call | flops 1073741824 | bytes 7340052 | tf_op jit(solution)/shard_map/pallas_call | solution.py:52
  118.3 3.2 %shard_map.89 = (bf16[256,2048]{1,0:T(8,128)(2,1)S(1)}, bf16[16,128,128]{2,1,0:T(8,128)(2,1)S(1)}) custom-call(f32[256,2048]{1,0:T(8,128)S(1)} %shard_map.87.mine_ref, f32[256,2048]{1,0:T(8,128)} %collective-permute-done.16.theirs_ref, bf16[256,2048]{1,0:T(8,128)(2,1)S(1)} %bitcast.23), custom_call_target="tpu_custom_call" | custom-call | flops 134217728 | bytes 6815744 | tf_op jit(solution)/shard_map/pallas_call | solution.py:52
  123.2 8.5 %all-to-all-start.2 = ((bf16[16,128,128]{2,1,0:T(8,128)(2,1)}), bf16[16,128,128]{2,1,0:T(8,128)(2,1)}, u32[]{:S(2)}, u32[]{:S(2)}) async-start(bf16[16,128,128]{2,1,0:T(8,128)(2,1)} %copy-done.23), calls=%async_computation.2 | async-start | bytes 1048576 | tf_op jit(solution)/shard_map/all_to_all | solution.py:281
  131.8 2.9 %collective-permute-start.19 = (bf16[2048,128]{1,0:T(8,128)(2,1)}, bf16[2048,128]{1,0:T(8,128)(2,1)S(1)}, u32[]{:S(2)}, u32[]{:S(2)}) collective-permute-start(bf16[2048,128]{1,0:T(8,128)(2,1)} %copy-done.27), channel_id=1, source_target_pairs={{0,128},{64,192},{128,0},{192,64},{1,129},{65,193},{129,1},{193,65... | collective-permute-start | bytes 1572872 | tf_op jit(solution)/shard_map/ppermute | solution.py:34
  139.2 2.4 shard_map.98
  141.8 2.6 %collective-permute-start.26 = (bf16[512,512]{1,0:T(8,128)(2,1)S(1)}, bf16[512,512]{1,0:T(8,128)(2,1)S(1)}, u32[]{:S(2)}, u32[]{:S(2)}) collective-permute-start(bf16[512,512]{1,0:T(8,128)(2,1)S(1)} %get-tuple-element.47), channel_id=1, source_target_pairs={{0,12},{4,0},{8,4},{12,8},{1,13},{5,1},{9,5},{13,9},{2,14},{6,2},{... | collective-permute-start | bytes 1572872 | tf_op jit(solution)/shard_map/ppermute | solution.py:34
  144.3 8.0 %collective-permute-done.19.refs_2_ = bf16[2048,128]{1,0:T(8,128)(2,1)S(1)} collective-permute-done((bf16[2048,128]{1,0:T(8,128)(2,1)}, bf16[2048,128]{1,0:T(8,128)(2,1)S(1)}, u32[]{:S(2)}, u32[]{:S(2)}) %collective-permute-start.19) | collective-permute-done | bytes 524320 | tf_op jit(solution)/shard_map/ppermute | solution.py:34
  152.4 9.7 %collective-permute-done.20.refs_3_ = bf16[2048,128]{1,0:T(8,128)(2,1)S(1)} collective-permute-done((bf16[2048,128]{1,0:T(8,128)(2,1)}, bf16[2048,128]{1,0:T(8,128)(2,1)S(1)}, u32[]{:S(2)}, u32[]{:S(2)}) %collective-permute-start.20) | collective-permute-done | bytes 524320 | tf_op jit(solution)/shard_map/ppermute | solution.py:34
  162.1 1.3 shard_map.97
  163.6 3.0 %collective-permute-done.24.refs_1_ = bf16[512,512]{1,0:T(8,128)(2,1)S(1)} collective-permute-done((bf16[512,512]{1,0:T(8,128)(2,1)S(1)}, bf16[512,512]{1,0:T(8,128)(2,1)S(1)}, u32[]{:S(2)}, u32[]{:S(2)}) %collective-permute-start.24) | collective-permute-done | bytes 524320 | tf_op jit(solution)/shard_map/ppermute | solution.py:34
  168.5 1.4 collective-permute-start.28
  169.9 3.1 %collective-permute-done.21.refs_1_ = bf16[512,128]{1,0:T(8,128)(2,1)S(1)} collective-permute-done((bf16[512,128]{1,0:T(8,128)(2,1)S(1)}, bf16[512,128]{1,0:T(8,128)(2,1)S(1)}, u32[]{:S(2)}, u32[]{:S(2)}) %collective-permute-start.21) | collective-permute-done | bytes 131104 | tf_op jit(solution)/shard_map/ppermute | solution.py:34
  175.1 1.8 collective-permute-done.29.refs_7_
  177.6 1.5 collective-permute-start.31
  179.1 3.5 %collective-permute-start.32 = (bf16[128,128]{1,0:T(8,128)(2,1)S(1)}, bf16[128,128]{1,0:T(8,128)(2,1)S(1)}, u32[]{:S(2)}, u32[]{:S(2)}) collective-permute-start(bf16[128,128]{1,0:T(8,128)(2,1)S(1)} %get-tuple-element.55), channel_id=1, source_target_pairs={{0,3},{1,0},{2,1},{3,2},{32,35},{33,32},{34,33},{35,34},{4,7},{5,4... | collective-permute-start | bytes 98312 | tf_op jit(solution)/shard_map/ppermute | solution.py:348
  182.6 1.6 collective-permute-start.33
  184.6 2.5 %collective-permute-start.35 = (bf16[128,128]{1,0:T(8,128)(2,1)S(1)}, bf16[128,128]{1,0:T(8,128)(2,1)S(1)}, u32[]{:S(2)}, u32[]{:S(2)}) collective-permute-start(bf16[128,128]{1,0:T(8,128)(2,1)S(1)} %get-tuple-element.58), channel_id=1, source_target_pairs={{0,34},{1,35},{2,32},{3,33},{32,2},{33,3},{34,0},{35,1},{4,38},{5,... | collective-permute-start | bytes 98312 | tf_op jit(solution)/shard_map/ppermute | solution.py:348
  187.1 3.5 %collective-permute-start.36 = (bf16[128,128]{1,0:T(8,128)(2,1)S(1)}, bf16[128,128]{1,0:T(8,128)(2,1)S(1)}, u32[]{:S(2)}, u32[]{:S(2)}) collective-permute-start(bf16[128,128]{1,0:T(8,128)(2,1)S(1)} %get-tuple-element.59), channel_id=1, source_target_pairs={{0,35},{1,32},{2,33},{3,34},{32,3},{33,0},{34,1},{35,2},{4,39},{5,... | collective-permute-start | bytes 98312 | tf_op jit(solution)/shard_map/ppermute | solution.py:348
  190.6 1.3 collective-permute-done.36.refs_7_
  192.8 10.9 %all-to-all-start.4 = ((bf16[16,128,128]{2,1,0:T(8,128)(2,1)}), bf16[16,128,128]{2,1,0:T(8,128)(2,1)}, u32[]{:S(2)}, u32[]{:S(2)}) async-start(bf16[16,128,128]{2,1,0:T(8,128)(2,1)} %copy-done.11), calls=%async_computation.4 | async-start | bytes 1048576 | tf_op jit(solution)/shard_map/all_to_all | solution.py:354
  205.6 7.8 %all-to-all-done.4.i_ref = bf16[16,128,128]{2,1,0:T(8,128)(2,1)} async-done(((bf16[16,128,128]{2,1,0:T(8,128)(2,1)}), bf16[16,128,128]{2,1,0:T(8,128)(2,1)}, u32[]{:S(2)}, u32[]{:S(2)}) %all-to-all-start.4) | async-done | bytes 524320 | tf_op jit(solution)/shard_map/all_to_all | solution.py:354
  213.5 5.2 %all-to-all-start.3 = ((bf16[16,128,128]{2,1,0:T(8,128)(2,1)}), bf16[16,128,128]{2,1,0:T(8,128)(2,1)}, u32[]{:S(2)}, u32[]{:S(2)}) async-start(bf16[16,128,128]{2,1,0:T(8,128)(2,1)} %copy-done.12), calls=%async_computation.3 | async-start | bytes 1048576 | tf_op jit(solution)/shard_map/all_to_all | solution.py:283
  219.9 4.3 %shard_map.92 = bf16[256,2048]{1,0:T(8,128)(2,1)} custom-call(bf16[256,2048]{1,0:T(8,128)(2,1)S(1)} %copy-done.17, bf16[256,2048]{1,0:T(8,128)(2,1)S(1)} %bitcast.16, bf16[256,2048]{1,0:T(8,128)(2,1)S(1)} %bitcast.20, bf16[16,128,128]{2,1,0:T(8,128)(2,1)S(1)} %all-to-all-done.1.p_ref), custom_call_target="tpu_custom_call" | custom-call | flops 671088640 | bytes 4718592 | tf_op jit(solution)/shard_map/pallas_call | solution.py:52
  224.2 2.1 shard_map.102
  226.4 2.2 all-to-all-done.3.l_ref
  228.6 1.2 copy-done.7
  231.0 7.8 %shard_map.94 = (bf16[256,2048]{1,0:T(8,128)(2,1)}, bf16[256,2048]{1,0:T(8,128)(2,1)}) custom-call(bf16[256,2048]{1,0:T(8,128)(2,1)S(1)} %copy-done.18, bf16[256,2048]{1,0:T(8,128)(2,1)S(1)} %bitcast.24, bf16[256,2048]{1,0:T(8,128)(2,1)S(1)} %bitcast.17, bf16[256,2048]{1,0:T(8,128)(2,1)S(1)} %bitcast.21, bf16[16,128,128]{2,1,0:T(8,128)(2,1)} %all-to-all-done.3.l_ref), custom_call_target="tpu_custom_call" | custom-call | flops 1342177280 | bytes 6815744 | tf_op jit(solution)/shard_map/pallas_call | solution.py:52
  (115 shorter events, 33.2 us)
Async XLA Ops:
  0.6 12.1 %copy-start = (bf16[128,2048]{1,0:T(8,128)(2,1)S(1)}, bf16[128,2048]{1,0:T(8,128)(2,1)}, u32[]{:S(2)}) copy-start(bf16[128,2048]{1,0:T(8,128)(2,1)} %param.8) | copy-start | bytes 1572868
  3.2 18.1 %copy-start.8 = (bf16[1,256,2048]{2,1,0:T(8,128)(2,1)S(1)}, bf16[1,256,2048]{2,1,0:T(8,128)(2,1)}, u32[]{:S(2)}) copy-start(bf16[1,256,2048]{2,1,0:T(8,128)(2,1)} %param.9) | copy-start | bytes 3145732
  5.4 57.9 %all-to-all-start = ((bf16[16,128,128]{2,1,0:T(8,128)(2,1)}), bf16[16,128,128]{2,1,0:T(8,128)(2,1)S(1)}, u32[]{:S(2)}, u32[]{:S(2)}) async-start(bf16[16,128,128]{2,1,0:T(8,128)(2,1)} %shard_map.90), calls=%async_computation | async-start | bytes 1048576 | tf_op jit(solution)/shard_map/all_to_all | solution.py:281
  12.8 9.6 %collective-permute-start = (bf16[128,512]{1,0:T(8,128)(2,1)S(1)}, bf16[128,512]{1,0:T(8,128)(2,1)S(1)}, u32[]{:S(2)}, u32[]{:S(2)}) collective-permute-start(bf16[128,512]{1,0:T(8,128)(2,1)S(1)} %constant_dynamic-slice_fusion.1.refs_0_), channel_id=1, source_target_pairs={{1,0},{2,1},{3,2},{0,3},{5,4},{6,5},{7,6},{4,7},{9,8},{10,9},{11,1... | collective-permute-start | bytes 393224 | tf_op jit(solution)/shard_map/ppermute | solution.py:29
  18.0 11.1 %collective-permute-start.1 = (bf16[128,512]{1,0:T(8,128)(2,1)S(1)}, bf16[128,512]{1,0:T(8,128)(2,1)S(1)}, u32[]{:S(2)}, u32[]{:S(2)}) collective-permute-start(bf16[128,512]{1,0:T(8,128)(2,1)S(1)} %constant_dynamic-slice_fusion.1.refs_0_), channel_id=1, source_target_pairs={{2,0},{3,1},{0,2},{1,3},{6,4},{7,5},{4,6},{5,7},{10,8},{11,9},{8,1... | collective-permute-start | bytes 393224 | tf_op jit(solution)/shard_map/ppermute | solution.py:29
  19.1 16.9 %collective-permute-start.2 = (bf16[128,512]{1,0:T(8,128)(2,1)S(1)}, bf16[128,512]{1,0:T(8,128)(2,1)S(1)}, u32[]{:S(2)}, u32[]{:S(2)}) collective-permute-start(bf16[128,512]{1,0:T(8,128)(2,1)S(1)} %constant_dynamic-slice_fusion.1.refs_0_), channel_id=1, source_target_pairs={{3,0},{0,1},{1,2},{2,3},{7,4},{4,5},{5,6},{6,7},{11,8},{8,9},{9,10... | collective-permute-start | bytes 393224 | tf_op jit(solution)/shard_map/ppermute | solution.py:29
  21.3 40.9 %collective-permute-start.15 = (bf16[256,1024]{1,0:T(8,128)(2,1)S(1)}, bf16[256,1024]{1,0:T(8,128)(2,1)}, u32[]{:S(2)}, u32[]{:S(2)}) collective-permute-start(bf16[256,1024]{1,0:T(8,128)(2,1)S(1)} %dynamic-slice_bitcast_fusion), channel_id=1, source_target_pairs={{0,16},{16,0},{1,17},{17,1},{2,18},{18,2},{3,19},{19,3},{4,20},{20... | collective-permute-start | bytes 1572872 | tf_op jit(solution)/shard_map/ppermute | solution.py:25
  37.4 25.3 %collective-permute-start.3 = (bf16[512,512]{1,0:T(8,128)(2,1)}, bf16[512,512]{1,0:T(8,128)(2,1)S(1)}, u32[]{:S(2)}, u32[]{:S(2)}) collective-permute-start(bf16[512,512]{1,0:T(8,128)(2,1)} %shard_map.84.a0), channel_id=1, source_target_pairs={{4,0},{8,4},{12,8},{0,12},{5,1},{9,5},{13,9},{1,13},{6,2},{10,6},{... | collective-permute-start | bytes 1572872 | tf_op jit(solution)/shard_map/ppermute | solution.py:29
  39.9 3.7 %collective-permute-start.6 = (bf16[128,128]{1,0:T(8,128)(2,1)S(1)}, bf16[128,128]{1,0:T(8,128)(2,1)S(1)}, u32[]{:S(2)}, u32[]{:S(2)}) collective-permute-start(bf16[128,128]{1,0:T(8,128)(2,1)S(1)} %constant_dynamic-slice_fusion.refs_0_), channel_id=1, source_target_pairs={{1,0},{2,1},{3,2},{0,3},{5,4},{6,5},{7,6},{4,7},{9,8},{10,9},{11,1... | collective-permute-start | bytes 98312 | tf_op jit(solution)/shard_map/ppermute | solution.py:29
  41.1 7.0 %collective-permute-start.7 = (bf16[128,128]{1,0:T(8,128)(2,1)S(1)}, bf16[128,128]{1,0:T(8,128)(2,1)S(1)}, u32[]{:S(2)}, u32[]{:S(2)}) collective-permute-start(bf16[128,128]{1,0:T(8,128)(2,1)S(1)} %constant_dynamic-slice_fusion.refs_0_), channel_id=1, source_target_pairs={{2,0},{3,1},{0,2},{1,3},{6,4},{7,5},{4,6},{5,7},{10,8},{11,9},{8,1... | collective-permute-start | bytes 98312 | tf_op jit(solution)/shard_map/ppermute | solution.py:29
  42.4 5.8 %collective-permute-start.8 = (bf16[128,128]{1,0:T(8,128)(2,1)S(1)}, bf16[128,128]{1,0:T(8,128)(2,1)S(1)}, u32[]{:S(2)}, u32[]{:S(2)}) collective-permute-start(bf16[128,128]{1,0:T(8,128)(2,1)S(1)} %constant_dynamic-slice_fusion.refs_0_), channel_id=1, source_target_pairs={{3,0},{0,1},{1,2},{2,3},{7,4},{4,5},{5,6},{6,7},{11,8},{8,9},{9,10... | collective-permute-start | bytes 98312 | tf_op jit(solution)/shard_map/ppermute | solution.py:29
  48.7 6.3 %collective-permute-start.9 = (bf16[512,128]{1,0:T(8,128)(2,1)S(1)}, bf16[512,128]{1,0:T(8,128)(2,1)S(1)}, u32[]{:S(2)}, u32[]{:S(2)}) collective-permute-start(bf16[512,128]{1,0:T(8,128)(2,1)S(1)} %shard_map.85.refs_0_), channel_id=1, source_target_pairs={{4,0},{8,4},{12,8},{0,12},{5,1},{9,5},{13,9},{1,13},{6,2},{10,6},{... | collective-permute-start | bytes 393224 | tf_op jit(solution)/shard_map/ppermute | solution.py:29
  49.4 6.7 %collective-permute-start.10 = (bf16[512,128]{1,0:T(8,128)(2,1)S(1)}, bf16[512,128]{1,0:T(8,128)(2,1)S(1)}, u32[]{:S(2)}, u32[]{:S(2)}) collective-permute-start(bf16[512,128]{1,0:T(8,128)(2,1)S(1)} %shard_map.85.refs_0_), channel_id=1, source_target_pairs={{8,0},{12,4},{0,8},{4,12},{9,1},{13,5},{1,9},{5,13},{10,2},{14,6},... | collective-permute-start | bytes 393224 | tf_op jit(solution)/shard_map/ppermute | solution.py:29
  49.6 9.4 %collective-permute-start.11 = (bf16[512,128]{1,0:T(8,128)(2,1)S(1)}, bf16[512,128]{1,0:T(8,128)(2,1)S(1)}, u32[]{:S(2)}, u32[]{:S(2)}) collective-permute-start(bf16[512,128]{1,0:T(8,128)(2,1)S(1)} %shard_map.85.refs_0_), channel_id=1, source_target_pairs={{12,0},{0,4},{4,8},{8,12},{13,1},{1,5},{5,9},{9,13},{14,2},{2,6},{... | collective-permute-start | bytes 393224 | tf_op jit(solution)/shard_map/ppermute | solution.py:29
  55.0 29.7 %collective-permute-start.4 = (bf16[512,512]{1,0:T(8,128)(2,1)}, bf16[512,512]{1,0:T(8,128)(2,1)}, u32[]{:S(2)}, u32[]{:S(2)}) collective-permute-start(bf16[512,512]{1,0:T(8,128)(2,1)} %shard_map.84.a0), channel_id=1, source_target_pairs={{8,0},{12,4},{0,8},{4,12},{9,1},{13,5},{1,9},{5,13},{10,2},{14,6},... | collective-permute-start | bytes 1572872 | tf_op jit(solution)/shard_map/ppermute | solution.py:29
  56.1 28.6 %collective-permute-start.5 = (bf16[512,512]{1,0:T(8,128)(2,1)}, bf16[512,512]{1,0:T(8,128)(2,1)}, u32[]{:S(2)}, u32[]{:S(2)}) collective-permute-start(bf16[512,512]{1,0:T(8,128)(2,1)} %shard_map.84.a0), channel_id=1, source_target_pairs={{12,0},{0,4},{4,8},{8,12},{13,1},{1,5},{5,9},{9,13},{14,2},{2,6},{... | collective-permute-start | bytes 1572872 | tf_op jit(solution)/shard_map/ppermute | solution.py:29
  60.4 24.3 %collective-permute-start.12 = (bf16[2048,128]{1,0:T(8,128)(2,1)}, bf16[2048,128]{1,0:T(8,128)(2,1)}, u32[]{:S(2)}, u32[]{:S(2)}) collective-permute-start(bf16[2048,128]{1,0:T(8,128)(2,1)} %shard_map.86.b0), channel_id=1, source_target_pairs={{64,0},{128,64},{192,128},{0,192},{65,1},{129,65},{193,129},{1,193... | collective-permute-start | bytes 1572872 | tf_op jit(solution)/shard_map/ppermute | solution.py:29
  62.2 22.6 %collective-permute-start.13 = (bf16[2048,128]{1,0:T(8,128)(2,1)}, bf16[2048,128]{1,0:T(8,128)(2,1)}, u32[]{:S(2)}, u32[]{:S(2)}) collective-permute-start(bf16[2048,128]{1,0:T(8,128)(2,1)} %shard_map.86.b0), channel_id=1, source_target_pairs={{128,0},{192,64},{0,128},{64,192},{129,1},{193,65},{1,129},{65,193... | collective-permute-start | bytes 1572872 | tf_op jit(solution)/shard_map/ppermute | solution.py:29
  62.7 22.0 %collective-permute-start.14 = (bf16[2048,128]{1,0:T(8,128)(2,1)}, bf16[2048,128]{1,0:T(8,128)(2,1)}, u32[]{:S(2)}, u32[]{:S(2)}) collective-permute-start(bf16[2048,128]{1,0:T(8,128)(2,1)} %shard_map.86.b0), channel_id=1, source_target_pairs={{192,0},{0,64},{64,128},{128,192},{193,1},{1,65},{65,129},{129,193... | collective-permute-start | bytes 1572872 | tf_op jit(solution)/shard_map/ppermute | solution.py:29
  64.2 36.9 %all-to-all-start.1 = ((bf16[16,128,128]{2,1,0:T(8,128)(2,1)}), bf16[16,128,128]{2,1,0:T(8,128)(2,1)S(1)}, u32[]{:S(2)}, u32[]{:S(2)}) async-start(bf16[16,128,128]{2,1,0:T(8,128)(2,1)} %shard_map.91), calls=%async_computation.1 | async-start | bytes 1048576 | tf_op jit(solution)/shard_map/all_to_all | solution.py:283
  84.7 16.4 %copy-start.2 = (bf16[1,256,2048]{2,1,0:T(8,128)(2,1)S(1)}, bf16[1,256,2048]{2,1,0:T(8,128)(2,1)}, u32[]{:S(2)}) copy-start(bf16[1,256,2048]{2,1,0:T(8,128)(2,1)} %param.6) | copy-start | bytes 3145732
  84.7 16.4 %copy-start.4 = (bf16[1,256,2048]{2,1,0:T(8,128)(2,1)S(1)}, bf16[1,256,2048]{2,1,0:T(8,128)(2,1)}, u32[]{:S(2)}) copy-start(bf16[1,256,2048]{2,1,0:T(8,128)(2,1)} %param.7) | copy-start | bytes 3145732
  90.7 27.5 %collective-permute-start.16 = (f32[256,2048]{1,0:T(8,128)}, f32[256,2048]{1,0:T(8,128)}, u32[]{:S(2)}, u32[]{:S(2)}) collective-permute-start(f32[256,2048]{1,0:T(8,128)} %shard_map.88), channel_id=1, source_target_pairs={{0,16},{16,0},{1,17},{17,1},{2,18},{18,2},{3,19},{19,3},{4,20},{20... | collective-permute-start | bytes 6291464 | tf_op jit(solution)/shard_map/ppermute | solution.py:25
  105.5 9.4 %copy-start.15 = (bf16[512,512]{1,0:T(8,128)(2,1)S(1)}, bf16[512,512]{1,0:T(8,128)(2,1)}, u32[]{:S(2)}) copy-start(bf16[512,512]{1,0:T(8,128)(2,1)} %copy-done.13) | copy-start | bytes 1572868
  105.5 2.7 %collective-permute-start.17 = (bf16[2048,256]{1,0:T(8,128)(2,1)S(1)}, bf16[2048,256]{1,0:T(8,128)(2,1)S(1)}, u32[]{:S(2)}, u32[]{:S(2)}) collective-permute-start(bf16[2048,256]{1,0:T(8,128)(2,1)S(1)} %shard_map.95.mine_ref), channel_id=1, source_target_pairs={{0,16},{16,0},{1,17},{17,1},{2,18},{18,2},{3,19},{19,3},{4,20},{20... | collective-permute-start | bytes 3145736 | tf_op jit(solution)/shard_map/ppermute | solution.py:25
  114.8 26.9 %collective-permute-start.18 = (bf16[2048,128]{1,0:T(8,128)(2,1)}, bf16[2048,128]{1,0:T(8,128)(2,1)}, u32[]{:S(2)}, u32[]{:S(2)}) collective-permute-start(bf16[2048,128]{1,0:T(8,128)(2,1)} %get-tuple-element.37), channel_id=1, source_target_pairs={{0,64},{64,128},{128,192},{192,0},{1,65},{65,129},{129,193},{193,1... | collective-permute-start | bytes 1572872 | tf_op jit(solution)/shard_map/ppermute | solution.py:34
  123.2 69.5 %all-to-all-start.2 = ((bf16[16,128,128]{2,1,0:T(8,128)(2,1)}), bf16[16,128,128]{2,1,0:T(8,128)(2,1)}, u32[]{:S(2)}, u32[]{:S(2)}) async-start(bf16[16,128,128]{2,1,0:T(8,128)(2,1)} %copy-done.23), calls=%async_computation.2 | async-start | bytes 1048576 | tf_op jit(solution)/shard_map/all_to_all | solution.py:281
  131.8 20.6 %collective-permute-start.19 = (bf16[2048,128]{1,0:T(8,128)(2,1)}, bf16[2048,128]{1,0:T(8,128)(2,1)S(1)}, u32[]{:S(2)}, u32[]{:S(2)}) collective-permute-start(bf16[2048,128]{1,0:T(8,128)(2,1)} %copy-done.27), channel_id=1, source_target_pairs={{0,128},{64,192},{128,0},{192,64},{1,129},{65,193},{129,1},{193,65... | collective-permute-start | bytes 1572872 | tf_op jit(solution)/shard_map/ppermute | solution.py:34
  134.6 27.5 %collective-permute-start.20 = (bf16[2048,128]{1,0:T(8,128)(2,1)}, bf16[2048,128]{1,0:T(8,128)(2,1)S(1)}, u32[]{:S(2)}, u32[]{:S(2)}) collective-permute-start(bf16[2048,128]{1,0:T(8,128)(2,1)} %copy-done.26), channel_id=1, source_target_pairs={{0,192},{64,0},{128,64},{192,128},{1,193},{65,1},{129,65},{193,129... | collective-permute-start | bytes 1572872 | tf_op jit(solution)/shard_map/ppermute | solution.py:34
  139.2 22.9 %copy-start.22 = (bf16[2048,128]{1,0:T(8,128)(2,1)S(1)}, bf16[2048,128]{1,0:T(8,128)(2,1)}, u32[]{:S(2)}) copy-start(bf16[2048,128]{1,0:T(8,128)(2,1)} %copy-done.21) | copy-start | bytes 1572868
  141.6 25.1 %collective-permute-start.24 = (bf16[512,512]{1,0:T(8,128)(2,1)S(1)}, bf16[512,512]{1,0:T(8,128)(2,1)S(1)}, u32[]{:S(2)}, u32[]{:S(2)}) collective-permute-start(bf16[512,512]{1,0:T(8,128)(2,1)S(1)} %get-tuple-element.45), channel_id=1, source_target_pairs={{0,4},{4,8},{8,12},{12,0},{1,5},{5,9},{9,13},{13,1},{2,6},{6,10},{... | collective-permute-start | bytes 1572872 | tf_op jit(solution)/shard_map/ppermute | solution.py:34
  141.7 25.0 %collective-permute-start.25 = (bf16[512,512]{1,0:T(8,128)(2,1)S(1)}, bf16[512,512]{1,0:T(8,128)(2,1)S(1)}, u32[]{:S(2)}, u32[]{:S(2)}) collective-permute-start(bf16[512,512]{1,0:T(8,128)(2,1)S(1)} %get-tuple-element.46), channel_id=1, source_target_pairs={{0,8},{4,12},{8,0},{12,4},{1,9},{5,13},{9,1},{13,5},{2,10},{6,14},... | collective-permute-start | bytes 1572872 | tf_op jit(solution)/shard_map/ppermute | solution.py:34
  141.8 25.2 %collective-permute-start.26 = (bf16[512,512]{1,0:T(8,128)(2,1)S(1)}, bf16[512,512]{1,0:T(8,128)(2,1)S(1)}, u32[]{:S(2)}, u32[]{:S(2)}) collective-permute-start(bf16[512,512]{1,0:T(8,128)(2,1)S(1)} %get-tuple-element.47), channel_id=1, source_target_pairs={{0,12},{4,0},{8,4},{12,8},{1,13},{5,1},{9,5},{13,9},{2,14},{6,2},{... | collective-permute-start | bytes 1572872 | tf_op jit(solution)/shard_map/ppermute | solution.py:34
  163.4 9.6 %collective-permute-start.21 = (bf16[512,128]{1,0:T(8,128)(2,1)S(1)}, bf16[512,128]{1,0:T(8,128)(2,1)S(1)}, u32[]{:S(2)}, u32[]{:S(2)}) collective-permute-start(bf16[512,128]{1,0:T(8,128)(2,1)S(1)} %get-tuple-element.41), channel_id=1, source_target_pairs={{0,4},{4,8},{8,12},{12,0},{1,5},{5,9},{9,13},{13,1},{2,6},{6,10},{... | collective-permute-start | bytes 393224 | tf_op jit(solution)/shard_map/ppermute | solution.py:34
  163.5 10.6 %collective-permute-start.22 = (bf16[512,128]{1,0:T(8,128)(2,1)S(1)}, bf16[512,128]{1,0:T(8,128)(2,1)S(1)}, u32[]{:S(2)}, u32[]{:S(2)}) collective-permute-start(bf16[512,128]{1,0:T(8,128)(2,1)S(1)} %get-tuple-element.42), channel_id=1, source_target_pairs={{0,8},{4,12},{8,0},{12,4},{1,9},{5,13},{9,1},{13,5},{2,10},{6,14},... | collective-permute-start | bytes 393224 | tf_op jit(solution)/shard_map/ppermute | solution.py:34
  166.6 7.5 %collective-permute-start.23 = (bf16[512,128]{1,0:T(8,128)(2,1)S(1)}, bf16[512,128]{1,0:T(8,128)(2,1)S(1)}, u32[]{:S(2)}, u32[]{:S(2)}) collective-permute-start(bf16[512,128]{1,0:T(8,128)(2,1)S(1)} %get-tuple-element.43), channel_id=1, source_target_pairs={{0,12},{4,0},{8,4},{12,8},{1,13},{5,1},{9,5},{13,9},{2,14},{6,2},{... | collective-permute-start | bytes 393224 | tf_op jit(solution)/shard_map/ppermute | solution.py:34
  167.8 6.3 %collective-permute-start.27 = (bf16[512,128]{1,0:T(8,128)(2,1)S(1)}, bf16[512,128]{1,0:T(8,128)(2,1)S(1)}, u32[]{:S(2)}, u32[]{:S(2)}) collective-permute-start(bf16[512,128]{1,0:T(8,128)(2,1)S(1)} %get-tuple-element.49), channel_id=1, source_target_pairs={{0,64},{64,128},{128,192},{192,0},{1,65},{65,129},{129,193},{193,1... | collective-permute-start | bytes 393224 | tf_op jit(solution)/shard_map/ppermute | solution.py:34
  168.5 6.6 %collective-permute-start.28 = (bf16[512,128]{1,0:T(8,128)(2,1)S(1)}, bf16[512,128]{1,0:T(8,128)(2,1)S(1)}, u32[]{:S(2)}, u32[]{:S(2)}) collective-permute-start(bf16[512,128]{1,0:T(8,128)(2,1)S(1)} %get-tuple-element.50), channel_id=1, source_target_pairs={{0,128},{64,192},{128,0},{192,64},{1,129},{65,193},{129,1},{193,65... | collective-permute-start | bytes 393224 | tf_op jit(solution)/shard_map/ppermute | solution.py:34
  173.0 3.8 %collective-permute-start.29 = (bf16[512,128]{1,0:T(8,128)(2,1)S(1)}, bf16[512,128]{1,0:T(8,128)(2,1)S(1)}, u32[]{:S(2)}, u32[]{:S(2)}) collective-permute-start(bf16[512,128]{1,0:T(8,128)(2,1)S(1)} %get-tuple-element.51), channel_id=1, source_target_pairs={{0,192},{64,0},{128,64},{192,128},{1,193},{65,1},{129,65},{193,129... | collective-permute-start | bytes 393224 | tf_op jit(solution)/shard_map/ppermute | solution.py:34
  177.5 7.1 %collective-permute-start.30 = (bf16[128,128]{1,0:T(8,128)(2,1)S(1)}, bf16[128,128]{1,0:T(8,128)(2,1)S(1)}, u32[]{:S(2)}, u32[]{:S(2)}) collective-permute-start(bf16[128,128]{1,0:T(8,128)(2,1)S(1)} %get-tuple-element.53), channel_id=1, source_target_pairs={{0,1},{1,2},{2,3},{3,0},{32,33},{33,34},{34,35},{35,32},{4,5},{5,6... | collective-permute-start | bytes 98312 | tf_op jit(solution)/shard_map/ppermute | solution.py:348
  177.6 9.5 %collective-permute-start.31 = (bf16[128,128]{1,0:T(8,128)(2,1)S(1)}, bf16[128,128]{1,0:T(8,128)(2,1)S(1)}, u32[]{:S(2)}, u32[]{:S(2)}) collective-permute-start(bf16[128,128]{1,0:T(8,128)(2,1)S(1)} %get-tuple-element.54), channel_id=1, source_target_pairs={{0,2},{1,3},{2,0},{3,1},{32,34},{33,35},{34,32},{35,33},{4,6},{5,7... | collective-permute-start | bytes 98312 | tf_op jit(solution)/shard_map/ppermute | solution.py:348
  179.1 11.5 %collective-permute-start.32 = (bf16[128,128]{1,0:T(8,128)(2,1)S(1)}, bf16[128,128]{1,0:T(8,128)(2,1)S(1)}, u32[]{:S(2)}, u32[]{:S(2)}) collective-permute-start(bf16[128,128]{1,0:T(8,128)(2,1)S(1)} %get-tuple-element.55), channel_id=1, source_target_pairs={{0,3},{1,0},{2,1},{3,2},{32,35},{33,32},{34,33},{35,34},{4,7},{5,4... | collective-permute-start | bytes 98312 | tf_op jit(solution)/shard_map/ppermute | solution.py:348
  182.6 8.0 %collective-permute-start.33 = (bf16[128,128]{1,0:T(8,128)(2,1)S(1)}, bf16[128,128]{1,0:T(8,128)(2,1)S(1)}, u32[]{:S(2)}, u32[]{:S(2)}) collective-permute-start(bf16[128,128]{1,0:T(8,128)(2,1)S(1)} %get-tuple-element.56), channel_id=1, source_target_pairs={{0,32},{1,33},{2,34},{3,35},{32,0},{33,1},{34,2},{35,3},{4,36},{5,... | collective-permute-start | bytes 98312 | tf_op jit(solution)/shard_map/ppermute | solution.py:348
  184.2 6.4 %collective-permute-start.34 = (bf16[128,128]{1,0:T(8,128)(2,1)S(1)}, bf16[128,128]{1,0:T(8,128)(2,1)S(1)}, u32[]{:S(2)}, u32[]{:S(2)}) collective-permute-start(bf16[128,128]{1,0:T(8,128)(2,1)S(1)} %get-tuple-element.57), channel_id=1, source_target_pairs={{0,33},{1,34},{2,35},{3,32},{32,1},{33,2},{34,3},{35,0},{4,37},{5,... | collective-permute-start | bytes 98312 | tf_op jit(solution)/shard_map/ppermute | solution.py:348
  184.6 6.0 %collective-permute-start.35 = (bf16[128,128]{1,0:T(8,128)(2,1)S(1)}, bf16[128,128]{1,0:T(8,128)(2,1)S(1)}, u32[]{:S(2)}, u32[]{:S(2)}) collective-permute-start(bf16[128,128]{1,0:T(8,128)(2,1)S(1)} %get-tuple-element.58), channel_id=1, source_target_pairs={{0,34},{1,35},{2,32},{3,33},{32,2},{33,3},{34,0},{35,1},{4,38},{5,... | collective-permute-start | bytes 98312 | tf_op jit(solution)/shard_map/ppermute | solution.py:348
  187.1 4.8 %collective-permute-start.36 = (bf16[128,128]{1,0:T(8,128)(2,1)S(1)}, bf16[128,128]{1,0:T(8,128)(2,1)S(1)}, u32[]{:S(2)}, u32[]{:S(2)}) collective-permute-start(bf16[128,128]{1,0:T(8,128)(2,1)S(1)} %get-tuple-element.59), channel_id=1, source_target_pairs={{0,35},{1,32},{2,33},{3,34},{32,3},{33,0},{34,1},{35,2},{4,39},{5,... | collective-permute-start | bytes 98312 | tf_op jit(solution)/shard_map/ppermute | solution.py:348
  192.8 20.7 %all-to-all-start.4 = ((bf16[16,128,128]{2,1,0:T(8,128)(2,1)}), bf16[16,128,128]{2,1,0:T(8,128)(2,1)}, u32[]{:S(2)}, u32[]{:S(2)}) async-start(bf16[16,128,128]{2,1,0:T(8,128)(2,1)} %copy-done.11), calls=%async_computation.4 | async-start | bytes 1048576 | tf_op jit(solution)/shard_map/all_to_all | solution.py:354
  213.5 15.1 %all-to-all-start.3 = ((bf16[16,128,128]{2,1,0:T(8,128)(2,1)}), bf16[16,128,128]{2,1,0:T(8,128)(2,1)}, u32[]{:S(2)}, u32[]{:S(2)}) async-start(bf16[16,128,128]{2,1,0:T(8,128)(2,1)} %copy-done.12), calls=%async_computation.3 | async-start | bytes 1048576 | tf_op jit(solution)/shard_map/all_to_all | solution.py:283
  (22 other events, 44.7 us)

commit v2 on v0

--- a/solution.py
+++ b/solution.py
@@ -11,6 +11,8 @@
 HEAD = 128
 F32 = jnp.float32
 BF16 = jnp.bfloat16
+
+ALL_ROOM = 60 * 2**20
 
 
 def dot(a, b, da, db):
@@ -48,14 +50,14 @@
         in_specs = [small if a.dtype == jnp.int32 else full for a in args]
         out_specs = jax.tree.map(lambda o: full, out)
     if room is None:
-        room = 2 * size + 8 * 2**20
+        room = size + 6 * 2**20
     return pl.pallas_call(
         body,
         out_shape=out,
         in_specs=list(in_specs),
         out_specs=out_specs,
         cost_estimate=pl.CostEstimate(flops=flops, bytes_accessed=size, transcendentals=0),
-        compiler_params=pltpu.CompilerParams(vmem_limit_bytes=min(room, 56 * 2**20)),
+        compiler_params=pltpu.CompilerParams(vmem_limit_bytes=room),
         **kwargs,
     )(*args)
 
@@ -224,9 +226,17 @@
 
 
 def place_body(at_ref, *refs):
+    size, half = refs[0].shape[0], refs[4].shape[1]
+    for k in range(4):
+        s = block(at_ref[3], k, size)
+        refs[4][s, :] = refs[k][:, :half]
+        refs[5][s, :] = refs[k][:, half:]
+
+
+def stack_body(at_ref, *refs):
     size = refs[0].shape[0]
     for k in range(4):
-        refs[4][block(at_ref[3], k, size), :] = refs[k][...]
+        refs[4][block(at_ref[2], k, size), :] = refs[k][...]
 
 
 def projected_body(other, at_ref, og_ref, a0, a1, a2, a3, b0, b1, b2, b3, o_ref):
@@ -265,7 +275,7 @@
 
     key_states = call(
         states_body, shape((HEADS, HEAD, HEAD)), k, v,
-        grid=heads, in_specs=[rows, rows], out_specs=STATE_SPEC, flops=token_flops,
+        grid=heads, in_specs=[rows, rows], out_specs=STATE_SPEC, flops=token_flops, room=ALL_ROOM,
     )
 
     def exchange(states, reverse):
@@ -273,15 +283,16 @@
         sums = call(functools.partial(scan_body, reverse), shape(by_head.shape), by_head, flops=by_head.size)
         return lax.all_to_all(sums, CTX, 0, 0)
 
-    wa = lax.dynamic_slice(out_weight, (0, core * width), (out_weight.shape[0], width // 2))
-    wb = lax.dynamic_slice(
-        out_weight, (0, core * width + width // 2 + y * (width // 8)), (out_weight.shape[0], width // 8)
-    )
-    za = copies(wa, "zh")
-    wb = lax.all_to_all(jnp.broadcast_to(wb[None], (16, *wb.shape)), FSDP, 0, 0).reshape(inner, -1)
+    half, part = width // 2, width // 8
+    wa = lax.dynamic_slice(out_weight, (0, core * width), (out_weight.shape[0], half))
+    wb = lax.dynamic_slice(out_weight, (0, core * width + half + y * part), (out_weight.shape[0], part))
+    wz = copies(jnp.concatenate([wa, wb], axis=1), "zh")
+    z_rows = 4 * out_weight.shape[0]
+    wa, wb = call(place_body, [shape((z_rows, half)), shape((z_rows, part))], at, *wz)
+    xb = copies(wb, "x")
+    xa = copies(wa, "x")
+    wb = call(stack_body, shape((inner, part)), at, *xb)
     yb = copies(wb, "y")
-    wa = call(place_body, shape((4 * out_weight.shape[0], wa.shape[1])), at, *za)
-    xa = copies(wa, "x")
     prior = exchange(key_states, False)
 
     attended = call(
@@ -291,6 +302,15 @@
     )
     partner = from_core(attended)
 
+    gw_flops = 2 * inner * 2 * tokens * (width // 2)
+    gy = call(
+        weight_y_body, [shape((inner, width // 8))] * 4, at, attended, partner, og, oog,
+        flops=gw_flops,
+    )
+    gx = call(
+        weight_x_body, [shape((inner // 4, width // 2))] * 4, at, attended, partner, og, oog,
+        flops=gw_flops,
+    )
     project_flops = 2 * tokens * inner * width
     for_partner = call(
         functools.partial(projected_body, True), shape((tokens, inner), F32), at, oog, *xa, *yb,
@@ -298,15 +318,6 @@
     )
     from_partner = from_core(for_partner)
 
-    gw_flops = 2 * inner * 2 * tokens * (width // 2)
-    gy = call(
-        weight_y_body, [shape((inner, width // 8))] * 4, at, attended, partner, og, oog,
-        flops=gw_flops,
-    )
-    gx = call(
-        weight_x_body, [shape((inner // 4, width // 2))] * 4, at, attended, partner, og, oog,
-        flops=gw_flops,
-    )
     mine = call(
         functools.partial(projected_body, False), shape((tokens, inner), F32), at, og, *xa, *yb,
         flops=project_flops,
@@ -325,12 +336,12 @@
     gxy = spread(gxy, "y")
     grad_queries = call(
         functools.partial(grad_queries_body, factor), shape((tokens, inner)), ga, k, v, prior,
-        grid=heads, in_specs=[rows, rows, rows, STATE_SPEC], out_specs=rows, flops=5 * token_flops,
+        grid=heads, in_specs=[rows, rows, rows, STATE_SPEC], out_specs=rows, flops=5 * token_flops, room=ALL_ROOM,
     )
     gz = call(add_then_z_body, shape((8, inner // 16, width // 8)), *gyx, *gxy)
     grad_keys, grad_values = call(
         functools.partial(grad_keys_values_body, factor), [shape((tokens, inner))] * 2, ga, q, k, v, later,
-        grid=heads, in_specs=[rows, rows, rows, rows, STATE_SPEC], out_specs=[rows, rows], flops=10 * token_flops,
+        grid=heads, in_specs=[rows, rows, rows, rows, STATE_SPEC], out_specs=[rows, rows], flops=10 * token_flops, room=ALL_ROOM,
     )
     gz = lax.all_to_all(gz, ("zl", "zh"), 0, 0)
     total = call(add_then_all_body, shape((16, inner // 16, width // 8)), gz)

time: 275 us -> 218 us (0.79)
  starting transfers between devices: 109 us -> 80.3 us
  blocking collectives: 16.8 us -> 0 us
  local copies, waits for them, and re-layouts: 18.6 us -> 10.5 us
  waiting for transfers between devices: 85.6 us -> 77.6 us
  Pallas kernels: 42.6 us -> 47.5 us
    ppermute x3, starting transfers between devices: 21.1 us -> 0.98 us  [from_core(): return lax.ppermute(v, 'c', [(0, 1), (1, 0)])]
    all_to_all x1 -> x0, blocking collectives: 16.8 us -> none  [exchange(): by_head = lax.all_to_all(states, CTX, 0, 0)]
    ppermute x9 -> x12, waiting for transfers between devices: 18.9 us -> 33.6 us  [copies(): lax.ppermute(v, axis, [((i + k) % 4, i) for i in range(4)])]
    ppermute x12, waiting for transfers between devices: 37.9 us -> 25.7 us  [spread(): lax.ppermute(pieces[k], axis, [(i, (i + k) % 4) for i in range(4)])]
    all_to_all x1 -> x0, starting transfers between devices: 9.9 us -> none  [local(): lax.all_to_all(jnp.broadcast_to(wb[None], (16, *wb.shape)), FSDP, 0, 0)]
    all_to_all x1, starting transfers between devices: 18.1 us -> 8.96 us  [local(): gz = lax.all_to_all(gz, ('zl', 'zh'), 0, 0)]
    all_to_all x1 -> x2, waiting for transfers between devices: 8.91 us -> 0.01 us  [exchange(): by_head = lax.all_to_all(states, CTX, 0, 0)]
    ppermute x9 -> x12, starting transfers between devices: 16.2 us -> 24.5 us  [copies(): lax.ppermute(v, axis, [((i + k) % 4, i) for i in range(4)])]
  transfers between devices with their start and end apart: 30 -> 33, of which waited for: 15 -> 12; matrix products, arithmetic and copies ran while one was open for 1% -> 0% of each run, Pallas kernels for 12% -> 21%
where the time goes in v2:
time: 218 us; the launch traced here: 217 us
  starting transfers between devices  80.3 us (37%)
  waiting for transfers between devices  77.6 us (36%)
  Pallas kernels  47.5 us (22%)
  local copies, waits for them, and re-layouts  10.5 us (5%)
    pallas_call x18, Pallas kernels, call(): pl.pallas_call(body, out_shape=out, in_specs=list(in_specs), out_specs=ou...  47.5 us
    ppermute x12, waiting for transfers between devices, copies(): lax.ppermute(v, axis, [((i + k) % 4, i) for i in range(4)])  33.6 us
    ppermute x12, waiting for transfers between devices, spread(): lax.ppermute(pieces[k], axis, [(i, (i + k) % 4) for i in range(4)])  25.7 us
    ppermute x12, starting transfers between devices, copies(): lax.ppermute(v, axis, [((i + k) % 4, i) for i in range(4)])  24.5 us
    all_to_all x2, starting transfers between devices, exchange(): return lax.all_to_all(sums, CTX, 0, 0)  17 us
    ppermute x12, starting transfers between devices, spread(): lax.ppermute(pieces[k], axis, [(i, (i + k) % 4) for i in range(4)])  13.3 us
    all_to_all x2, starting transfers between devices, exchange(): by_head = lax.all_to_all(states, CTX, 0, 0)  11 us
    unnamed x48, local copies, waits for them, and re-layouts  9.64 us
  transfers between devices with their start and end apart: 33, of which 12 were waited for; matrix products, arithmetic and copies ran while one was open for 0% of the time, Pallas kernels for 21%

profile of v2, /device:TPU:1, one launch (start us, length us, event | category | flops | bytes accessed | tf_op | source)
XLA Modules:
  0.0 216.9 jit_solution(4806649157981686609)
XLA Ops:
  0.7 1.0 copy-done
  1.8 6.9 %collective-permute-start = (bf16[128,640]{1,0:T(8,128)(2,1)S(1)}, bf16[128,640]{1,0:T(8,128)(2,1)S(1)}, u32[]{:S(2)}, u32[]{:S(2)}) collective-permute-start(bf16[128,640]{1,0:T(8,128)(2,1)S(1)} %pad_maximum_fusion.refs_0_), channel_id=1, source_target_pairs={{1,0},{2,1},{3,2},{0,3},{5,4},{6,5},{7,6},{4,7},{9,8},{10,9},{11,1... | collective-permute-start | bytes 491528 | tf_op jit(solution)/shard_map/ppermute | solution.py:31
  8.7 1.0 collective-permute-start.1
  9.7 2.3 %collective-permute-start.2 = (bf16[128,640]{1,0:T(8,128)(2,1)S(1)}, bf16[128,640]{1,0:T(8,128)(2,1)S(1)}, u32[]{:S(2)}, u32[]{:S(2)}) collective-permute-start(bf16[128,640]{1,0:T(8,128)(2,1)S(1)} %pad_maximum_fusion.refs_0_), channel_id=1, source_target_pairs={{3,0},{0,1},{1,2},{2,3},{7,4},{4,5},{5,6},{6,7},{11,8},{8,9},{9,10... | collective-permute-start | bytes 491528 | tf_op jit(solution)/shard_map/ppermute | solution.py:31
  11.9 4.0 %shard_map.89 = bf16[16,128,128]{2,1,0:T(8,128)(2,1)} custom-call(bf16[256,2048]{1,0:T(8,128)(2,1)} %bitcast.13, bf16[256,2048]{1,0:T(8,128)(2,1)} %bitcast.17), custom_call_target="tpu_custom_call" | custom-call | flops 134217728 | bytes 2621440 | tf_op jit(solution)/shard_map/pallas_call | solution.py:54
  15.9 6.5 %all-to-all-start = ((bf16[16,128,128]{2,1,0:T(8,128)(2,1)}), bf16[16,128,128]{2,1,0:T(8,128)(2,1)S(1)}, u32[]{:S(2)}, u32[]{:S(2)}) async-start(bf16[16,128,128]{2,1,0:T(8,128)(2,1)} %shard_map.89), calls=%async_computation | async-start | bytes 1048576 | tf_op jit(solution)/shard_map/all_to_all | solution.py:282
  23.4 1.4 shard_map.84
  24.8 2.5 %collective-permute-start.3 = (bf16[512,512]{1,0:T(8,128)(2,1)}, bf16[512,512]{1,0:T(8,128)(2,1)S(1)}, u32[]{:S(2)}, u32[]{:S(2)}) collective-permute-start(bf16[512,512]{1,0:T(8,128)(2,1)} %get-tuple-element.26.a0), channel_id=1, source_target_pairs={{4,0},{8,4},{12,8},{0,12},{5,1},{9,5},{13,9},{1,13},{6,2},{10,6},{... | collective-permute-start | bytes 1572872 | tf_op jit(solution)/shard_map/ppermute | solution.py:31
  28.7 13.2 %collective-permute-done.6.refs_1_ = bf16[512,128]{1,0:T(8,128)(2,1)S(1)} collective-permute-done((bf16[512,128]{1,0:T(8,128)(2,1)S(1)}, bf16[512,128]{1,0:T(8,128)(2,1)S(1)}, u32[]{:S(2)}, u32[]{:S(2)}) %collective-permute-start.6) | collective-permute-done | bytes 131104 | tf_op jit(solution)/shard_map/ppermute | solution.py:31
  41.9 1.7 collective-permute-start.4
  43.6 4.3 %collective-permute-start.5 = (bf16[512,512]{1,0:T(8,128)(2,1)}, bf16[512,512]{1,0:T(8,128)(2,1)}, u32[]{:S(2)}, u32[]{:S(2)}) collective-permute-start(bf16[512,512]{1,0:T(8,128)(2,1)} %get-tuple-element.26.a0), channel_id=1, source_target_pairs={{12,0},{0,4},{4,8},{8,12},{13,1},{1,5},{5,9},{9,13},{14,2},{2,6},{... | collective-permute-start | bytes 1572872 | tf_op jit(solution)/shard_map/ppermute | solution.py:31
  48.0 1.4 shard_map.85.b0
  49.3 3.1 %collective-permute-start.9 = (bf16[2048,128]{1,0:T(8,128)(2,1)}, bf16[2048,128]{1,0:T(8,128)(2,1)}, u32[]{:S(2)}, u32[]{:S(2)}) collective-permute-start(bf16[2048,128]{1,0:T(8,128)(2,1)} %shard_map.85.b0), channel_id=1, source_target_pairs={{64,0},{128,64},{192,128},{0,192},{65,1},{129,65},{193,129},{1,193... | collective-permute-start | bytes 1572872 | tf_op jit(solution)/shard_map/ppermute | solution.py:31
  54.5 7.9 %all-to-all-start.1 = ((bf16[16,128,128]{2,1,0:T(8,128)(2,1)}), bf16[16,128,128]{2,1,0:T(8,128)(2,1)S(1)}, u32[]{:S(2)}, u32[]{:S(2)}) async-start(bf16[16,128,128]{2,1,0:T(8,128)(2,1)} %shard_map.90), calls=%async_computation.1 | async-start | bytes 1048576 | tf_op jit(solution)/shard_map/all_to_all | solution.py:284
  62.4 6.4 %collective-permute-done.5.a3 = bf16[512,512]{1,0:T(8,128)(2,1)} collective-permute-done((bf16[512,512]{1,0:T(8,128)(2,1)}, bf16[512,512]{1,0:T(8,128)(2,1)}, u32[]{:S(2)}, u32[]{:S(2)}) %collective-permute-start.5) | collective-permute-done | bytes 524320 | tf_op jit(solution)/shard_map/ppermute | solution.py:31
  68.8 14.0 %collective-permute-done.11.b3 = bf16[2048,128]{1,0:T(8,128)(2,1)} collective-permute-done((bf16[2048,128]{1,0:T(8,128)(2,1)}, bf16[2048,128]{1,0:T(8,128)(2,1)}, u32[]{:S(2)}, u32[]{:S(2)}) %collective-permute-start.11) | collective-permute-done | bytes 524320 | tf_op jit(solution)/shard_map/ppermute | solution.py:31
  82.8 1.0 copy-done.10
  83.9 1.0 copy-done.16
  84.9 4.6 %shard_map.87 = f32[256,2048]{1,0:T(8,128)} custom-call(s32[4]{0:T(128)S(1)} %pad_add_fusion.at_ref, bf16[256,1024]{1,0:T(8,128)(2,1)S(1)} %copy-done.16, bf16[512,512]{1,0:T(8,128)(2,1)} %get-tuple-element.26.a0, bf16[512,512]{1,0:T(8,128)(2,1)S(1)} %copy-done.10, bf16[512,512]{1,0:T(8,128)(2,1)} %collective-permute-done.4.a2, ...), custom_call_target="tpu_custom_call" | custom-call | flops 1073741824 | bytes 6815760 | tf_op jit(solution)/shard_map/pallas_call | solution.py:54
  90.2 1.4 copy-done.4
  91.6 3.1 %shard_map.94.mine_ref = bf16[2048,256]{1,0:T(8,128)(2,1)S(1)} custom-call(bf16[256,2048]{1,0:T(8,128)(2,1)S(1)} %bitcast.22, bf16[256,2048]{1,0:T(8,128)(2,1)S(1)} %bitcast.16, bf16[256,2048]{1,0:T(8,128)(2,1)S(1)} %bitcast.20, bf16[16,128,128]{2,1,0:T(8,128)(2,1)S(1)} %all-to-all-done.1.p_ref), custom_call_target="tpu_custom_call" | custom-call | flops 671088640 | bytes 4718592 | tf_op jit(solution)/shard_map/pallas_call | solution.py:54
  95.0 2.6 %collective-permute-done.14.theirs_ref = bf16[2048,256]{1,0:T(8,128)(2,1)S(1)} collective-permute-done((bf16[2048,256]{1,0:T(8,128)(2,1)S(1)}, bf16[2048,256]{1,0:T(8,128)(2,1)S(1)}, u32[]{:S(2)}, u32[]{:S(2)}) %collective-permute-start.14) | collective-permute-done | bytes 1048608 | tf_op jit(solution)/shard_map/ppermute | solution.py:27
  97.7 3.3 %shard_map.95 = (bf16[2048,128]{1,0:T(8,128)(2,1)S(1)}, bf16[2048,128]{1,0:T(8,128)(2,1)}, bf16[2048,128]{1,0:T(8,128)(2,1)S(1)}, bf16[2048,128]{1,0:T(8,128)(2,1)S(1)}) custom-call(s32[4]{0:T(128)S(1)} %pad_add_fusion.at_ref, bf16[2048,256]{1,0:T(8,128)(2,1)S(1)} %shard_map.94.mine_ref, bf16[2048,256]{1,0:T(8,128)(2,1)S(1)} %collective-permute-done.14.theirs_ref, ...), custom_call_target="tpu_custom_call" | custom-call | flops 1073741824 | bytes 5767184 | tf_op jit(solution)/shard_map/pallas_call | solution.py:54
  102.6 3.4 %shard_map.86.mine_ref = f32[256,2048]{1,0:T(8,128)S(1)} custom-call(s32[4]{0:T(128)S(1)} %pad_add_fusion.at_ref, bf16[256,2048]{1,0:T(8,128)(2,1)S(1)} %bitcast.25, bf16[512,512]{1,0:T(8,128)(2,1)} %get-tuple-element.26.a0, bf16[512,512]{1,0:T(8,128)(2,1)S(1)} %copy-done.11, bf16[512,512]{1,0:T(8,128)(2,1)} %collective-permute-done.4.a2, ...), custom_call_target="tpu_custom_call" | custom-call | flops 1073741824 | bytes 7340048 | tf_op jit(solution)/shard_map/pallas_call | solution.py:54
  106.0 4.2 %shard_map.88 = (bf16[256,2048]{1,0:T(8,128)(2,1)S(1)}, bf16[16,128,128]{2,1,0:T(8,128)(2,1)}) custom-call(f32[256,2048]{1,0:T(8,128)S(1)} %shard_map.86.mine_ref, f32[256,2048]{1,0:T(8,128)} %collective-permute-done.13.theirs_ref, bf16[256,2048]{1,0:T(8,128)(2,1)S(1)} %bitcast.23), custom_call_target="tpu_custom_call" | custom-call | flops 134217728 | bytes 6815744 | tf_op jit(solution)/shard_map/pallas_call | solution.py:54
  111.2 4.6 %all-to-all-start.2 = ((bf16[16,128,128]{2,1,0:T(8,128)(2,1)}), bf16[16,128,128]{2,1,0:T(8,128)(2,1)S(1)}, u32[]{:S(2)}, u32[]{:S(2)}) async-start(bf16[16,128,128]{2,1,0:T(8,128)(2,1)} %get-tuple-element.29), calls=%async_computation.2 | async-start | bytes 1048576 | tf_op jit(solution)/shard_map/all_to_all | solution.py:282
  115.8 2.9 %collective-permute-start.16 = (bf16[2048,128]{1,0:T(8,128)(2,1)}, bf16[2048,128]{1,0:T(8,128)(2,1)S(1)}, u32[]{:S(2)}, u32[]{:S(2)}) collective-permute-start(bf16[2048,128]{1,0:T(8,128)(2,1)} %copy-done.22), channel_id=1, source_target_pairs={{0,128},{64,192},{128,0},{192,64},{1,129},{65,193},{129,1},{193,65... | collective-permute-start | bytes 1572872 | tf_op jit(solution)/shard_map/ppermute | solution.py:36
  119.5 1.2 copy-done.14
  120.7 1.2 copy-done.20
  122.0 1.8 shard_map.97
  124.6 1.9 collective-permute-start.23
  126.5 9.8 %collective-permute-done.16.refs_2_ = bf16[2048,128]{1,0:T(8,128)(2,1)S(1)} collective-permute-done((bf16[2048,128]{1,0:T(8,128)(2,1)}, bf16[2048,128]{1,0:T(8,128)(2,1)S(1)}, u32[]{:S(2)}, u32[]{:S(2)}) %collective-permute-start.16) | collective-permute-done | bytes 524320 | tf_op jit(solution)/shard_map/ppermute | solution.py:36
  136.3 9.7 %collective-permute-done.17.refs_3_ = bf16[2048,128]{1,0:T(8,128)(2,1)S(1)} collective-permute-done((bf16[2048,128]{1,0:T(8,128)(2,1)}, bf16[2048,128]{1,0:T(8,128)(2,1)S(1)}, u32[]{:S(2)}, u32[]{:S(2)}) %collective-permute-start.17) | collective-permute-done | bytes 524320 | tf_op jit(solution)/shard_map/ppermute | solution.py:36
  146.1 1.3 shard_map.96
  148.8 1.3 collective-permute-start.20
  151.0 1.3 collective-permute-start.24
  152.3 1.6 collective-permute-start.25
  153.9 2.2 %collective-permute-done.18.refs_1_ = bf16[512,128]{1,0:T(8,128)(2,1)S(1)} collective-permute-done((bf16[512,128]{1,0:T(8,128)(2,1)S(1)}, bf16[512,128]{1,0:T(8,128)(2,1)S(1)}, u32[]{:S(2)}, u32[]{:S(2)}) %collective-permute-start.18) | collective-permute-done | bytes 131104 | tf_op jit(solution)/shard_map/ppermute | solution.py:36
  156.1 1.8 collective-permute-start.26
  158.5 2.6 %collective-permute-done.26.refs_7_ = bf16[512,128]{1,0:T(8,128)(2,1)S(1)} collective-permute-done((bf16[512,128]{1,0:T(8,128)(2,1)S(1)}, bf16[512,128]{1,0:T(8,128)(2,1)S(1)}, u32[]{:S(2)}, u32[]{:S(2)}) %collective-permute-start.26) | collective-permute-done | bytes 131104 | tf_op jit(solution)/shard_map/ppermute | solution.py:36
  162.0 9.0 %all-to-all-start.4 = ((bf16[8,128,128]{2,1,0:T(8,128)(2,1)}), bf16[8,128,128]{2,1,0:T(8,128)(2,1)S(1)}, u32[]{:S(2)}, u32[]{:S(2)}) async-start(bf16[8,128,128]{2,1,0:T(8,128)(2,1)} %shard_map.99), calls=%async_computation.4 | async-start | bytes 524288 | tf_op jit(solution)/shard_map/all_to_all | solution.py:346
  171.8 6.9 %all-to-all-done.4.i_ref = bf16[8,128,128]{2,1,0:T(8,128)(2,1)S(1)} async-done(((bf16[8,128,128]{2,1,0:T(8,128)(2,1)}), bf16[8,128,128]{2,1,0:T(8,128)(2,1)S(1)}, u32[]{:S(2)}, u32[]{:S(2)}) %all-to-all-start.4) | async-done | bytes 262176 | tf_op jit(solution)/shard_map/all_to_all | solution.py:346
  178.7 9.1 %all-to-all-start.3 = ((bf16[16,128,128]{2,1,0:T(8,128)(2,1)}), bf16[16,128,128]{2,1,0:T(8,128)(2,1)S(1)}, u32[]{:S(2)}, u32[]{:S(2)}) async-start(bf16[16,128,128]{2,1,0:T(8,128)(2,1)} %shard_map.92), calls=%async_computation.3 | async-start | bytes 1048576 | tf_op jit(solution)/shard_map/all_to_all | solution.py:284
  188.7 8.8 %all-to-all-done.3.l_ref = bf16[16,128,128]{2,1,0:T(8,128)(2,1)S(1)} async-done(((bf16[16,128,128]{2,1,0:T(8,128)(2,1)}), bf16[16,128,128]{2,1,0:T(8,128)(2,1)S(1)}, u32[]{:S(2)}, u32[]{:S(2)}) %all-to-all-start.3) | async-done | bytes 524320 | tf_op jit(solution)/shard_map/all_to_all | solution.py:284
  197.5 4.6 %all-to-all-start.5 = ((bf16[16,128,128]{2,1,0:T(8,128)(2,1)}), bf16[16,128,128]{2,1,0:T(8,128)(2,1)S(1)}, u32[]{:S(2)}, u32[]{:S(2)}) async-start(bf16[16,128,128]{2,1,0:T(8,128)(2,1)} %shard_map.100), calls=%async_computation.5 | async-start | bytes 1048576 | tf_op jit(solution)/shard_map/all_to_all | solution.py:348
  202.1 5.7 %shard_map.91 = bf16[256,2048]{1,0:T(8,128)(2,1)} custom-call(bf16[256,2048]{1,0:T(8,128)(2,1)} %copy-done.12, bf16[256,2048]{1,0:T(8,128)(2,1)} %bitcast.14, bf16[256,2048]{1,0:T(8,128)(2,1)} %bitcast.18, bf16[16,128,128]{2,1,0:T(8,128)(2,1)} %copy-done.3), custom_call_target="tpu_custom_call" | custom-call | flops 671088640 | bytes 4718592 | tf_op jit(solution)/shard_map/pallas_call | solution.py:54
  207.8 8.0 %shard_map.93 = (bf16[256,2048]{1,0:T(8,128)(2,1)}, bf16[256,2048]{1,0:T(8,128)(2,1)}) custom-call(bf16[256,2048]{1,0:T(8,128)(2,1)} %copy-done.12, bf16[256,2048]{1,0:T(8,128)(2,1)} %bitcast.21, bf16[256,2048]{1,0:T(8,128)(2,1)} %bitcast.15, bf16[256,2048]{1,0:T(8,128)(2,1)} %bitcast.19, bf16[16,128,128]{2,1,0:T(8,128)(2,1)} %copy-done.23), custom_call_target="tpu_custom_call" | custom-call | flops 1342177280 | bytes 6815744 | tf_op jit(solution)/shard_map/pallas_call | solution.py:54
  215.8 1.1 shard_map.101
  (89 shorter events, 15.4 us)
Async XLA Ops:
  1.7 20.6 %copy-start.6 = (bf16[1,256,2048]{2,1,0:T(8,128)(2,1)S(1)}, bf16[1,256,2048]{2,1,0:T(8,128)(2,1)}, u32[]{:S(2)}) copy-start(bf16[1,256,2048]{2,1,0:T(8,128)(2,1)} %param.9) | copy-start | bytes 3145732
  1.8 21.6 %collective-permute-start = (bf16[128,640]{1,0:T(8,128)(2,1)S(1)}, bf16[128,640]{1,0:T(8,128)(2,1)S(1)}, u32[]{:S(2)}, u32[]{:S(2)}) collective-permute-start(bf16[128,640]{1,0:T(8,128)(2,1)S(1)} %pad_maximum_fusion.refs_0_), channel_id=1, source_target_pairs={{1,0},{2,1},{3,2},{0,3},{5,4},{6,5},{7,6},{4,7},{9,8},{10,9},{11,1... | collective-permute-start | bytes 491528 | tf_op jit(solution)/shard_map/ppermute | solution.py:31
  8.7 14.7 %collective-permute-start.1 = (bf16[128,640]{1,0:T(8,128)(2,1)S(1)}, bf16[128,640]{1,0:T(8,128)(2,1)S(1)}, u32[]{:S(2)}, u32[]{:S(2)}) collective-permute-start(bf16[128,640]{1,0:T(8,128)(2,1)S(1)} %pad_maximum_fusion.refs_0_), channel_id=1, source_target_pairs={{2,0},{3,1},{0,2},{1,3},{6,4},{7,5},{4,6},{5,7},{10,8},{11,9},{8,1... | collective-permute-start | bytes 491528 | tf_op jit(solution)/shard_map/ppermute | solution.py:31
  9.7 13.7 %collective-permute-start.2 = (bf16[128,640]{1,0:T(8,128)(2,1)S(1)}, bf16[128,640]{1,0:T(8,128)(2,1)S(1)}, u32[]{:S(2)}, u32[]{:S(2)}) collective-permute-start(bf16[128,640]{1,0:T(8,128)(2,1)S(1)} %pad_maximum_fusion.refs_0_), channel_id=1, source_target_pairs={{3,0},{0,1},{1,2},{2,3},{7,4},{4,5},{5,6},{6,7},{11,8},{8,9},{9,10... | collective-permute-start | bytes 491528 | tf_op jit(solution)/shard_map/ppermute | solution.py:31
  15.9 37.7 %all-to-all-start = ((bf16[16,128,128]{2,1,0:T(8,128)(2,1)}), bf16[16,128,128]{2,1,0:T(8,128)(2,1)S(1)}, u32[]{:S(2)}, u32[]{:S(2)}) async-start(bf16[16,128,128]{2,1,0:T(8,128)(2,1)} %shard_map.89), calls=%async_computation | async-start | bytes 1048576 | tf_op jit(solution)/shard_map/all_to_all | solution.py:282
  23.2 29.2 %collective-permute-start.12 = (bf16[256,1024]{1,0:T(8,128)(2,1)}, bf16[256,1024]{1,0:T(8,128)(2,1)S(1)}, u32[]{:S(2)}, u32[]{:S(2)}) collective-permute-start(bf16[256,1024]{1,0:T(8,128)(2,1)} %dynamic-slice_bitcast_fusion), channel_id=1, source_target_pairs={{0,16},{16,0},{1,17},{17,1},{2,18},{18,2},{3,19},{19,3},{4,20},{20... | collective-permute-start | bytes 1572872 | tf_op jit(solution)/shard_map/ppermute | solution.py:27
  24.8 28.3 %collective-permute-start.3 = (bf16[512,512]{1,0:T(8,128)(2,1)}, bf16[512,512]{1,0:T(8,128)(2,1)S(1)}, u32[]{:S(2)}, u32[]{:S(2)}) collective-permute-start(bf16[512,512]{1,0:T(8,128)(2,1)} %get-tuple-element.26.a0), channel_id=1, source_target_pairs={{4,0},{8,4},{12,8},{0,12},{5,1},{9,5},{13,9},{1,13},{6,2},{10,6},{... | collective-permute-start | bytes 1572872 | tf_op jit(solution)/shard_map/ppermute | solution.py:31
  27.3 14.6 %collective-permute-start.6 = (bf16[512,128]{1,0:T(8,128)(2,1)S(1)}, bf16[512,128]{1,0:T(8,128)(2,1)S(1)}, u32[]{:S(2)}, u32[]{:S(2)}) collective-permute-start(bf16[512,128]{1,0:T(8,128)(2,1)S(1)} %get-tuple-element.27.refs_0_), channel_id=1, source_target_pairs={{4,0},{8,4},{12,8},{0,12},{5,1},{9,5},{13,9},{1,13},{6,2},{10,6},{... | collective-permute-start | bytes 393224 | tf_op jit(solution)/shard_map/ppermute | solution.py:31
  27.8 15.8 %collective-permute-start.7 = (bf16[512,128]{1,0:T(8,128)(2,1)S(1)}, bf16[512,128]{1,0:T(8,128)(2,1)S(1)}, u32[]{:S(2)}, u32[]{:S(2)}) collective-permute-start(bf16[512,128]{1,0:T(8,128)(2,1)S(1)} %get-tuple-element.27.refs_0_), channel_id=1, source_target_pairs={{8,0},{12,4},{0,8},{4,12},{9,1},{13,5},{1,9},{5,13},{10,2},{14,6},... | collective-permute-start | bytes 393224 | tf_op jit(solution)/shard_map/ppermute | solution.py:31
  28.0 19.9 %collective-permute-start.8 = (bf16[512,128]{1,0:T(8,128)(2,1)S(1)}, bf16[512,128]{1,0:T(8,128)(2,1)S(1)}, u32[]{:S(2)}, u32[]{:S(2)}) collective-permute-start(bf16[512,128]{1,0:T(8,128)(2,1)S(1)} %get-tuple-element.27.refs_0_), channel_id=1, source_target_pairs={{12,0},{0,4},{4,8},{8,12},{13,1},{1,5},{5,9},{9,13},{14,2},{2,6},{... | collective-permute-start | bytes 393224 | tf_op jit(solution)/shard_map/ppermute | solution.py:31
  41.9 20.5 %collective-permute-start.4 = (bf16[512,512]{1,0:T(8,128)(2,1)}, bf16[512,512]{1,0:T(8,128)(2,1)}, u32[]{:S(2)}, u32[]{:S(2)}) collective-permute-start(bf16[512,512]{1,0:T(8,128)(2,1)} %get-tuple-element.26.a0), channel_id=1, source_target_pairs={{8,0},{12,4},{0,8},{4,12},{9,1},{13,5},{1,9},{5,13},{10,2},{14,6},... | collective-permute-start | bytes 1572872 | tf_op jit(solution)/shard_map/ppermute | solution.py:31
  43.6 25.2 %collective-permute-start.5 = (bf16[512,512]{1,0:T(8,128)(2,1)}, bf16[512,512]{1,0:T(8,128)(2,1)}, u32[]{:S(2)}, u32[]{:S(2)}) collective-permute-start(bf16[512,512]{1,0:T(8,128)(2,1)} %get-tuple-element.26.a0), channel_id=1, source_target_pairs={{12,0},{0,4},{4,8},{8,12},{13,1},{1,5},{5,9},{9,13},{14,2},{2,6},{... | collective-permute-start | bytes 1572872 | tf_op jit(solution)/shard_map/ppermute | solution.py:31
  49.3 19.5 %collective-permute-start.9 = (bf16[2048,128]{1,0:T(8,128)(2,1)}, bf16[2048,128]{1,0:T(8,128)(2,1)}, u32[]{:S(2)}, u32[]{:S(2)}) collective-permute-start(bf16[2048,128]{1,0:T(8,128)(2,1)} %shard_map.85.b0), channel_id=1, source_target_pairs={{64,0},{128,64},{192,128},{0,192},{65,1},{129,65},{193,129},{1,193... | collective-permute-start | bytes 1572872 | tf_op jit(solution)/shard_map/ppermute | solution.py:31
  52.4 2.1 copy-start.15
  52.4 16.4 %collective-permute-start.10 = (bf16[2048,128]{1,0:T(8,128)(2,1)}, bf16[2048,128]{1,0:T(8,128)(2,1)}, u32[]{:S(2)}, u32[]{:S(2)}) collective-permute-start(bf16[2048,128]{1,0:T(8,128)(2,1)} %shard_map.85.b0), channel_id=1, source_target_pairs={{128,0},{192,64},{0,128},{64,192},{129,1},{193,65},{1,129},{65,193... | collective-permute-start | bytes 1572872 | tf_op jit(solution)/shard_map/ppermute | solution.py:31
  53.0 1.5 copy-start.9
  53.0 29.8 %collective-permute-start.11 = (bf16[2048,128]{1,0:T(8,128)(2,1)}, bf16[2048,128]{1,0:T(8,128)(2,1)}, u32[]{:S(2)}, u32[]{:S(2)}) collective-permute-start(bf16[2048,128]{1,0:T(8,128)(2,1)} %shard_map.85.b0), channel_id=1, source_target_pairs={{192,0},{0,64},{64,128},{128,192},{193,1},{1,65},{65,129},{129,193... | collective-permute-start | bytes 1572872 | tf_op jit(solution)/shard_map/ppermute | solution.py:31
  54.5 35.6 %all-to-all-start.1 = ((bf16[16,128,128]{2,1,0:T(8,128)(2,1)}), bf16[16,128,128]{2,1,0:T(8,128)(2,1)S(1)}, u32[]{:S(2)}, u32[]{:S(2)}) async-start(bf16[16,128,128]{2,1,0:T(8,128)(2,1)} %shard_map.90), calls=%async_computation.1 | async-start | bytes 1048576 | tf_op jit(solution)/shard_map/all_to_all | solution.py:284
  62.4 27.8 %copy-start.1 = (bf16[1,256,2048]{2,1,0:T(8,128)(2,1)S(1)}, bf16[1,256,2048]{2,1,0:T(8,128)(2,1)}, u32[]{:S(2)}) copy-start(bf16[1,256,2048]{2,1,0:T(8,128)(2,1)} %param.6) | copy-start | bytes 3145732
  62.4 27.7 %copy-start.2 = (bf16[1,256,2048]{2,1,0:T(8,128)(2,1)S(1)}, bf16[1,256,2048]{2,1,0:T(8,128)(2,1)}, u32[]{:S(2)}) copy-start(bf16[1,256,2048]{2,1,0:T(8,128)(2,1)} %param.7) | copy-start | bytes 3145732
  89.5 16.4 %collective-permute-start.13 = (f32[256,2048]{1,0:T(8,128)}, f32[256,2048]{1,0:T(8,128)}, u32[]{:S(2)}, u32[]{:S(2)}) collective-permute-start(f32[256,2048]{1,0:T(8,128)} %shard_map.87), channel_id=1, source_target_pairs={{0,16},{16,0},{1,17},{17,1},{2,18},{18,2},{3,19},{19,3},{4,20},{20... | collective-permute-start | bytes 6291464 | tf_op jit(solution)/shard_map/ppermute | solution.py:27
  90.1 4.6 %copy-start.3 = (bf16[16,128,128]{2,1,0:T(8,128)(2,1)}, bf16[16,128,128]{2,1,0:T(8,128)(2,1)S(1)}, u32[]{:S(2)}) copy-start(bf16[16,128,128]{2,1,0:T(8,128)(2,1)S(1)} %all-to-all-done.1.p_ref) | copy-start | bytes 1572868
  91.6 6.1 %copy-start.7 = (bf16[1,256,2048]{2,1,0:T(8,128)(2,1)S(1)}, bf16[1,256,2048]{2,1,0:T(8,128)(2,1)}, u32[]{:S(2)}) copy-start(bf16[1,256,2048]{2,1,0:T(8,128)(2,1)} %param.9) | copy-start | bytes 3145732
  91.6 6.1 %copy-start.17 = (bf16[256,1024]{1,0:T(8,128)(2,1)S(1)}, bf16[256,1024]{1,0:T(8,128)(2,1)}, u32[]{:S(2)}) copy-start(bf16[256,1024]{1,0:T(8,128)(2,1)} %copy-done.15) | copy-start | bytes 1572868
  94.7 7.8 %copy-start.13 = (bf16[2048,256]{1,0:T(8,128)(2,1)}, bf16[2048,256]{1,0:T(8,128)(2,1)S(1)}, u32[]{:S(2)}) copy-start(bf16[2048,256]{1,0:T(8,128)(2,1)S(1)} %shard_map.94.mine_ref) | copy-start | bytes 3145732
  94.7 7.8 %copy-start.11 = (bf16[512,512]{1,0:T(8,128)(2,1)S(1)}, bf16[512,512]{1,0:T(8,128)(2,1)}, u32[]{:S(2)}) copy-start(bf16[512,512]{1,0:T(8,128)(2,1)} %copy-done.9) | copy-start | bytes 1572868
  94.7 2.9 %collective-permute-start.14 = (bf16[2048,256]{1,0:T(8,128)(2,1)S(1)}, bf16[2048,256]{1,0:T(8,128)(2,1)S(1)}, u32[]{:S(2)}, u32[]{:S(2)}) collective-permute-start(bf16[2048,256]{1,0:T(8,128)(2,1)S(1)} %shard_map.94.mine_ref), channel_id=1, source_target_pairs={{0,16},{16,0},{1,17},{17,1},{2,18},{18,2},{3,19},{19,3},{4,20},{20... | collective-permute-start | bytes 3145736 | tf_op jit(solution)/shard_map/ppermute | solution.py:27
  97.7 4.9 %copy-start.19 = (bf16[2048,256]{1,0:T(8,128)(2,1)}, bf16[2048,256]{1,0:T(8,128)(2,1)S(1)}, u32[]{:S(2)}) copy-start(bf16[2048,256]{1,0:T(8,128)(2,1)S(1)} %collective-permute-done.14.theirs_ref) | copy-start | bytes 3145732
  102.6 3.4 %copy-start.5 = (bf16[1,256,2048]{2,1,0:T(8,128)(2,1)S(1)}, bf16[1,256,2048]{2,1,0:T(8,128)(2,1)}, u32[]{:S(2)}) copy-start(bf16[1,256,2048]{2,1,0:T(8,128)(2,1)} %param.5) | copy-start | bytes 3145732
  102.6 22.0 %collective-permute-start.15 = (bf16[2048,128]{1,0:T(8,128)(2,1)}, bf16[2048,128]{1,0:T(8,128)(2,1)}, u32[]{:S(2)}, u32[]{:S(2)}) collective-permute-start(bf16[2048,128]{1,0:T(8,128)(2,1)} %get-tuple-element.33), channel_id=1, source_target_pairs={{0,64},{64,128},{128,192},{192,0},{1,65},{65,129},{129,193},{193,1... | collective-permute-start | bytes 1572872 | tf_op jit(solution)/shard_map/ppermute | solution.py:36
  106.0 13.6 %copy-start.8 = (bf16[1,256,2048]{2,1,0:T(8,128)(2,1)S(1)}, bf16[1,256,2048]{2,1,0:T(8,128)(2,1)}, u32[]{:S(2)}) copy-start(bf16[1,256,2048]{2,1,0:T(8,128)(2,1)} %param.9) | copy-start | bytes 3145732
  106.0 13.5 %copy-start.18 = (bf16[256,1024]{1,0:T(8,128)(2,1)S(1)}, bf16[256,1024]{1,0:T(8,128)(2,1)}, u32[]{:S(2)}) copy-start(bf16[256,1024]{1,0:T(8,128)(2,1)} %copy-done.15) | copy-start | bytes 1572868
  111.2 50.8 %all-to-all-start.2 = ((bf16[16,128,128]{2,1,0:T(8,128)(2,1)}), bf16[16,128,128]{2,1,0:T(8,128)(2,1)S(1)}, u32[]{:S(2)}, u32[]{:S(2)}) async-start(bf16[16,128,128]{2,1,0:T(8,128)(2,1)} %get-tuple-element.29), calls=%async_computation.2 | async-start | bytes 1048576 | tf_op jit(solution)/shard_map/all_to_all | solution.py:282
  115.8 20.6 %collective-permute-start.16 = (bf16[2048,128]{1,0:T(8,128)(2,1)}, bf16[2048,128]{1,0:T(8,128)(2,1)S(1)}, u32[]{:S(2)}, u32[]{:S(2)}) collective-permute-start(bf16[2048,128]{1,0:T(8,128)(2,1)} %copy-done.22), channel_id=1, source_target_pairs={{0,128},{64,192},{128,0},{192,64},{1,129},{65,193},{129,1},{193,65... | collective-permute-start | bytes 1572872 | tf_op jit(solution)/shard_map/ppermute | solution.py:36
  118.6 27.5 %collective-permute-start.17 = (bf16[2048,128]{1,0:T(8,128)(2,1)}, bf16[2048,128]{1,0:T(8,128)(2,1)S(1)}, u32[]{:S(2)}, u32[]{:S(2)}) collective-permute-start(bf16[2048,128]{1,0:T(8,128)(2,1)} %copy-done.21), channel_id=1, source_target_pairs={{0,192},{64,0},{128,64},{192,128},{1,193},{65,1},{129,65},{193,129... | collective-permute-start | bytes 1572872 | tf_op jit(solution)/shard_map/ppermute | solution.py:36
  123.8 25.1 %collective-permute-start.21 = (bf16[512,512]{1,0:T(8,128)(2,1)S(1)}, bf16[512,512]{1,0:T(8,128)(2,1)S(1)}, u32[]{:S(2)}, u32[]{:S(2)}) collective-permute-start(bf16[512,512]{1,0:T(8,128)(2,1)S(1)} %get-tuple-element.41), channel_id=1, source_target_pairs={{0,4},{4,8},{8,12},{12,0},{1,5},{5,9},{9,13},{13,1},{2,6},{6,10},{... | collective-permute-start | bytes 1572872 | tf_op jit(solution)/shard_map/ppermute | solution.py:36
  123.9 26.3 %collective-permute-start.22 = (bf16[512,512]{1,0:T(8,128)(2,1)S(1)}, bf16[512,512]{1,0:T(8,128)(2,1)S(1)}, u32[]{:S(2)}, u32[]{:S(2)}) collective-permute-start(bf16[512,512]{1,0:T(8,128)(2,1)S(1)} %get-tuple-element.42), channel_id=1, source_target_pairs={{0,8},{4,12},{8,0},{12,4},{1,9},{5,13},{9,1},{13,5},{2,10},{6,14},... | collective-permute-start | bytes 1572872 | tf_op jit(solution)/shard_map/ppermute | solution.py:36
  124.6 25.6 %collective-permute-start.23 = (bf16[512,512]{1,0:T(8,128)(2,1)S(1)}, bf16[512,512]{1,0:T(8,128)(2,1)S(1)}, u32[]{:S(2)}, u32[]{:S(2)}) collective-permute-start(bf16[512,512]{1,0:T(8,128)(2,1)S(1)} %get-tuple-element.43), channel_id=1, source_target_pairs={{0,12},{4,0},{8,4},{12,8},{1,13},{5,1},{9,5},{13,9},{2,14},{6,2},{... | collective-permute-start | bytes 1572872 | tf_op jit(solution)/shard_map/ppermute | solution.py:36
  147.4 8.7 %collective-permute-start.18 = (bf16[512,128]{1,0:T(8,128)(2,1)S(1)}, bf16[512,128]{1,0:T(8,128)(2,1)S(1)}, u32[]{:S(2)}, u32[]{:S(2)}) collective-permute-start(bf16[512,128]{1,0:T(8,128)(2,1)S(1)} %get-tuple-element.37), channel_id=1, source_target_pairs={{0,4},{4,8},{8,12},{12,0},{1,5},{5,9},{9,13},{13,1},{2,6},{6,10},{... | collective-permute-start | bytes 393224 | tf_op jit(solution)/shard_map/ppermute | solution.py:36
  147.5 10.4 %collective-permute-start.19 = (bf16[512,128]{1,0:T(8,128)(2,1)S(1)}, bf16[512,128]{1,0:T(8,128)(2,1)S(1)}, u32[]{:S(2)}, u32[]{:S(2)}) collective-permute-start(bf16[512,128]{1,0:T(8,128)(2,1)S(1)} %get-tuple-element.38), channel_id=1, source_target_pairs={{0,8},{4,12},{8,0},{12,4},{1,9},{5,13},{9,1},{13,5},{2,10},{6,14},... | collective-permute-start | bytes 393224 | tf_op jit(solution)/shard_map/ppermute | solution.py:36
  148.8 9.0 %collective-permute-start.20 = (bf16[512,128]{1,0:T(8,128)(2,1)S(1)}, bf16[512,128]{1,0:T(8,128)(2,1)S(1)}, u32[]{:S(2)}, u32[]{:S(2)}) collective-permute-start(bf16[512,128]{1,0:T(8,128)(2,1)S(1)} %get-tuple-element.39), channel_id=1, source_target_pairs={{0,12},{4,0},{8,4},{12,8},{1,13},{5,1},{9,5},{13,9},{2,14},{6,2},{... | collective-permute-start | bytes 393224 | tf_op jit(solution)/shard_map/ppermute | solution.py:36
  151.0 6.9 %collective-permute-start.24 = (bf16[512,128]{1,0:T(8,128)(2,1)S(1)}, bf16[512,128]{1,0:T(8,128)(2,1)S(1)}, u32[]{:S(2)}, u32[]{:S(2)}) collective-permute-start(bf16[512,128]{1,0:T(8,128)(2,1)S(1)} %get-tuple-element.45), channel_id=1, source_target_pairs={{0,64},{64,128},{128,192},{192,0},{1,65},{65,129},{129,193},{193,1... | collective-permute-start | bytes 393224 | tf_op jit(solution)/shard_map/ppermute | solution.py:36
  152.3 6.2 %collective-permute-start.25 = (bf16[512,128]{1,0:T(8,128)(2,1)S(1)}, bf16[512,128]{1,0:T(8,128)(2,1)S(1)}, u32[]{:S(2)}, u32[]{:S(2)}) collective-permute-start(bf16[512,128]{1,0:T(8,128)(2,1)S(1)} %get-tuple-element.46), channel_id=1, source_target_pairs={{0,128},{64,192},{128,0},{192,64},{1,129},{65,193},{129,1},{193,65... | collective-permute-start | bytes 393224 | tf_op jit(solution)/shard_map/ppermute | solution.py:36
  156.1 5.1 %collective-permute-start.26 = (bf16[512,128]{1,0:T(8,128)(2,1)S(1)}, bf16[512,128]{1,0:T(8,128)(2,1)S(1)}, u32[]{:S(2)}, u32[]{:S(2)}) collective-permute-start(bf16[512,128]{1,0:T(8,128)(2,1)S(1)} %get-tuple-element.47), channel_id=1, source_target_pairs={{0,192},{64,0},{128,64},{192,128},{1,193},{65,1},{129,65},{193,129... | collective-permute-start | bytes 393224 | tf_op jit(solution)/shard_map/ppermute | solution.py:36
  162.0 16.7 %all-to-all-start.4 = ((bf16[8,128,128]{2,1,0:T(8,128)(2,1)}), bf16[8,128,128]{2,1,0:T(8,128)(2,1)S(1)}, u32[]{:S(2)}, u32[]{:S(2)}) async-start(bf16[8,128,128]{2,1,0:T(8,128)(2,1)} %shard_map.99), calls=%async_computation.4 | async-start | bytes 524288 | tf_op jit(solution)/shard_map/all_to_all | solution.py:346
  178.7 18.7 %all-to-all-start.3 = ((bf16[16,128,128]{2,1,0:T(8,128)(2,1)}), bf16[16,128,128]{2,1,0:T(8,128)(2,1)S(1)}, u32[]{:S(2)}, u32[]{:S(2)}) async-start(bf16[16,128,128]{2,1,0:T(8,128)(2,1)} %shard_map.92), calls=%async_computation.3 | async-start | bytes 1048576 | tf_op jit(solution)/shard_map/all_to_all | solution.py:284
  197.5 10.3 %copy-start.23 = (bf16[16,128,128]{2,1,0:T(8,128)(2,1)}, bf16[16,128,128]{2,1,0:T(8,128)(2,1)S(1)}, u32[]{:S(2)}) copy-start(bf16[16,128,128]{2,1,0:T(8,128)(2,1)S(1)} %all-to-all-done.3.l_ref) | copy-start | bytes 1572868
  197.5 18.3 %all-to-all-start.5 = ((bf16[16,128,128]{2,1,0:T(8,128)(2,1)}), bf16[16,128,128]{2,1,0:T(8,128)(2,1)S(1)}, u32[]{:S(2)}, u32[]{:S(2)}) async-start(bf16[16,128,128]{2,1,0:T(8,128)(2,1)} %shard_map.100), calls=%async_computation.5 | async-start | bytes 1048576 | tf_op jit(solution)/shard_map/all_to_all | solution.py:348
  (9 other events, 9.6 us)

commit v3 on v2

--- a/solution.py
+++ b/solution.py
@@ -1,4 +1,5 @@
 import functools
+import math
 
 import jax
 import jax.numpy as jnp
@@ -40,7 +41,7 @@
 def call(body, out, *args, grid=None, in_specs=None, out_specs=None, flops=0, room=None):
     size = sum(a.size * a.dtype.itemsize for a in args)
     outs = out if isinstance(out, (tuple, list)) else [out]
-    size += sum(o.size * jnp.dtype(o.dtype).itemsize for o in outs)
+    size += sum(math.prod(o.shape) * jnp.dtype(o.dtype).itemsize for o in outs)
     kwargs = {}
     if grid is not None:
         kwargs = dict(grid=grid)
@@ -66,7 +67,11 @@
     return jax.ShapeDtypeStruct(dims, dtype)
 
 
-PER = 4
+def in_hbm(dims, dtype=BF16):
+    return pltpu.HBM(dims, dtype)
+
+
+PER = 8
 
 
 def head_slices():
@@ -226,11 +231,9 @@
 
 
 def place_body(at_ref, *refs):
-    size, half = refs[0].shape[0], refs[4].shape[1]
-    for k in range(4):
-        s = block(at_ref[3], k, size)
-        refs[4][s, :] = refs[k][:, :half]
-        refs[5][s, :] = refs[k][:, half:]
+    size = refs[0].shape[0]
+    for k in range(4):
+        refs[4][block(at_ref[3], k, size), :] = refs[k][...]
 
 
 def stack_body(at_ref, *refs):
@@ -280,15 +283,17 @@
 
     def exchange(states, reverse):
         by_head = lax.all_to_all(states, CTX, 0, 0)
-        sums = call(functools.partial(scan_body, reverse), shape(by_head.shape), by_head, flops=by_head.size)
+        sums = call(functools.partial(scan_body, reverse), in_hbm(by_head.shape), by_head, flops=by_head.size)
         return lax.all_to_all(sums, CTX, 0, 0)
 
     half, part = width // 2, width // 8
     wa = lax.dynamic_slice(out_weight, (0, core * width), (out_weight.shape[0], half))
     wb = lax.dynamic_slice(out_weight, (0, core * width + half + y * part), (out_weight.shape[0], part))
-    wz = copies(jnp.concatenate([wa, wb], axis=1), "zh")
+    zb = copies(wb, "zh")
+    za = copies(wa, "zh")
     z_rows = 4 * out_weight.shape[0]
-    wa, wb = call(place_body, [shape((z_rows, half)), shape((z_rows, part))], at, *wz)
+    wb = call(place_body, shape((z_rows, part)), at, *zb)
+    wa = call(place_body, shape((z_rows, half)), at, *za)
     xb = copies(wb, "x")
     xa = copies(wa, "x")
     wb = call(stack_body, shape((inner, part)), at, *xb)
@@ -325,7 +330,7 @@
     gy = spread(gy, "y")
     gx = spread(gx, "x")
     ga, grad_states = call(
-        grad_attn_body, [shape((tokens, inner)), shape((HEADS, HEAD, HEAD))], mine, from_partner, q,
+        grad_attn_body, [in_hbm((tokens, inner)), in_hbm((HEADS, HEAD, HEAD))], mine, from_partner, q,
         grid=heads, in_specs=[rows, rows, rows], out_specs=[rows, STATE_SPEC], flops=token_flops,
     )
     quarter = shape((inner // 4, width // 8))
@@ -344,7 +349,7 @@
         grid=heads, in_specs=[rows, rows, rows, rows, STATE_SPEC], out_specs=[rows, rows], flops=10 * token_flops, room=ALL_ROOM,
     )
     gz = lax.all_to_all(gz, ("zl", "zh"), 0, 0)
-    total = call(add_then_all_body, shape((16, inner // 16, width // 8)), gz)
+    total = call(add_then_all_body, in_hbm((16, inner // 16, width // 8)), gz)
     gathered = lax.all_to_all(total, CTX, 0, 0)
     grad_weight = call(functools.partial(finish_weight_body, scale), shape((inner // 16, 2 * width), F32), gathered)
 

time: 218 us -> 213 us (0.977)
  waiting for transfers between devices: 77.6 us -> 53.2 us
  starting transfers between devices: 80.3 us -> 103 us
  Pallas kernels: 47.5 us -> 44.9 us
    ppermute x12 -> x15, waiting for transfers between devices: 33.6 us -> 7.72 us  [copies(): lax.ppermute(v, axis, [((i + k) % 4, i) for i in range(4)])]
    all_to_all x2, starting transfers between devices: 17 us -> 29.4 us  [exchange(): return lax.all_to_all(sums, CTX, 0, 0)]
    ppermute x3, starting transfers between devices: 0.98 us -> 13.3 us  [from_core(): return lax.ppermute(v, 'c', [(0, 1), (1, 0)])]
    all_to_all x1, starting transfers between devices: 8.96 us -> 4.62 us  [local(): gz = lax.all_to_all(gz, ('zl', 'zh'), 0, 0)]
    ppermute x12 -> x15, starting transfers between devices: 24.5 us -> 27.5 us  [copies(): lax.ppermute(v, axis, [((i + k) % 4, i) for i in range(4)])]
    pallas_call x18 -> x19, Pallas kernels: 47.5 us -> 44.9 us  [call(): pl.pallas_call(body, out_shape=out, in_specs=list(in_specs), out_specs=ou...]
    unnamed x48 -> x44, local copies, waits for them, and re-layouts: 9.64 us -> 9.02 us
  transfers between devices with their start and end apart: 33 -> 36, of which waited for: 12 -> 14; matrix products, arithmetic and copies ran while one was open for 0% -> 0% of each run, Pallas kernels for 21% -> 21%
where the time goes in v3:
time: 213 us; the launch traced here: 212 us
  starting transfers between devices  103 us (48%)
  waiting for transfers between devices  53.2 us (25%)
  Pallas kernels  44.9 us (21%)
  local copies, waits for them, and re-layouts  9.88 us (5%)
    pallas_call x19, Pallas kernels, call(): pl.pallas_call(body, out_shape=out, in_specs=list(in_specs), out_specs=ou...  44.9 us
    all_to_all x2, starting transfers between devices, exchange(): return lax.all_to_all(sums, CTX, 0, 0)  29.4 us
    ppermute x15, starting transfers between devices, copies(): lax.ppermute(v, axis, [((i + k) % 4, i) for i in range(4)])  27.5 us
    ppermute x12, waiting for transfers between devices, spread(): lax.ppermute(pieces[k], axis, [(i, (i + k) % 4) for i in range(4)])  27.1 us
    ppermute x3, starting transfers between devices, from_core(): return lax.ppermute(v, 'c', [(0, 1), (1, 0)])  13.3 us
    all_to_all x2, starting transfers between devices, exchange(): by_head = lax.all_to_all(states, CTX, 0, 0)  12.2 us
    ppermute x12, starting transfers between devices, spread(): lax.ppermute(pieces[k], axis, [(i, (i + k) % 4) for i in range(4)])  11.5 us
    unnamed x44, local copies, waits for them, and re-layouts  9.02 us
  transfers between devices with their start and end apart: 36, of which 14 were waited for; matrix products, arithmetic and copies ran while one was open for 0% of the time, Pallas kernels for 21%

profile of v3, /device:TPU:1, one launch (start us, length us, event | category | flops | bytes accessed | tf_op | source)
XLA Modules:
  0.0 212.2 jit_solution(13418276151607310006)
XLA Ops:
  1.7 6.9 %collective-permute-start = (bf16[128,512]{1,0:T(8,128)(2,1)S(1)}, bf16[128,512]{1,0:T(8,128)(2,1)S(1)}, u32[]{:S(2)}, u32[]{:S(2)}) collective-permute-start(bf16[128,512]{1,0:T(8,128)(2,1)S(1)} %constant_dynamic-slice_fusion.1.refs_0_), channel_id=1, source_target_pairs={{1,0},{2,1},{3,2},{0,3},{5,4},{6,5},{7,6},{4,7},{9,8},{10,9},{11,1... | collective-permute-start | bytes 393224 | tf_op jit(solution)/shard_map/ppermute | solution.py:32
  9.6 2.3 %collective-permute-start.2 = (bf16[128,512]{1,0:T(8,128)(2,1)S(1)}, bf16[128,512]{1,0:T(8,128)(2,1)S(1)}, u32[]{:S(2)}, u32[]{:S(2)}) collective-permute-start(bf16[128,512]{1,0:T(8,128)(2,1)S(1)} %constant_dynamic-slice_fusion.1.refs_0_), channel_id=1, source_target_pairs={{3,0},{0,1},{1,2},{2,3},{7,4},{4,5},{5,6},{6,7},{11,8},{8,9},{9,10... | collective-permute-start | bytes 393224 | tf_op jit(solution)/shard_map/ppermute | solution.py:32
  11.9 2.6 %shard_map.90 = bf16[16,128,128]{2,1,0:T(8,128)(2,1)} custom-call(bf16[256,2048]{1,0:T(8,128)(2,1)} %bitcast.13, bf16[256,2048]{1,0:T(8,128)(2,1)} %bitcast.17), custom_call_target="tpu_custom_call" | custom-call | flops 134217728 | bytes 2621440 | tf_op jit(solution)/shard_map/pallas_call | solution.py:55
  14.5 6.5 %all-to-all-start = ((bf16[16,128,128]{2,1,0:T(8,128)(2,1)}), bf16[16,128,128]{2,1,0:T(8,128)(2,1)S(1)}, u32[]{:S(2)}, u32[]{:S(2)}) async-start(bf16[16,128,128]{2,1,0:T(8,128)(2,1)} %shard_map.90), calls=%async_computation | async-start | bytes 1048576 | tf_op jit(solution)/shard_map/all_to_all | solution.py:285
  22.0 1.4 shard_map.84.a0
  23.4 2.5 %collective-permute-start.3 = (bf16[512,512]{1,0:T(8,128)(2,1)}, bf16[512,512]{1,0:T(8,128)(2,1)S(1)}, u32[]{:S(2)}, u32[]{:S(2)}) collective-permute-start(bf16[512,512]{1,0:T(8,128)(2,1)} %shard_map.84.a0), channel_id=1, source_target_pairs={{4,0},{8,4},{12,8},{0,12},{5,1},{9,5},{13,9},{1,13},{6,2},{10,6},{... | collective-permute-start | bytes 1572872 | tf_op jit(solution)/shard_map/ppermute | solution.py:32
  25.9 2.0 collective-permute-start.6
  27.9 3.7 %collective-permute-start.7 = (bf16[128,128]{1,0:T(8,128)(2,1)S(1)}, bf16[128,128]{1,0:T(8,128)(2,1)S(1)}, u32[]{:S(2)}, u32[]{:S(2)}) collective-permute-start(bf16[128,128]{1,0:T(8,128)(2,1)S(1)} %constant_dynamic-slice_fusion.refs_0_), channel_id=1, source_target_pairs={{2,0},{3,1},{0,2},{1,3},{6,4},{7,5},{4,6},{5,7},{10,8},{11,9},{8,1... | collective-permute-start | bytes 98312 | tf_op jit(solution)/shard_map/ppermute | solution.py:32
  32.3 2.3 %collective-permute-done.7.refs_2_ = bf16[128,128]{1,0:T(8,128)(2,1)S(1)} collective-permute-done((bf16[128,128]{1,0:T(8,128)(2,1)S(1)}, bf16[128,128]{1,0:T(8,128)(2,1)S(1)}, u32[]{:S(2)}, u32[]{:S(2)}) %collective-permute-start.7) | collective-permute-done | bytes 32800 | tf_op jit(solution)/shard_map/ppermute | solution.py:32
  34.7 2.1 collective-permute-done.8.refs_3_
  38.9 2.3 %collective-permute-done.9.refs_1_ = bf16[512,128]{1,0:T(8,128)(2,1)S(1)} collective-permute-done((bf16[512,128]{1,0:T(8,128)(2,1)S(1)}, bf16[512,128]{1,0:T(8,128)(2,1)S(1)}, u32[]{:S(2)}, u32[]{:S(2)}) %collective-permute-start.9) | collective-permute-done | bytes 131104 | tf_op jit(solution)/shard_map/ppermute | solution.py:32
  41.2 1.2 collective-permute-start.4
  43.4 1.9 collective-permute-start.5
  45.3 1.4 shard_map.86.b0
  46.6 2.8 %collective-permute-start.12 = (bf16[2048,128]{1,0:T(8,128)(2,1)}, bf16[2048,128]{1,0:T(8,128)(2,1)}, u32[]{:S(2)}, u32[]{:S(2)}) collective-permute-start(bf16[2048,128]{1,0:T(8,128)(2,1)} %shard_map.86.b0), channel_id=1, source_target_pairs={{64,0},{128,64},{192,128},{0,192},{65,1},{129,65},{193,129},{1,193... | collective-permute-start | bytes 1572872 | tf_op jit(solution)/shard_map/ppermute | solution.py:32
  51.3 20.4 %all-to-all-start.1 = ((bf16[16,128,128]{2,1,0:T(8,128)(2,1)}), bf16[16,128,128]{2,1,0:T(8,128)(2,1)S(1)}, u32[]{:S(2)}, u32[]{:S(2)}) async-start(bf16[16,128,128]{2,1,0:T(8,128)(2,1)} %shard_map.91), calls=%async_computation.1 | async-start | bytes 1048576 | tf_op jit(solution)/shard_map/all_to_all | solution.py:287
  71.8 1.2 copy-done.10
  74.0 4.6 %shard_map.88 = f32[256,2048]{1,0:T(8,128)} custom-call(s32[4]{0:T(128)S(1)} %pad_add_fusion.at_ref, bf16[256,1024]{1,0:T(8,128)(2,1)S(1)} %copy-done.15, bf16[512,512]{1,0:T(8,128)(2,1)} %shard_map.84.a0, bf16[512,512]{1,0:T(8,128)(2,1)S(1)} %copy-done.10, bf16[512,512]{1,0:T(8,128)(2,1)} %collective-permute-done.4.a2, ...), custom_call_target="tpu_custom_call" | custom-call | flops 1073741824 | bytes 6815760 | tf_op jit(solution)/shard_map/pallas_call | solution.py:55
  78.6 13.1 %collective-permute-start.16 = (f32[256,2048]{1,0:T(8,128)}, f32[256,2048]{1,0:T(8,128)}, u32[]{:S(2)}, u32[]{:S(2)}) collective-permute-start(f32[256,2048]{1,0:T(8,128)} %shard_map.88), channel_id=1, source_target_pairs={{0,16},{16,0},{1,17},{17,1},{2,18},{18,2},{3,19},{19,3},{4,20},{20... | collective-permute-start | bytes 6291464 | tf_op jit(solution)/shard_map/ppermute | solution.py:28
  91.8 1.4 copy-done.4
  93.2 2.8 %shard_map.95.mine_ref = bf16[2048,256]{1,0:T(8,128)(2,1)S(1)} custom-call(bf16[256,2048]{1,0:T(8,128)(2,1)S(1)} %bitcast.22, bf16[256,2048]{1,0:T(8,128)(2,1)S(1)} %bitcast.16, bf16[256,2048]{1,0:T(8,128)(2,1)S(1)} %bitcast.20, bf16[16,128,128]{2,1,0:T(8,128)(2,1)S(1)} %all-to-all-done.1.p_ref), custom_call_target="tpu_custom_call" | custom-call | flops 671088640 | bytes 4718592 | tf_op jit(solution)/shard_map/pallas_call | solution.py:55
  96.1 2.6 %collective-permute-done.17.theirs_ref = bf16[2048,256]{1,0:T(8,128)(2,1)S(1)} collective-permute-done((bf16[2048,256]{1,0:T(8,128)(2,1)S(1)}, bf16[2048,256]{1,0:T(8,128)(2,1)S(1)}, u32[]{:S(2)}, u32[]{:S(2)}) %collective-permute-start.17) | collective-permute-done | bytes 1048608 | tf_op jit(solution)/shard_map/ppermute | solution.py:28
  98.8 3.3 %shard_map.96 = (bf16[2048,128]{1,0:T(8,128)(2,1)S(1)}, bf16[2048,128]{1,0:T(8,128)(2,1)}, bf16[2048,128]{1,0:T(8,128)(2,1)S(1)}, bf16[2048,128]{1,0:T(8,128)(2,1)S(1)}) custom-call(s32[4]{0:T(128)S(1)} %pad_add_fusion.at_ref, bf16[2048,256]{1,0:T(8,128)(2,1)S(1)} %shard_map.95.mine_ref, bf16[2048,256]{1,0:T(8,128)(2,1)S(1)} %collective-permute-done.17.theirs_ref, ...), custom_call_target="tpu_custom_call" | custom-call | flops 1073741824 | bytes 5767184 | tf_op jit(solution)/shard_map/pallas_call | solution.py:55
  102.9 3.4 %shard_map.87.mine_ref = f32[256,2048]{1,0:T(8,128)S(1)} custom-call(s32[4]{0:T(128)S(1)} %pad_add_fusion.at_ref, bf16[256,2048]{1,0:T(8,128)(2,1)S(1)} %bitcast.25, bf16[512,512]{1,0:T(8,128)(2,1)} %shard_map.84.a0, bf16[512,512]{1,0:T(8,128)(2,1)S(1)} %copy-done.11, bf16[512,512]{1,0:T(8,128)(2,1)} %collective-permute-done.4.a2, ...), custom_call_target="tpu_custom_call" | custom-call | flops 1073741824 | bytes 7340048 | tf_op jit(solution)/shard_map/pallas_call | solution.py:55
  106.3 3.0 %shard_map.89 = (bf16[256,2048]{1,0:T(8,128)(2,1)}, bf16[16,128,128]{2,1,0:T(8,128)(2,1)}) custom-call(f32[256,2048]{1,0:T(8,128)S(1)} %shard_map.87.mine_ref, f32[256,2048]{1,0:T(8,128)} %collective-permute-done.16.theirs_ref, bf16[256,2048]{1,0:T(8,128)(2,1)S(1)} %bitcast.23), custom_call_target="tpu_custom_call" | custom-call | flops 134217728 | bytes 6815744 | tf_op jit(solution)/shard_map/pallas_call | solution.py:55
  109.3 5.7 %all-to-all-start.2 = ((bf16[16,128,128]{2,1,0:T(8,128)(2,1)}), bf16[16,128,128]{2,1,0:T(8,128)(2,1)S(1)}, u32[]{:S(2)}, u32[]{:S(2)}) async-start(bf16[16,128,128]{2,1,0:T(8,128)(2,1)} %get-tuple-element.25), calls=%async_computation.2 | async-start | bytes 1048576 | tf_op jit(solution)/shard_map/all_to_all | solution.py:285
  115.0 2.9 %collective-permute-start.19 = (bf16[2048,128]{1,0:T(8,128)(2,1)}, bf16[2048,128]{1,0:T(8,128)(2,1)S(1)}, u32[]{:S(2)}, u32[]{:S(2)}) collective-permute-start(bf16[2048,128]{1,0:T(8,128)(2,1)} %copy-done.20), channel_id=1, source_target_pairs={{0,128},{64,192},{128,0},{192,64},{1,129},{65,193},{129,1},{193,65... | collective-permute-start | bytes 1572872 | tf_op jit(solution)/shard_map/ppermute | solution.py:37
  118.8 1.2 copy-done.13
  121.0 1.2 copy-done.19
  122.2 1.8 shard_map.98
  124.2 2.6 %collective-permute-start.26 = (bf16[512,512]{1,0:T(8,128)(2,1)S(1)}, bf16[512,512]{1,0:T(8,128)(2,1)S(1)}, u32[]{:S(2)}, u32[]{:S(2)}) collective-permute-start(bf16[512,512]{1,0:T(8,128)(2,1)S(1)} %get-tuple-element.39), channel_id=1, source_target_pairs={{0,12},{4,0},{8,4},{12,8},{1,13},{5,1},{9,5},{13,9},{2,14},{6,2},{... | collective-permute-start | bytes 1572872 | tf_op jit(solution)/shard_map/ppermute | solution.py:37
  126.8 8.8 %collective-permute-done.19.refs_2_ = bf16[2048,128]{1,0:T(8,128)(2,1)S(1)} collective-permute-done((bf16[2048,128]{1,0:T(8,128)(2,1)}, bf16[2048,128]{1,0:T(8,128)(2,1)S(1)}, u32[]{:S(2)}, u32[]{:S(2)}) %collective-permute-start.19) | collective-permute-done | bytes 524320 | tf_op jit(solution)/shard_map/ppermute | solution.py:37
  135.6 9.7 %collective-permute-done.20.refs_3_ = bf16[2048,128]{1,0:T(8,128)(2,1)S(1)} collective-permute-done((bf16[2048,128]{1,0:T(8,128)(2,1)S(1)}, bf16[2048,128]{1,0:T(8,128)(2,1)S(1)}, u32[]{:S(2)}, u32[]{:S(2)}) %collective-permute-start.20) | collective-permute-done | bytes 524320 | tf_op jit(solution)/shard_map/ppermute | solution.py:37
  145.3 1.3 shard_map.97
  146.8 2.2 %collective-permute-done.24.refs_1_ = bf16[512,512]{1,0:T(8,128)(2,1)S(1)} collective-permute-done((bf16[512,512]{1,0:T(8,128)(2,1)S(1)}, bf16[512,512]{1,0:T(8,128)(2,1)S(1)}, u32[]{:S(2)}, u32[]{:S(2)}) %collective-permute-start.24) | collective-permute-done | bytes 524320 | tf_op jit(solution)/shard_map/ppermute | solution.py:37
  150.3 1.2 collective-permute-start.27
  151.6 1.6 collective-permute-start.28
  153.2 2.6 %collective-permute-done.21.refs_1_ = bf16[512,128]{1,0:T(8,128)(2,1)S(1)} collective-permute-done((bf16[512,128]{1,0:T(8,128)(2,1)S(1)}, bf16[512,128]{1,0:T(8,128)(2,1)S(1)}, u32[]{:S(2)}, u32[]{:S(2)}) %collective-permute-start.21) | collective-permute-done | bytes 131104 | tf_op jit(solution)/shard_map/ppermute | solution.py:37
  155.8 1.7 collective-permute-start.29
  158.1 3.1 %collective-permute-done.29.refs_7_ = bf16[512,128]{1,0:T(8,128)(2,1)S(1)} collective-permute-done((bf16[512,128]{1,0:T(8,128)(2,1)S(1)}, bf16[512,128]{1,0:T(8,128)(2,1)S(1)}, u32[]{:S(2)}, u32[]{:S(2)}) %collective-permute-start.29) | collective-permute-done | bytes 131104 | tf_op jit(solution)/shard_map/ppermute | solution.py:37
  162.0 4.6 %all-to-all-start.4 = ((bf16[8,128,128]{2,1,0:T(8,128)(2,1)}), bf16[8,128,128]{2,1,0:T(8,128)(2,1)S(1)}, u32[]{:S(2)}, u32[]{:S(2)}) async-start(bf16[8,128,128]{2,1,0:T(8,128)(2,1)} %shard_map.100), calls=%async_computation.4 | async-start | bytes 524288 | tf_op jit(solution)/shard_map/all_to_all | solution.py:351
  167.5 6.9 %all-to-all-done.4.i_ref = bf16[8,128,128]{2,1,0:T(8,128)(2,1)S(1)} async-done(((bf16[8,128,128]{2,1,0:T(8,128)(2,1)}), bf16[8,128,128]{2,1,0:T(8,128)(2,1)S(1)}, u32[]{:S(2)}, u32[]{:S(2)}) %all-to-all-start.4) | async-done | bytes 262176 | tf_op jit(solution)/shard_map/all_to_all | solution.py:351
  174.4 9.0 %all-to-all-start.3 = ((bf16[16,128,128]{2,1,0:T(8,128)(2,1)}), bf16[16,128,128]{2,1,0:T(8,128)(2,1)S(1)}, u32[]{:S(2)}, u32[]{:S(2)}) async-start(bf16[16,128,128]{2,1,0:T(8,128)(2,1)} %shard_map.93), calls=%async_computation.3 | async-start | bytes 1048576 | tf_op jit(solution)/shard_map/all_to_all | solution.py:287
  184.3 8.8 %all-to-all-done.3.l_ref = bf16[16,128,128]{2,1,0:T(8,128)(2,1)S(1)} async-done(((bf16[16,128,128]{2,1,0:T(8,128)(2,1)}), bf16[16,128,128]{2,1,0:T(8,128)(2,1)S(1)}, u32[]{:S(2)}, u32[]{:S(2)}) %all-to-all-start.3) | async-done | bytes 524320 | tf_op jit(solution)/shard_map/all_to_all | solution.py:287
  193.1 4.6 %all-to-all-start.5 = ((bf16[16,128,128]{2,1,0:T(8,128)(2,1)}), bf16[16,128,128]{2,1,0:T(8,128)(2,1)S(1)}, u32[]{:S(2)}, u32[]{:S(2)}) async-start(bf16[16,128,128]{2,1,0:T(8,128)(2,1)} %shard_map.101), calls=%async_computation.5 | async-start | bytes 1048576 | tf_op jit(solution)/shard_map/all_to_all | solution.py:353
  197.7 5.4 %shard_map.92 = bf16[256,2048]{1,0:T(8,128)(2,1)} custom-call(bf16[256,2048]{1,0:T(8,128)(2,1)} %get-tuple-element.24.g_ref, bf16[256,2048]{1,0:T(8,128)(2,1)} %bitcast.14, bf16[256,2048]{1,0:T(8,128)(2,1)} %bitcast.18, bf16[16,128,128]{2,1,0:T(8,128)(2,1)} %copy-done.3), custom_call_target="tpu_custom_call" | custom-call | flops 671088640 | bytes 4718592 | tf_op jit(solution)/shard_map/pallas_call | solution.py:55
  203.1 8.0 %shard_map.94 = (bf16[256,2048]{1,0:T(8,128)(2,1)}, bf16[256,2048]{1,0:T(8,128)(2,1)}) custom-call(bf16[256,2048]{1,0:T(8,128)(2,1)} %get-tuple-element.24.g_ref, bf16[256,2048]{1,0:T(8,128)(2,1)} %bitcast.21, bf16[256,2048]{1,0:T(8,128)(2,1)} %bitcast.15, bf16[256,2048]{1,0:T(8,128)(2,1)} %bitcast.19, bf16[16,128,128]{2,1,0:T(8,128)(2,1)} %copy-done.21), custom_call_target="tpu_custom_call" | custom-call | flops 1342177280 | bytes 6815744 | tf_op jit(solution)/shard_map/pallas_call | solution.py:55
  211.1 1.1 shard_map.102
  (91 shorter events, 17.4 us)
Async XLA Ops:
  0.6 20.3 %copy-start.6 = (bf16[1,256,2048]{2,1,0:T(8,128)(2,1)S(1)}, bf16[1,256,2048]{2,1,0:T(8,128)(2,1)}, u32[]{:S(2)}) copy-start(bf16[1,256,2048]{2,1,0:T(8,128)(2,1)} %param.9) | copy-start | bytes 3145732
  1.7 20.3 %collective-permute-start = (bf16[128,512]{1,0:T(8,128)(2,1)S(1)}, bf16[128,512]{1,0:T(8,128)(2,1)S(1)}, u32[]{:S(2)}, u32[]{:S(2)}) collective-permute-start(bf16[128,512]{1,0:T(8,128)(2,1)S(1)} %constant_dynamic-slice_fusion.1.refs_0_), channel_id=1, source_target_pairs={{1,0},{2,1},{3,2},{0,3},{5,4},{6,5},{7,6},{4,7},{9,8},{10,9},{11,1... | collective-permute-start | bytes 393224 | tf_op jit(solution)/shard_map/ppermute | solution.py:32
  8.6 13.4 %collective-permute-start.1 = (bf16[128,512]{1,0:T(8,128)(2,1)S(1)}, bf16[128,512]{1,0:T(8,128)(2,1)S(1)}, u32[]{:S(2)}, u32[]{:S(2)}) collective-permute-start(bf16[128,512]{1,0:T(8,128)(2,1)S(1)} %constant_dynamic-slice_fusion.1.refs_0_), channel_id=1, source_target_pairs={{2,0},{3,1},{0,2},{1,3},{6,4},{7,5},{4,6},{5,7},{10,8},{11,9},{8,1... | collective-permute-start | bytes 393224 | tf_op jit(solution)/shard_map/ppermute | solution.py:32
  9.6 12.4 %collective-permute-start.2 = (bf16[128,512]{1,0:T(8,128)(2,1)S(1)}, bf16[128,512]{1,0:T(8,128)(2,1)S(1)}, u32[]{:S(2)}, u32[]{:S(2)}) collective-permute-start(bf16[128,512]{1,0:T(8,128)(2,1)S(1)} %constant_dynamic-slice_fusion.1.refs_0_), channel_id=1, source_target_pairs={{3,0},{0,1},{1,2},{2,3},{7,4},{4,5},{5,6},{6,7},{11,8},{8,9},{9,10... | collective-permute-start | bytes 393224 | tf_op jit(solution)/shard_map/ppermute | solution.py:32
  14.5 35.9 %all-to-all-start = ((bf16[16,128,128]{2,1,0:T(8,128)(2,1)}), bf16[16,128,128]{2,1,0:T(8,128)(2,1)S(1)}, u32[]{:S(2)}, u32[]{:S(2)}) async-start(bf16[16,128,128]{2,1,0:T(8,128)(2,1)} %shard_map.90), calls=%async_computation | async-start | bytes 1048576 | tf_op jit(solution)/shard_map/all_to_all | solution.py:285
  21.8 27.7 %collective-permute-start.15 = (bf16[256,1024]{1,0:T(8,128)(2,1)}, bf16[256,1024]{1,0:T(8,128)(2,1)S(1)}, u32[]{:S(2)}, u32[]{:S(2)}) collective-permute-start(bf16[256,1024]{1,0:T(8,128)(2,1)} %dynamic-slice_bitcast_fusion), channel_id=1, source_target_pairs={{0,16},{16,0},{1,17},{17,1},{2,18},{18,2},{3,19},{19,3},{4,20},{20... | collective-permute-start | bytes 1572872 | tf_op jit(solution)/shard_map/ppermute | solution.py:28
  23.4 26.3 %collective-permute-start.3 = (bf16[512,512]{1,0:T(8,128)(2,1)}, bf16[512,512]{1,0:T(8,128)(2,1)S(1)}, u32[]{:S(2)}, u32[]{:S(2)}) collective-permute-start(bf16[512,512]{1,0:T(8,128)(2,1)} %shard_map.84.a0), channel_id=1, source_target_pairs={{4,0},{8,4},{12,8},{0,12},{5,1},{9,5},{13,9},{1,13},{6,2},{10,6},{... | collective-permute-start | bytes 1572872 | tf_op jit(solution)/shard_map/ppermute | solution.py:32
  25.9 6.5 %collective-permute-start.6 = (bf16[128,128]{1,0:T(8,128)(2,1)S(1)}, bf16[128,128]{1,0:T(8,128)(2,1)S(1)}, u32[]{:S(2)}, u32[]{:S(2)}) collective-permute-start(bf16[128,128]{1,0:T(8,128)(2,1)S(1)} %constant_dynamic-slice_fusion.refs_0_), channel_id=1, source_target_pairs={{1,0},{2,1},{3,2},{0,3},{5,4},{6,5},{7,6},{4,7},{9,8},{10,9},{11,1... | collective-permute-start | bytes 98312 | tf_op jit(solution)/shard_map/ppermute | solution.py:32
  27.9 6.8 %collective-permute-start.7 = (bf16[128,128]{1,0:T(8,128)(2,1)S(1)}, bf16[128,128]{1,0:T(8,128)(2,1)S(1)}, u32[]{:S(2)}, u32[]{:S(2)}) collective-permute-start(bf16[128,128]{1,0:T(8,128)(2,1)S(1)} %constant_dynamic-slice_fusion.refs_0_), channel_id=1, source_target_pairs={{2,0},{3,1},{0,2},{1,3},{6,4},{7,5},{4,6},{5,7},{10,8},{11,9},{8,1... | collective-permute-start | bytes 98312 | tf_op jit(solution)/shard_map/ppermute | solution.py:32
  31.6 5.1 %collective-permute-start.8 = (bf16[128,128]{1,0:T(8,128)(2,1)S(1)}, bf16[128,128]{1,0:T(8,128)(2,1)S(1)}, u32[]{:S(2)}, u32[]{:S(2)}) collective-permute-start(bf16[128,128]{1,0:T(8,128)(2,1)S(1)} %constant_dynamic-slice_fusion.refs_0_), channel_id=1, source_target_pairs={{3,0},{0,1},{1,2},{2,3},{7,4},{4,5},{5,6},{6,7},{11,8},{8,9},{9,10... | collective-permute-start | bytes 98312 | tf_op jit(solution)/shard_map/ppermute | solution.py:32
  37.3 3.9 %collective-permute-start.9 = (bf16[512,128]{1,0:T(8,128)(2,1)S(1)}, bf16[512,128]{1,0:T(8,128)(2,1)S(1)}, u32[]{:S(2)}, u32[]{:S(2)}) collective-permute-start(bf16[512,128]{1,0:T(8,128)(2,1)S(1)} %shard_map.85.refs_0_), channel_id=1, source_target_pairs={{4,0},{8,4},{12,8},{0,12},{5,1},{9,5},{13,9},{1,13},{6,2},{10,6},{... | collective-permute-start | bytes 393224 | tf_op jit(solution)/shard_map/ppermute | solution.py:32
  37.9 5.4 %collective-permute-start.10 = (bf16[512,128]{1,0:T(8,128)(2,1)S(1)}, bf16[512,128]{1,0:T(8,128)(2,1)S(1)}, u32[]{:S(2)}, u32[]{:S(2)}) collective-permute-start(bf16[512,128]{1,0:T(8,128)(2,1)S(1)} %shard_map.85.refs_0_), channel_id=1, source_target_pairs={{8,0},{12,4},{0,8},{4,12},{9,1},{13,5},{1,9},{5,13},{10,2},{14,6},... | collective-permute-start | bytes 393224 | tf_op jit(solution)/shard_map/ppermute | solution.py:32
  38.1 7.2 %collective-permute-start.11 = (bf16[512,128]{1,0:T(8,128)(2,1)S(1)}, bf16[512,128]{1,0:T(8,128)(2,1)S(1)}, u32[]{:S(2)}, u32[]{:S(2)}) collective-permute-start(bf16[512,128]{1,0:T(8,128)(2,1)S(1)} %shard_map.85.refs_0_), channel_id=1, source_target_pairs={{12,0},{0,4},{4,8},{8,12},{13,1},{1,5},{5,9},{9,13},{14,2},{2,6},{... | collective-permute-start | bytes 393224 | tf_op jit(solution)/shard_map/ppermute | solution.py:32
  41.2 30.5 %collective-permute-start.4 = (bf16[512,512]{1,0:T(8,128)(2,1)}, bf16[512,512]{1,0:T(8,128)(2,1)}, u32[]{:S(2)}, u32[]{:S(2)}) collective-permute-start(bf16[512,512]{1,0:T(8,128)(2,1)} %shard_map.84.a0), channel_id=1, source_target_pairs={{8,0},{12,4},{0,8},{4,12},{9,1},{13,5},{1,9},{5,13},{10,2},{14,6},... | collective-permute-start | bytes 1572872 | tf_op jit(solution)/shard_map/ppermute | solution.py:32
  43.4 28.4 %collective-permute-start.5 = (bf16[512,512]{1,0:T(8,128)(2,1)}, bf16[512,512]{1,0:T(8,128)(2,1)}, u32[]{:S(2)}, u32[]{:S(2)}) collective-permute-start(bf16[512,512]{1,0:T(8,128)(2,1)} %shard_map.84.a0), channel_id=1, source_target_pairs={{12,0},{0,4},{4,8},{8,12},{13,1},{1,5},{5,9},{9,13},{14,2},{2,6},{... | collective-permute-start | bytes 1572872 | tf_op jit(solution)/shard_map/ppermute | solution.py:32
  46.6 25.1 %collective-permute-start.12 = (bf16[2048,128]{1,0:T(8,128)(2,1)}, bf16[2048,128]{1,0:T(8,128)(2,1)}, u32[]{:S(2)}, u32[]{:S(2)}) collective-permute-start(bf16[2048,128]{1,0:T(8,128)(2,1)} %shard_map.86.b0), channel_id=1, source_target_pairs={{64,0},{128,64},{192,128},{0,192},{65,1},{129,65},{193,129},{1,193... | collective-permute-start | bytes 1572872 | tf_op jit(solution)/shard_map/ppermute | solution.py:32
  49.5 22.3 %collective-permute-start.13 = (bf16[2048,128]{1,0:T(8,128)(2,1)}, bf16[2048,128]{1,0:T(8,128)(2,1)}, u32[]{:S(2)}, u32[]{:S(2)}) collective-permute-start(bf16[2048,128]{1,0:T(8,128)(2,1)} %shard_map.86.b0), channel_id=1, source_target_pairs={{128,0},{192,64},{0,128},{64,192},{129,1},{193,65},{1,129},{65,193... | collective-permute-start | bytes 1572872 | tf_op jit(solution)/shard_map/ppermute | solution.py:32
  49.7 22.1 %collective-permute-start.14 = (bf16[2048,128]{1,0:T(8,128)(2,1)}, bf16[2048,128]{1,0:T(8,128)(2,1)}, u32[]{:S(2)}, u32[]{:S(2)}) collective-permute-start(bf16[2048,128]{1,0:T(8,128)(2,1)} %shard_map.86.b0), channel_id=1, source_target_pairs={{192,0},{0,64},{64,128},{128,192},{193,1},{1,65},{65,129},{129,193... | collective-permute-start | bytes 1572872 | tf_op jit(solution)/shard_map/ppermute | solution.py:32
  51.3 40.5 %all-to-all-start.1 = ((bf16[16,128,128]{2,1,0:T(8,128)(2,1)}), bf16[16,128,128]{2,1,0:T(8,128)(2,1)S(1)}, u32[]{:S(2)}, u32[]{:S(2)}) async-start(bf16[16,128,128]{2,1,0:T(8,128)(2,1)} %shard_map.91), calls=%async_computation.1 | async-start | bytes 1048576 | tf_op jit(solution)/shard_map/all_to_all | solution.py:287
  71.7 20.0 %copy-start.1 = (bf16[1,256,2048]{2,1,0:T(8,128)(2,1)S(1)}, bf16[1,256,2048]{2,1,0:T(8,128)(2,1)}, u32[]{:S(2)}) copy-start(bf16[1,256,2048]{2,1,0:T(8,128)(2,1)} %param.6) | copy-start | bytes 3145732
  71.7 20.0 %copy-start.2 = (bf16[1,256,2048]{2,1,0:T(8,128)(2,1)S(1)}, bf16[1,256,2048]{2,1,0:T(8,128)(2,1)}, u32[]{:S(2)}) copy-start(bf16[1,256,2048]{2,1,0:T(8,128)(2,1)} %param.7) | copy-start | bytes 3145732
  78.6 27.6 %collective-permute-start.16 = (f32[256,2048]{1,0:T(8,128)}, f32[256,2048]{1,0:T(8,128)}, u32[]{:S(2)}, u32[]{:S(2)}) collective-permute-start(f32[256,2048]{1,0:T(8,128)} %shard_map.88), channel_id=1, source_target_pairs={{0,16},{16,0},{1,17},{17,1},{2,18},{18,2},{3,19},{19,3},{4,20},{20... | collective-permute-start | bytes 6291464 | tf_op jit(solution)/shard_map/ppermute | solution.py:28
  91.8 4.2 %copy-start.3 = (bf16[16,128,128]{2,1,0:T(8,128)(2,1)}, bf16[16,128,128]{2,1,0:T(8,128)(2,1)S(1)}, u32[]{:S(2)}) copy-start(bf16[16,128,128]{2,1,0:T(8,128)(2,1)S(1)} %all-to-all-done.1.p_ref) | copy-start | bytes 1572868
  93.2 5.6 %copy-start.7 = (bf16[1,256,2048]{2,1,0:T(8,128)(2,1)S(1)}, bf16[1,256,2048]{2,1,0:T(8,128)(2,1)}, u32[]{:S(2)}) copy-start(bf16[1,256,2048]{2,1,0:T(8,128)(2,1)} %param.9) | copy-start | bytes 3145732
  93.2 5.6 %copy-start.16 = (bf16[256,1024]{1,0:T(8,128)(2,1)S(1)}, bf16[256,1024]{1,0:T(8,128)(2,1)}, u32[]{:S(2)}) copy-start(bf16[256,1024]{1,0:T(8,128)(2,1)} %copy-done.14) | copy-start | bytes 1572868
  96.0 6.9 %copy-start.12 = (bf16[2048,256]{1,0:T(8,128)(2,1)}, bf16[2048,256]{1,0:T(8,128)(2,1)S(1)}, u32[]{:S(2)}) copy-start(bf16[2048,256]{1,0:T(8,128)(2,1)S(1)} %shard_map.95.mine_ref) | copy-start | bytes 3145732
  96.0 6.9 %copy-start.11 = (bf16[512,512]{1,0:T(8,128)(2,1)S(1)}, bf16[512,512]{1,0:T(8,128)(2,1)}, u32[]{:S(2)}) copy-start(bf16[512,512]{1,0:T(8,128)(2,1)} %copy-done.9) | copy-start | bytes 1572868
  96.0 2.7 %collective-permute-start.17 = (bf16[2048,256]{1,0:T(8,128)(2,1)S(1)}, bf16[2048,256]{1,0:T(8,128)(2,1)S(1)}, u32[]{:S(2)}, u32[]{:S(2)}) collective-permute-start(bf16[2048,256]{1,0:T(8,128)(2,1)S(1)} %shard_map.95.mine_ref), channel_id=1, source_target_pairs={{0,16},{16,0},{1,17},{17,1},{2,18},{18,2},{3,19},{19,3},{4,20},{20... | collective-permute-start | bytes 3145736 | tf_op jit(solution)/shard_map/ppermute | solution.py:28
  98.7 3.3 %copy-start.18 = (bf16[2048,256]{1,0:T(8,128)(2,1)}, bf16[2048,256]{1,0:T(8,128)(2,1)S(1)}, u32[]{:S(2)}) copy-start(bf16[2048,256]{1,0:T(8,128)(2,1)S(1)} %collective-permute-done.17.theirs_ref) | copy-start | bytes 3145732
  102.8 3.4 %copy-start.5 = (bf16[1,256,2048]{2,1,0:T(8,128)(2,1)S(1)}, bf16[1,256,2048]{2,1,0:T(8,128)(2,1)}, u32[]{:S(2)}) copy-start(bf16[1,256,2048]{2,1,0:T(8,128)(2,1)} %param.5) | copy-start | bytes 3145732
  102.8 21.4 %collective-permute-start.18 = (bf16[2048,128]{1,0:T(8,128)(2,1)}, bf16[2048,128]{1,0:T(8,128)(2,1)}, u32[]{:S(2)}, u32[]{:S(2)}) collective-permute-start(bf16[2048,128]{1,0:T(8,128)(2,1)} %get-tuple-element.29), channel_id=1, source_target_pairs={{0,64},{64,128},{128,192},{192,0},{1,65},{65,129},{129,193},{193,1... | collective-permute-start | bytes 1572872 | tf_op jit(solution)/shard_map/ppermute | solution.py:37
  106.2 12.5 %copy-start.8 = (bf16[1,256,2048]{2,1,0:T(8,128)(2,1)S(1)}, bf16[1,256,2048]{2,1,0:T(8,128)(2,1)}, u32[]{:S(2)}) copy-start(bf16[1,256,2048]{2,1,0:T(8,128)(2,1)} %param.9) | copy-start | bytes 3145732
  109.3 52.7 %all-to-all-start.2 = ((bf16[16,128,128]{2,1,0:T(8,128)(2,1)}), bf16[16,128,128]{2,1,0:T(8,128)(2,1)S(1)}, u32[]{:S(2)}, u32[]{:S(2)}) async-start(bf16[16,128,128]{2,1,0:T(8,128)(2,1)} %get-tuple-element.25), calls=%async_computation.2 | async-start | bytes 1048576 | tf_op jit(solution)/shard_map/all_to_all | solution.py:285
  115.0 20.6 %collective-permute-start.19 = (bf16[2048,128]{1,0:T(8,128)(2,1)}, bf16[2048,128]{1,0:T(8,128)(2,1)S(1)}, u32[]{:S(2)}, u32[]{:S(2)}) collective-permute-start(bf16[2048,128]{1,0:T(8,128)(2,1)} %copy-done.20), channel_id=1, source_target_pairs={{0,128},{64,192},{128,0},{192,64},{1,129},{65,193},{129,1},{193,65... | collective-permute-start | bytes 1572872 | tf_op jit(solution)/shard_map/ppermute | solution.py:37
  117.9 27.5 %collective-permute-start.20 = (bf16[2048,128]{1,0:T(8,128)(2,1)S(1)}, bf16[2048,128]{1,0:T(8,128)(2,1)S(1)}, u32[]{:S(2)}, u32[]{:S(2)}) collective-permute-start(bf16[2048,128]{1,0:T(8,128)(2,1)S(1)} %get-tuple-element.31), channel_id=1, source_target_pairs={{0,192},{64,0},{128,64},{192,128},{1,193},{65,1},{129,65},{193,129... | collective-permute-start | bytes 1572872 | tf_op jit(solution)/shard_map/ppermute | solution.py:37
  124.0 25.0 %collective-permute-start.24 = (bf16[512,512]{1,0:T(8,128)(2,1)S(1)}, bf16[512,512]{1,0:T(8,128)(2,1)S(1)}, u32[]{:S(2)}, u32[]{:S(2)}) collective-permute-start(bf16[512,512]{1,0:T(8,128)(2,1)S(1)} %get-tuple-element.37), channel_id=1, source_target_pairs={{0,4},{4,8},{8,12},{12,0},{1,5},{5,9},{9,13},{13,1},{2,6},{6,10},{... | collective-permute-start | bytes 1572872 | tf_op jit(solution)/shard_map/ppermute | solution.py:37
  124.1 25.3 %collective-permute-start.25 = (bf16[512,512]{1,0:T(8,128)(2,1)S(1)}, bf16[512,512]{1,0:T(8,128)(2,1)S(1)}, u32[]{:S(2)}, u32[]{:S(2)}) collective-permute-start(bf16[512,512]{1,0:T(8,128)(2,1)S(1)} %get-tuple-element.38), channel_id=1, source_target_pairs={{0,8},{4,12},{8,0},{12,4},{1,9},{5,13},{9,1},{13,5},{2,10},{6,14},... | collective-permute-start | bytes 1572872 | tf_op jit(solution)/shard_map/ppermute | solution.py:37
  124.2 25.2 %collective-permute-start.26 = (bf16[512,512]{1,0:T(8,128)(2,1)S(1)}, bf16[512,512]{1,0:T(8,128)(2,1)S(1)}, u32[]{:S(2)}, u32[]{:S(2)}) collective-permute-start(bf16[512,512]{1,0:T(8,128)(2,1)S(1)} %get-tuple-element.39), channel_id=1, source_target_pairs={{0,12},{4,0},{8,4},{12,8},{1,13},{5,1},{9,5},{13,9},{2,14},{6,2},{... | collective-permute-start | bytes 1572872 | tf_op jit(solution)/shard_map/ppermute | solution.py:37
  146.7 9.1 %collective-permute-start.21 = (bf16[512,128]{1,0:T(8,128)(2,1)S(1)}, bf16[512,128]{1,0:T(8,128)(2,1)S(1)}, u32[]{:S(2)}, u32[]{:S(2)}) collective-permute-start(bf16[512,128]{1,0:T(8,128)(2,1)S(1)} %get-tuple-element.33), channel_id=1, source_target_pairs={{0,4},{4,8},{8,12},{12,0},{1,5},{5,9},{9,13},{13,1},{2,6},{6,10},{... | collective-permute-start | bytes 393224 | tf_op jit(solution)/shard_map/ppermute | solution.py:37
  146.7 10.7 %collective-permute-start.22 = (bf16[512,128]{1,0:T(8,128)(2,1)S(1)}, bf16[512,128]{1,0:T(8,128)(2,1)S(1)}, u32[]{:S(2)}, u32[]{:S(2)}) collective-permute-start(bf16[512,128]{1,0:T(8,128)(2,1)S(1)} %get-tuple-element.34), channel_id=1, source_target_pairs={{0,8},{4,12},{8,0},{12,4},{1,9},{5,13},{9,1},{13,5},{2,10},{6,14},... | collective-permute-start | bytes 393224 | tf_op jit(solution)/shard_map/ppermute | solution.py:37
  149.1 8.3 %collective-permute-start.23 = (bf16[512,128]{1,0:T(8,128)(2,1)S(1)}, bf16[512,128]{1,0:T(8,128)(2,1)S(1)}, u32[]{:S(2)}, u32[]{:S(2)}) collective-permute-start(bf16[512,128]{1,0:T(8,128)(2,1)S(1)} %get-tuple-element.35), channel_id=1, source_target_pairs={{0,12},{4,0},{8,4},{12,8},{1,13},{5,1},{9,5},{13,9},{2,14},{6,2},{... | collective-permute-start | bytes 393224 | tf_op jit(solution)/shard_map/ppermute | solution.py:37
  150.3 7.1 %collective-permute-start.27 = (bf16[512,128]{1,0:T(8,128)(2,1)S(1)}, bf16[512,128]{1,0:T(8,128)(2,1)S(1)}, u32[]{:S(2)}, u32[]{:S(2)}) collective-permute-start(bf16[512,128]{1,0:T(8,128)(2,1)S(1)} %get-tuple-element.41), channel_id=1, source_target_pairs={{0,64},{64,128},{128,192},{192,0},{1,65},{65,129},{129,193},{193,1... | collective-permute-start | bytes 393224 | tf_op jit(solution)/shard_map/ppermute | solution.py:37
  151.6 6.5 %collective-permute-start.28 = (bf16[512,128]{1,0:T(8,128)(2,1)S(1)}, bf16[512,128]{1,0:T(8,128)(2,1)S(1)}, u32[]{:S(2)}, u32[]{:S(2)}) collective-permute-start(bf16[512,128]{1,0:T(8,128)(2,1)S(1)} %get-tuple-element.42), channel_id=1, source_target_pairs={{0,128},{64,192},{128,0},{192,64},{1,129},{65,193},{129,1},{193,65... | collective-permute-start | bytes 393224 | tf_op jit(solution)/shard_map/ppermute | solution.py:37
  155.8 5.4 %collective-permute-start.29 = (bf16[512,128]{1,0:T(8,128)(2,1)S(1)}, bf16[512,128]{1,0:T(8,128)(2,1)S(1)}, u32[]{:S(2)}, u32[]{:S(2)}) collective-permute-start(bf16[512,128]{1,0:T(8,128)(2,1)S(1)} %get-tuple-element.43), channel_id=1, source_target_pairs={{0,192},{64,0},{128,64},{192,128},{1,193},{65,1},{129,65},{193,129... | collective-permute-start | bytes 393224 | tf_op jit(solution)/shard_map/ppermute | solution.py:37
  162.0 12.4 %all-to-all-start.4 = ((bf16[8,128,128]{2,1,0:T(8,128)(2,1)}), bf16[8,128,128]{2,1,0:T(8,128)(2,1)S(1)}, u32[]{:S(2)}, u32[]{:S(2)}) async-start(bf16[8,128,128]{2,1,0:T(8,128)(2,1)} %shard_map.100), calls=%async_computation.4 | async-start | bytes 524288 | tf_op jit(solution)/shard_map/all_to_all | solution.py:351
  174.4 18.7 %all-to-all-start.3 = ((bf16[16,128,128]{2,1,0:T(8,128)(2,1)}), bf16[16,128,128]{2,1,0:T(8,128)(2,1)S(1)}, u32[]{:S(2)}, u32[]{:S(2)}) async-start(bf16[16,128,128]{2,1,0:T(8,128)(2,1)} %shard_map.93), calls=%async_computation.3 | async-start | bytes 1048576 | tf_op jit(solution)/shard_map/all_to_all | solution.py:287
  193.0 10.0 %copy-start.21 = (bf16[16,128,128]{2,1,0:T(8,128)(2,1)}, bf16[16,128,128]{2,1,0:T(8,128)(2,1)S(1)}, u32[]{:S(2)}) copy-start(bf16[16,128,128]{2,1,0:T(8,128)(2,1)S(1)} %all-to-all-done.3.l_ref) | copy-start | bytes 1572868
  193.1 18.1 %all-to-all-start.5 = ((bf16[16,128,128]{2,1,0:T(8,128)(2,1)}), bf16[16,128,128]{2,1,0:T(8,128)(2,1)S(1)}, u32[]{:S(2)}, u32[]{:S(2)}) async-start(bf16[16,128,128]{2,1,0:T(8,128)(2,1)} %shard_map.101), calls=%async_computation.5 | async-start | bytes 1048576 | tf_op jit(solution)/shard_map/all_to_all | solution.py:353
  (10 other events, 12.4 us)
